TPU v7x, 512 devices: a whole 4x4x16 slice. The times are simulated.
512 devices in a mesh: blk: 64 (over x, z), head: 8 (over y, core).
Axes of the slice: x: 4, y: 4, z: 16, core: 2. Of those that a mesh axis runs over, the one named last changes fastest.
Arguments:
- acceptance_vector: bfloat16 [8192, 4096], P('blk', 'head'), may hold values from -6 to 6
- lookup_vector_array: bfloat16 [8192, 4096], P('blk', 'head'), may hold values from -2 to 2
- payload_vector_array: bfloat16 [8192, 4096], P('blk', 'head'), may hold values from -6 to 6
- raw_gating_signal: bfloat16 [8192, 4096], P('blk', 'head'), may hold values from -6 to 6
- raw_forgetting_rate: bfloat16 [8192, 4096], P('blk', 'head'), may hold values from -16 to 1
- current_reward_vector: float32 [4096], P('head'), may hold values from -1.5 to 1.5
- memory_following_query: bfloat16 [2, 4096, 64], P(None, 'head'), may hold values from -24 to 24
- group_layernorm_scaling: float32 [4096], P('head'), may hold values from 0.25 to 1.75
- closing_layernorm_scaling: float32 [4096], replicated, may hold values from 0.25 to 1.75
- skip_stream_input: bfloat16 [8192, 4096], P(('blk', 'head')), may hold values from -6 to 6
- closing_projection: bfloat16 [4096, 4096], P('head', 'blk'), may hold values from -0.09375 to 0.09375
- vocabulary_readout: bfloat16 [32768, 4096], P('blk'), may hold values from -15.625 to 15.625
- following_labels: int32 [8192], P(('blk', 'head')), may hold values from 0 to 32767
- response_indicator: int32 [8192], P(('blk', 'head')), may hold values 0 or 1
- baseline_logarithmic_likelihood: float32 [8192], P(('blk', 'head')), may hold values from -14 to -6
- rollout_for_segment: int32 [64], replicated, may hold values from 0 to 15, never falling along the last dimension, each value on 1 to 32 neighbouring positions
- query_text_for_rollout: int32 [16], replicated, may hold values from 0 to 1
Outputs:
- token_ratio: float32 [8192], P(('blk', 'head'))
- seq_ratio: float32 [16], replicated
Inputs may be any that keep to these rules, and one draw needn't show every extreme that they name: `rollout_for_segment`: sequences fill whole consecutive blocks, each 1 to 32 blocks, one exactly 32; ids start at 0 and rise by one at each new sequence.
All inputs are finite; a program needn't handle non-finite values. No bound on the sum of `response_indicator` on one device may be relied on, other than what follows from the above.
Results may differ from a plain program's by a relative error of at most 0.0017.
Values may be sent and summed in bfloat16 or wider, within the bound.
No kernel may reach another device: no remote copies, remote signals or barrier semaphores. Data moves between devices by JAX's collectives and lax.ppermute only.
A program may use at most 128 MiB of HBM per device.

v0:
```python
import jax
import jax.numpy as jnp
from jax import lax
from jax.sharding import PartitionSpec as P

GROUP_DIMENSION = 64
TOK_BLK = 128


def passed_along(value, axis, steps):
    count = lax.axis_size(axis)
    first, last = (max(0, -steps), min(count, count - steps))
    return lax.ppermute(value, axis, [(source, source + steps) for source in range(first, last)])


def joined(part, axis, combine):
    gathered = jax.tree.map(lambda a: lax.all_gather(a, axis), part)

    def take(source):
        return jax.tree.map(lambda a: lax.dynamic_index_in_dim(a, source, 0, False), gathered)

    return lax.fori_loop(
        1, lax.axis_size(axis), lambda source, state: combine(state, take(source)), take(0)
    )


def per_device(
    acceptance_vector,
    lookup_vector_array,
    payload_vector_array,
    raw_gating_signal,
    raw_forgetting_rate,
    current_reward_vector,
    memory_following_query,
    group_layernorm_scaling,
    closing_layernorm_scaling,
    skip_stream_input,
    closing_projection,
    vocabulary_readout,
    following_labels,
    response_indicator,
    baseline_logarithmic_likelihood,
    rollout_for_segment,
    query_text_for_rollout,
):
    n_blk = lax.axis_size("blk")
    blk_index = lax.axis_index("blk")
    rows, width = acceptance_vector.shape
    local_attention_groups = width // GROUP_DIMENSION
    sub = 16
    nsub = rows // sub
    highest = lax.Precision.HIGHEST

    def split(a):
        return (
            a.astype(jnp.float32)
            .reshape(nsub, sub, local_attention_groups, GROUP_DIMENSION)
            .transpose(0, 2, 1, 3)
        )

    inherited_memory = split(acceptance_vector)
    lookup_vectors = split(lookup_vector_array)
    vals = split(payload_vector_array)
    log_decay = -jnp.exp(split(raw_forgetting_rate))
    inclusive = jnp.cumsum(log_decay, axis=2)
    exclusive = inclusive - log_decay
    last = inclusive[:, :, -1, :]
    this_seq = rollout_for_segment[blk_index]
    prev_seq = rollout_for_segment[jnp.maximum(blk_index - 1, 0)]
    starts = jnp.logical_or(blk_index == 0, this_seq != prev_seq).astype(jnp.float32)
    prompt = (
        memory_following_query[query_text_for_rollout[this_seq]]
        .astype(jnp.float32)
        .reshape(local_attention_groups, GROUP_DIMENSION, GROUP_DIMENSION)
    )
    later = jnp.arange(sub)[:, None] > jnp.arange(sub)[None, :]
    spread = exclusive[:, :, :, None, :] - inclusive[:, :, None, :, :]
    weights = jnp.where(later[None, None, :, :, None], jnp.exp(jnp.minimum(spread, 0.0)), 0.0)
    scores = jnp.sum(
        inherited_memory[:, :, :, None, :] * lookup_vectors[:, :, None, :, :] * weights, axis=-1
    )
    group_current_reward = current_reward_vector.reshape(local_attention_groups, GROUP_DIMENSION)
    diagonal_term = jnp.sum(
        inherited_memory * lookup_vectors * group_current_reward[None, :, None, :], axis=-1
    )
    wkv = (
        jnp.einsum("nhts,nhsj->nhtj", scores, vals, precision=highest)
        + diagonal_term[..., None] * vals
    )
    keys_late = lookup_vectors * jnp.exp(last[:, :, None, :] - inclusive)
    delta = jnp.einsum("nhsi,nhsj->nhij", keys_late, vals, precision=highest)

    def advance(state, item):
        change, fall = item
        return (jnp.exp(fall)[:, :, None] * state + change, state)

    end_state, entering = lax.scan(advance, starts * prompt, (delta, last))
    wkv = wkv + jnp.einsum(
        "nhti,nhij->nhtj", inherited_memory * jnp.exp(exclusive), entering, precision=highest
    )
    block_fall = jnp.exp(jnp.sum(last, axis=0)) * (1.0 - starts)

    def relay_step(step, incoming):
        leaving = block_fall[:, :, None] * incoming + end_state
        return passed_along(leaving, "blk", 1)

    incoming = lax.fori_loop(0, n_blk // 2 - 1, relay_step, jnp.zeros_like(end_state))
    offsets = jnp.cumsum(last, axis=0) - last
    carried = inherited_memory * jnp.exp(exclusive + offsets[:, :, None, :])
    wkv = wkv + (1.0 - starts) * jnp.einsum("nhti,hij->nhtj", carried, incoming, precision=highest)
    mean = jnp.mean(wkv, axis=-1, keepdims=True)
    var = jnp.mean((wkv - mean) ** 2, axis=-1, keepdims=True)
    normal_h = (wkv - mean) / jnp.sqrt(var + 0.00064)
    normal_h = normal_h.transpose(0, 2, 1, 3).reshape(rows, width) * group_layernorm_scaling
    mixed = (normal_h * jax.nn.silu(raw_gating_signal.astype(jnp.float32))).astype(jnp.bfloat16)
    partial_out = jnp.dot(
        mixed,
        lax.all_gather(closing_projection, "blk", axis=1, tiled=True),
        preferred_element_type=jnp.float32,
    )
    own_rows = lax.psum_scatter(partial_out, "head", scatter_dimension=0, tiled=True)
    hidden = skip_stream_input.astype(jnp.float32) + own_rows
    hmean = jnp.mean(hidden, axis=-1, keepdims=True)
    hvar = jnp.mean((hidden - hmean) ** 2, axis=-1, keepdims=True)
    normed = ((hidden - hmean) / jnp.sqrt(hvar + 1e-05) * closing_layernorm_scaling).astype(
        jnp.bfloat16
    )
    local_rows = normed.shape[0]
    vocab_local = vocabulary_readout.shape[0]
    vocab_base = blk_index * vocab_local
    rows_n = lax.all_gather(normed, "blk", axis=0, tiled=True)
    rows_t = lax.all_gather(following_labels, "blk", axis=0, tiled=True)
    logits = lax.dot_general(
        rows_n, vocabulary_readout, (((1,), (1,)), ((), ())), preferred_element_type=jnp.float32
    )
    top = jnp.max(logits, axis=1)
    grand_sum = jnp.sum(jnp.exp(logits - top[:, None]), axis=1)
    entry = jnp.arange(vocab_local, dtype=jnp.int32)[None, :] + vocab_base
    picked = jnp.sum(jnp.where(entry == rows_t[:, None], logits, 0.0), axis=1)
    top, grand_sum, picked = tuple((new for new in (top, grand_sum, picked)))

    def join(first, second):
        peak = jnp.maximum(first[0], second[0])
        summed = first[1] * jnp.exp(first[0] - peak) + second[1] * jnp.exp(second[0] - peak)
        return (peak, summed, first[2] + second[2])

    top, grand_sum, picked = joined((top, grand_sum, picked), "blk", join)
    logp = picked - top - jnp.log(grand_sum)
    mine = lax.dynamic_slice_in_dim(logp, blk_index * local_rows, local_rows)
    token_ratio = response_indicator.astype(jnp.float32) * (mine - baseline_logarithmic_likelihood)
    seq_count = query_text_for_rollout.shape[0]
    marker = (jnp.arange(seq_count, dtype=jnp.int32) == this_seq).astype(jnp.float32)
    partial_seq = marker * (jnp.sum(token_ratio) / TOK_BLK)
    seq_ratio = lax.psum(partial_seq, ("blk", "head"))
    return (token_ratio, seq_ratio)


def solution(mesh):
    placed = (
        P("blk", "head"),
        P("blk", "head"),
        P("blk", "head"),
        P("blk", "head"),
        P("blk", "head"),
        P("head"),
        P(None, "head", None),
        P("head"),
        P(),
        P(("blk", "head"), None),
        P("head", "blk"),
        P("blk", None),
        P(("blk", "head")),
        P(("blk", "head")),
        P(("blk", "head")),
        P(),
        P(),
    )
    return jax.shard_map(
        per_device, mesh=mesh, in_specs=placed, out_specs=(P(("blk", "head")), P()), check_vma=False
    )
```

profile of v0, /device:TPU:1, one launch (start us, length us, event | category | flops | bytes accessed | tf_op | source)
XLA Modules:
  0.0 976.3 jit_solution(5648357997811550387)
XLA Ops:
  9.1 4.9 fusion.11
  25.3 7.4 while.41
  41.9 301.2 %while.42 = (s32[]{:T(128)}, f32[8,64,64]{2,1,0:T(8,128)S(1)}, f32[8,64]{1,0:T(8,128)S(1)}, f32[8,64,64]{2,1,0:T(8,128)S(1)}, s32[]{:T(128)}) while((s32[]{:T(128)}, f32[8,64,64]{2,1,0:T(8,128)S(1)}, f32[8,64]{1,0:T(8,128)S(1)}, f32[8,64,64]{2,1,0:T(8,128)S(1)}, s32[]{:T(128)}) %tuple.86), condition=%wide.region_7.8_spmd, body=%wide.region_6.7_spmd.sunk | while | flops 65538 | bytes 919653 | solution.py:107
  50.2 5.4 collective-permute-start
  59.4 5.0 collective-permute-start
  68.2 4.6 collective-permute-start
  76.6 5.9 collective-permute-start
  86.2 5.3 collective-permute-start
  94.8 5.2 collective-permute-start
  104.6 5.6 collective-permute-start
  114.3 8.7 collective-permute-start
  123.0 8.9 collective-permute-done
  136.3 7.5 collective-permute-done
  143.9 5.6 collective-permute-start
  149.6 7.7 collective-permute-done
  173.7 4.6 collective-permute-start
  181.8 5.5 collective-permute-start
  190.7 5.3 collective-permute-start
  199.4 5.5 collective-permute-start
  208.4 5.0 collective-permute-start
  217.2 5.3 collective-permute-start
  222.6 4.7 collective-permute-done
  227.5 5.5 collective-permute-start
  233.0 5.7 collective-permute-done
  238.9 6.0 collective-permute-start
  244.9 5.2 collective-permute-done
  250.2 4.8 collective-permute-start
  266.7 5.2 collective-permute-start
  275.3 5.3 collective-permute-start
  284.0 5.3 collective-permute-start
  292.8 5.0 collective-permute-start
  301.5 5.3 collective-permute-start
  306.9 4.6 collective-permute-done
  311.6 5.6 collective-permute-start
  317.2 5.7 collective-permute-done
  323.1 6.0 collective-permute-start
  329.1 5.3 collective-permute-done
  334.6 4.6 collective-permute-start
  345.3 5.0 fusion.26
  350.4 98.3 %reduce-scatter.2.cloned.1.call-done = f32[16,4096]{1,0:T(8,128)} async-done(((f32[128,4096]{1,0:T(8,128)}), f32[16,4096]{1,0:T(8,128)}) %reduce-scatter.2.cloned.1.call-update) | async-done | bytes 262160 | tf_op jit(solution)/shard_map/reduce_scatter | solution.py:121
  454.9 23.9 %all-reduce = s32[1024]{0:T(1024)S(1)} all-reduce(s32[1024]{0:T(1024)S(1)} %dynamic-update-slice), channel_id=1, replica_groups=mesh['blk'=64,'head'=8] {'blk'}, use_global_device_ids=true, to_apply=%add | all-reduce | flops 1024 | bytes 8192
  478.8 124.2 %all-gather.8.cloned.1.call-done = bf16[1024,4096]{1,0:T(8,128)(2,1)} async-done(((bf16[16,4096]{1,0:T(8,128)(2,1)}), bf16[1024,4096]{1,0:T(8,128)(2,1)}) %all-gather.8.cloned.1.call-update) | async-done | bytes 8388624 | tf_op jit(solution)/shard_map/all_gather | solution.py:131
  603.0 8.2 fusion.38
  611.8 61.3 %all-gather.1 = f32[65536]{0:T(1024)S(1)} all-gather(f32[1024]{0:T(1024)S(1)} %get-tuple-element.237), channel_id=3, replica_groups=mesh['blk'=64,'head'=8] {'blk'}, dimensions={0}, use_global_device_ids=true | all-gather | bytes 266240 | tf_op jit(solution)/shard_map/all_gather | solution.py:17
  673.2 63.6 %all-gather.2 = f32[65536]{0:T(1024)S(1)} all-gather(f32[1024]{0:T(1024)S(1)} %get-tuple-element.236), channel_id=4, replica_groups=mesh['blk'=64,'head'=8] {'blk'}, dimensions={0}, use_global_device_ids=true | all-gather | bytes 266240 | tf_op jit(solution)/shard_map/all_gather | solution.py:17
  736.8 63.0 %all-gather = f32[65536]{0:T(1024)S(1)} all-gather(f32[1024]{0:T(1024)S(1)} %get-tuple-element.289), channel_id=2, replica_groups=mesh['blk'=64,'head'=8] {'blk'}, dimensions={0}, use_global_device_ids=true | all-gather | bytes 266240 | tf_op jit(solution)/shard_map/all_gather | solution.py:17
  799.9 5.9 while.43
  808.4 161.3 %psum.7 = f32[16]{0:T(128)} all-reduce(f32[16]{0:T(128)S(1)} %compare_select_fusion), channel_id=1, replica_groups=mesh['blk'=64,'head'=8] {'blk','head'}, use_global_device_ids=true, to_apply=%region_20.21 | all-reduce | flops 16 | bytes 128 | tf_op jit(solution)/shard_map/psum | solution.py:154
  (433 shorter events, 140.9 us)
Async XLA Ops:
  7.2 7.9 copy-start.14
  7.2 10.5 %copy-start.17 = (s32[16]{0:T(128)S(1)}, s32[16]{0:T(128)}, u32[]{:S(2)}) copy-start(s32[16]{0:T(128)} %param.39) | copy-start | bytes 196
  7.2 14.3 %copy-start.10 = (bf16[2,512,64]{1,2,0:T(8,128)(2,1)S(1)}, bf16[2,512,64]{1,2,0:T(8,128)(2,1)}, u32[]{:S(2)}) copy-start(bf16[2,512,64]{1,2,0:T(8,128)(2,1)} %param.29) | copy-start | bytes 393220
  7.2 14.5 %copy-start.6 = (bf16[128,512]{1,0:T(8,128)(2,1)S(1)}, bf16[128,512]{1,0:T(8,128)(2,1)}, u32[]{:S(2)}) copy-start(bf16[128,512]{1,0:T(8,128)(2,1)} %param.23) | copy-start | bytes 393220
  7.2 338.0 %all-gather.6.cloned.1.call-start = ((), (), s32[]{:S(2)}) async-start(), calls=%async_computation.1 | async-start | bytes 4259840 | tf_op jit(solution)/shard_map/all_gather | solution.py:118
  7.9 440.7 %reduce-scatter.2.cloned.1.call-start = ((), (), s32[]{:S(2)}) async-start(), calls=%async_computation.2 | async-start | bytes 2359296 | tf_op jit(solution)/shard_map/reduce_scatter | solution.py:121
  9.0 12.9 %copy-start.7 = (bf16[128,512]{1,0:T(8,128)(2,1)S(1)}, bf16[128,512]{1,0:T(8,128)(2,1)}, u32[]{:S(2)}) copy-start(bf16[128,512]{1,0:T(8,128)(2,1)} %param.24) | copy-start | bytes 393220
  9.1 12.9 %copy-start.13 = (f32[512]{0:T(512)S(1)}, f32[512]{0:T(512)}, u32[]{:S(2)}) copy-start(f32[512]{0:T(512)} %param.28) | copy-start | bytes 6148
  9.1 13.0 %copy-start.8 = (bf16[128,512]{1,0:T(8,128)(2,1)S(1)}, bf16[128,512]{1,0:T(8,128)(2,1)}, u32[]{:S(2)}) copy-start(bf16[128,512]{1,0:T(8,128)(2,1)} %param.25) | copy-start | bytes 393220
  22.0 1.5 copy-start.1
  34.2 3.5 copy-start
  42.0 8.0 collective-permute-start
  50.2 9.0 collective-permute-start
  59.4 8.7 collective-permute-start
  68.2 8.3 collective-permute-start
  76.6 9.4 collective-permute-start
  86.2 8.5 collective-permute-start
  94.8 9.6 collective-permute-start
  104.6 9.6 collective-permute-start
  114.3 17.5 %collective-permute-start = (f32[8,64,64]{2,1,0:T(8,128)S(1)}, f32[8,64,64]{2,1,0:T(8,128)S(1)}, u32[]{:S(2)}, u32[]{:S(2)}) collective-permute-start(f32[8,64,64]{2,1,0:T(8,128)S(1)} %multiply_add_fusion.4), channel_id=1, source_target_pairs={{0,8},{8,16},{16,24},{24,32},{32,40},{40,48},{48,56},{56,64},{64,7... | collective-permute-start | bytes 393224 | tf_op jit(solution)/shard_map/while/body/eval_jaxpr/ppermute | solution.py:13
  132.0 11.8 %collective-permute-start = (f32[8,64,64]{2,1,0:T(8,128)S(1)}, f32[8,64,64]{2,1,0:T(8,128)S(1)}, u32[]{:S(2)}, u32[]{:S(2)}) collective-permute-start(f32[8,64,64]{2,1,0:T(8,128)S(1)} %multiply_add_fusion.4), channel_id=1, source_target_pairs={{0,8},{8,16},{16,24},{24,32},{32,40},{40,48},{48,56},{56,64},{64,7... | collective-permute-start | bytes 393224 | tf_op jit(solution)/shard_map/while/body/eval_jaxpr/ppermute | solution.py:13
  143.9 13.4 %collective-permute-start = (f32[8,64,64]{2,1,0:T(8,128)S(1)}, f32[8,64,64]{2,1,0:T(8,128)S(1)}, u32[]{:S(2)}, u32[]{:S(2)}) collective-permute-start(f32[8,64,64]{2,1,0:T(8,128)S(1)} %multiply_add_fusion.4), channel_id=1, source_target_pairs={{0,8},{8,16},{16,24},{24,32},{32,40},{40,48},{48,56},{56,64},{64,7... | collective-permute-start | bytes 393224 | tf_op jit(solution)/shard_map/while/body/eval_jaxpr/ppermute | solution.py:13
  157.4 8.5 collective-permute-start
  166.1 7.5 collective-permute-start
  173.7 7.9 collective-permute-start
  181.8 8.8 collective-permute-start
  190.7 8.6 collective-permute-start
  199.4 8.8 collective-permute-start
  208.4 8.7 collective-permute-start
  217.2 10.1 %collective-permute-start = (f32[8,64,64]{2,1,0:T(8,128)S(1)}, f32[8,64,64]{2,1,0:T(8,128)S(1)}, u32[]{:S(2)}, u32[]{:S(2)}) collective-permute-start(f32[8,64,64]{2,1,0:T(8,128)S(1)} %multiply_add_fusion.4), channel_id=1, source_target_pairs={{0,8},{8,16},{16,24},{24,32},{32,40},{40,48},{48,56},{56,64},{64,7... | collective-permute-start | bytes 393224 | tf_op jit(solution)/shard_map/while/body/eval_jaxpr/ppermute | solution.py:13
  227.5 11.3 %collective-permute-start = (f32[8,64,64]{2,1,0:T(8,128)S(1)}, f32[8,64,64]{2,1,0:T(8,128)S(1)}, u32[]{:S(2)}, u32[]{:S(2)}) collective-permute-start(f32[8,64,64]{2,1,0:T(8,128)S(1)} %multiply_add_fusion.4), channel_id=1, source_target_pairs={{0,8},{8,16},{16,24},{24,32},{32,40},{40,48},{48,56},{56,64},{64,7... | collective-permute-start | bytes 393224 | tf_op jit(solution)/shard_map/while/body/eval_jaxpr/ppermute | solution.py:13
  238.9 11.2 %collective-permute-start = (f32[8,64,64]{2,1,0:T(8,128)S(1)}, f32[8,64,64]{2,1,0:T(8,128)S(1)}, u32[]{:S(2)}, u32[]{:S(2)}) collective-permute-start(f32[8,64,64]{2,1,0:T(8,128)S(1)} %multiply_add_fusion.4), channel_id=1, source_target_pairs={{0,8},{8,16},{16,24},{24,32},{32,40},{40,48},{48,56},{56,64},{64,7... | collective-permute-start | bytes 393224 | tf_op jit(solution)/shard_map/while/body/eval_jaxpr/ppermute | solution.py:13
  250.2 8.8 collective-permute-start
  259.2 7.4 collective-permute-start
  266.7 8.4 collective-permute-start
  275.3 8.6 collective-permute-start
  284.0 8.6 collective-permute-start
  292.8 8.6 collective-permute-start
  301.5 9.9 %collective-permute-start = (f32[8,64,64]{2,1,0:T(8,128)S(1)}, f32[8,64,64]{2,1,0:T(8,128)S(1)}, u32[]{:S(2)}, u32[]{:S(2)}) collective-permute-start(f32[8,64,64]{2,1,0:T(8,128)S(1)} %multiply_add_fusion.4), channel_id=1, source_target_pairs={{0,8},{8,16},{16,24},{24,32},{32,40},{40,48},{48,56},{56,64},{64,7... | collective-permute-start | bytes 393224 | tf_op jit(solution)/shard_map/while/body/eval_jaxpr/ppermute | solution.py:13
  311.6 11.4 %collective-permute-start = (f32[8,64,64]{2,1,0:T(8,128)S(1)}, f32[8,64,64]{2,1,0:T(8,128)S(1)}, u32[]{:S(2)}, u32[]{:S(2)}) collective-permute-start(f32[8,64,64]{2,1,0:T(8,128)S(1)} %multiply_add_fusion.4), channel_id=1, source_target_pairs={{0,8},{8,16},{16,24},{24,32},{32,40},{40,48},{48,56},{56,64},{64,7... | collective-permute-start | bytes 393224 | tf_op jit(solution)/shard_map/while/body/eval_jaxpr/ppermute | solution.py:13
  323.1 11.3 %collective-permute-start = (f32[8,64,64]{2,1,0:T(8,128)S(1)}, f32[8,64,64]{2,1,0:T(8,128)S(1)}, u32[]{:S(2)}, u32[]{:S(2)}) collective-permute-start(f32[8,64,64]{2,1,0:T(8,128)S(1)} %multiply_add_fusion.4), channel_id=1, source_target_pairs={{0,8},{8,16},{16,24},{24,32},{32,40},{40,48},{48,56},{56,64},{64,7... | collective-permute-start | bytes 393224 | tf_op jit(solution)/shard_map/while/body/eval_jaxpr/ppermute | solution.py:13
  334.6 8.6 collective-permute-start
  350.3 98.3 %copy-start.5 = (bf16[16,4096]{1,0:T(8,128)(2,1)S(1)}, bf16[16,4096]{1,0:T(8,128)(2,1)}, u32[]{:S(2)}) copy-start(bf16[16,4096]{1,0:T(8,128)(2,1)} %param.32) | copy-start | bytes 393220
  350.3 100.6 %copy-start.11 = (f32[4096]{0:T(1024)S(1)}, f32[4096]{0:T(1024)}, u32[]{:S(2)}) copy-start(f32[4096]{0:T(1024)} %param.31) | copy-start | bytes 49156
  350.3 104.3 %copy-start.18 = (s32[16]{0:T(128)S(1)}, s32[16]{0:T(128)}, u32[]{:S(2)}) copy-start(s32[16]{0:T(128)} %param.35) | copy-start | bytes 196
  350.3 252.6 %all-gather.8.cloned.1.call-start = ((), (), s32[]{:S(2)}) async-start(), calls=%async_computation.3 | async-start | bytes 8519680 | tf_op jit(solution)/shard_map/all_gather | solution.py:131
  611.2 194.6 %copy-start.15 = (f32[16]{0:T(128)S(1)}, f32[16]{0:T(128)}, u32[]{:S(2)}) copy-start(f32[16]{0:T(128)} %param.37) | copy-start | bytes 196
  611.3 194.6 %copy-start.16 = (s32[16]{0:T(128)S(1)}, s32[16]{0:T(128)}, u32[]{:S(2)}) copy-start(s32[16]{0:T(128)} %param.36) | copy-start | bytes 196
  (5 other events, 5.7 us)
Sparse Core Ops, SparseCore 0:
  11.0 147.0 all-gather.5
  350.5 98.1 reduce-scatter.1
  452.8 150.1 all-gather.7
where the time goes:
time: 978 us; the launch traced here: 976 us
  blocking collectives  373 us (38%)
  waiting for transfers between devices  357 us (37%)
  starting transfers between devices  163 us (17%)
  other arithmetic  24 us (2%)
  between operations  20.8 us (2%)
  matrix products  19.8 us (2%)
  local copies, waits for them, and re-layouts  14.7 us (2%)
    all_gather x3, blocking collectives, joined(): gathered = jax.tree.map(lambda a: lax.all_gather(a, axis), part)  188 us
    ppermute x31, starting transfers between devices, passed_along(): lax.ppermute(value, axis, [(source, source + steps) for source in range(f...  163 us
    psum x1, blocking collectives, per_device(): seq_ratio = lax.psum(partial_seq, ('blk', 'head'))  161 us
    ppermute x31, waiting for transfers between devices, passed_along(): lax.ppermute(value, axis, [(source, source + steps) for source in range(f...  134 us
    all_gather x1, waiting for transfers between devices, per_device(): rows_n = lax.all_gather(normed, 'blk', axis=0, tiled=True)  124 us
    reduce_scatter x1, waiting for transfers between devices, per_device(): lax.psum_scatter(partial_out, 'head', scatter_dimension=0, tiled=True)  98.3 us
    unnamed x1, blocking collectives  23.9 us
  transfers between devices with their start and end apart: 34, of which 33 were waited for; matrix products, arithmetic and copies ran while one was open for 4% of the time, Pallas kernels for 0%

commit v1 on v0

v1 whole, which is shorter than its diff:
```python
import functools

import jax
import jax.numpy as jnp
from jax import lax
from jax.experimental import pallas as pl
from jax.experimental.pallas import tpu as pltpu
from jax.sharding import Mesh
from jax.sharding import PartitionSpec as P

CHAN = 64
LANES = 128
TOK_BLK = 128
SUB = 32
F32 = jnp.float32
BF16 = jnp.bfloat16


def parts2(a):
    high = a.astype(BF16)
    return high, (a - high.astype(F32)).astype(BF16)


def parts3(a):
    high, rest = a.astype(BF16), None
    rest = a - high.astype(F32)
    mid = rest.astype(BF16)
    return high, mid, (rest - mid.astype(F32)).astype(BF16)


def mm(a, b):
    return jnp.dot(a, b, preferred_element_type=F32)


def mm_t(a, b):
    return lax.dot_general(a, b, (((1,), (1,)), ((), ())), preferred_element_type=F32)


def running_log_decay(rate):
    log_decay = -jnp.exp(rate.astype(F32))
    rows = log_decay.shape[0]
    i = lax.broadcasted_iota(jnp.int32, (rows, rows), 0)
    j = lax.broadcasted_iota(jnp.int32, (rows, rows), 1)
    lower = (i >= j).astype(F32).astype(BF16)
    total = mm(
        jnp.concatenate([lower] * 3, axis=1), jnp.concatenate(parts3(log_decay), axis=0)
    )
    return log_decay, total


def left_lanes(rows):
    return lax.broadcasted_iota(jnp.int32, (rows, LANES), 1) < CHAN


def block_end_kernel(chunk_rows, k_ref, v_ref, w_ref, out_ref):
    _, inclusive = running_log_decay(w_ref[...])
    last = inclusive[TOK_BLK - 1 :, :]
    late = k_ref[...].astype(F32) * jnp.exp(last - inclusive)
    high, low = parts2(late.T)
    v = v_ref[...]
    both = mm(jnp.concatenate([high, low], axis=1), jnp.concatenate([v, v], axis=0))
    fall = jnp.exp(jnp.broadcast_to(last, (LANES, LANES)).T)
    left = left_lanes(CHAN)
    both = jnp.where(left, both[:CHAN], both[CHAN:])
    fall = jnp.where(left, fall[:CHAN], fall[CHAN:])
    for q in range(CHAN // chunk_rows):
        rows = slice(q * chunk_rows, (q + 1) * chunk_rows)
        out_ref[q, :chunk_rows, :] = both[rows]
        out_ref[q, chunk_rows:, :] = fall[rows]


def relay_kernel(chunk_rows, meta_ref, moved_ref, prompt_ref, out_ref):
    def step(b, state):
        prompt = jnp.where(meta_ref[1, b] == 0, prompt_ref[0], prompt_ref[1])
        state = jnp.where(meta_ref[0, b] != 0, prompt, state)
        out_ref[b] = state
        return moved_ref[b, chunk_rows:, :] * state + moved_ref[b, :chunk_rows, :]

    lax.fori_loop(
        0, moved_ref.shape[0], step, jnp.zeros((chunk_rows, LANES), F32), unroll=8
    )


def mix_kernel(r_ref, k_ref, v_ref, w_ref, g_ref, u_ref, scale_ref, state_ref, out_ref):
    r = r_ref[...].astype(F32)
    k = k_ref[...].astype(F32)
    v = v_ref[...]
    log_decay, inclusive = running_log_decay(w_ref[...])
    exclusive = inclusive - log_decay
    left = left_lanes(SUB)
    pieces = []
    for sub in range(TOK_BLK // SUB):
        a, b = sub * SUB, (sub + 1) * SUB
        pivot = inclusive[a + SUB // 2 - 1 : a + SUB // 2, :]
        rs = r[a:b] * jnp.exp(exclusive[a:b] - pivot)
        ks = k[:b] * jnp.exp(pivot - inclusive[:b])
        rs = jnp.concatenate([jnp.where(left, rs, 0.0), jnp.where(left, 0.0, rs)], axis=0)
        rh, rl = parts2(rs)
        kh, kl = parts2(ks)
        scores = mm_t(
            jnp.concatenate([rh, rl, rh], axis=1), jnp.concatenate([kh, kh, kl], axis=1)
        )
        t = lax.broadcasted_iota(jnp.int32, scores.shape, 0) % SUB + a
        s = lax.broadcasted_iota(jnp.int32, scores.shape, 1)
        sh, sl = parts2(jnp.where(s < t, scores, 0.0))
        both = mm(sh, v[:b]) + mm(sl, v[:b])
        pieces.append(jnp.where(left, both[:SUB], both[SUB:]))
    wkv = jnp.concatenate(pieces, axis=0)
    i = lax.broadcasted_iota(jnp.int32, (LANES, LANES), 0) // CHAN
    j = lax.broadcasted_iota(jnp.int32, (LANES, LANES), 1) // CHAN
    same = (i == j).astype(F32)
    ones = jnp.concatenate([same.astype(BF16)] * 2, axis=0)
    mean_of = jnp.concatenate([(same / CHAN).astype(BF16)] * 2, axis=0)
    now = mm(jnp.concatenate(parts2(r * k * u_ref[...]), axis=1), ones)
    wkv = wkv + now * v.astype(F32)
    state = state_ref[...]
    left = left_lanes(CHAN)
    state = jnp.concatenate([jnp.where(left, state, 0.0), jnp.where(left, 0.0, state)], axis=0)
    rh, rl = parts2(r * jnp.exp(exclusive))
    sh, sl = parts2(state)
    wkv = wkv + mm(
        jnp.concatenate([rh, rl, rh], axis=1), jnp.concatenate([sh, sh, sl], axis=0)
    )
    mean = mm(jnp.concatenate(parts2(wkv), axis=1), mean_of)
    off = wkv - mean
    var = mm(jnp.concatenate(parts2(off * off), axis=1), mean_of)
    g = g_ref[...].astype(F32)
    y = off / jnp.sqrt(var + 0.00064) * scale_ref[...]
    out_ref[...] = (y * (g / (1.0 + jnp.exp(-g)))).astype(out_ref.dtype)


def cost(flops, nbytes):
    return pl.CostEstimate(flops=flops, bytes_accessed=nbytes, transcendentals=0)


def shifted(value, axis, steps):
    count = lax.axis_size(axis)
    return lax.ppermute(value, axis, [(i, (i + steps) % count) for i in range(count)])


def per_device(
    acceptance_vector,
    lookup_vector_array,
    payload_vector_array,
    raw_gating_signal,
    raw_forgetting_rate,
    current_reward_vector,
    memory_following_query,
    group_layernorm_scaling,
    closing_layernorm_scaling,
    skip_stream_input,
    closing_projection,
    vocabulary_readout,
    following_labels,
    response_indicator,
    baseline_logarithmic_likelihood,
    rollout_for_segment,
    query_text_for_rollout,
):
    nx, nz, ny, nc = (lax.axis_size(a) for a in ("x", "z", "y", "c"))
    ix, iz, iy, ic = (lax.axis_index(a) for a in ("x", "z", "y", "c"))
    n_blk, n_head = nx * nz, ny * nc
    blk, head = ix * nz + iz, iy * nc + ic
    rows, width = acceptance_vector.shape
    embed = skip_stream_input.shape[1]
    pairs = width // LANES
    own = rows // n_head

    proj = lax.all_gather(closing_projection, "z", axis=1, tiled=True)
    share = vocabulary_readout.shape[0] // n_head
    vocab_share = lax.dynamic_slice_in_dim(vocabulary_readout, head * share, share)

    chunks = n_blk // pairs
    chunk_rows = CHAN // chunks
    col = pl.BlockSpec((rows, LANES), lambda p: (0, p))
    end = pl.pallas_call(
        functools.partial(block_end_kernel, chunk_rows),
        grid=(pairs,),
        in_specs=[col] * 3,
        out_specs=pl.BlockSpec((chunks, 2 * chunk_rows, LANES), lambda p: (p, 0, 0)),
        out_shape=jax.ShapeDtypeStruct((n_blk, 2 * chunk_rows, LANES), F32),
        cost_estimate=cost(pairs * 20_000_000, 3 * rows * width * 2),
    )(lookup_vector_array, payload_vector_array, raw_forgetting_rate)
    moved = lax.all_to_all(end, ("x", "z"), 0, 0, tiled=True)

    prev_seq = jnp.concatenate([jnp.full((1,), -1, jnp.int32), rollout_for_segment[:-1]])
    starts = (rollout_for_segment != prev_seq).astype(jnp.int32)
    meta = jnp.stack([starts, query_text_for_rollout[rollout_for_segment]])
    prompts = memory_following_query.shape[0]
    prompt = lax.dynamic_slice(
        memory_following_query.reshape(prompts, pairs, 2, CHAN, CHAN),
        (0, blk // chunks, 0, (blk % chunks) * chunk_rows, 0),
        (prompts, 1, 2, chunk_rows, CHAN),
    )[:, 0]
    prompt = prompt.transpose(0, 2, 1, 3).reshape(prompts, chunk_rows, LANES).astype(F32)
    vmem = pl.BlockSpec(memory_space=pltpu.VMEM)
    entering = pl.pallas_call(
        functools.partial(relay_kernel, chunk_rows),
        in_specs=[pl.BlockSpec(memory_space=pltpu.SMEM), vmem, vmem],
        out_specs=vmem,
        out_shape=jax.ShapeDtypeStruct((n_blk, chunk_rows, LANES), F32),
        cost_estimate=cost(1_000_000, 500_000),
    )(meta, moved, prompt)
    entering = lax.all_to_all(entering, ("x", "z"), 0, 0, tiled=True)
    entering = entering.reshape(pairs * CHAN, LANES)

    row = pl.BlockSpec((1, LANES), lambda p: (0, p))
    mixed = pl.pallas_call(
        mix_kernel,
        grid=(pairs,),
        in_specs=[col] * 5 + [row] * 2 + [pl.BlockSpec((CHAN, LANES), lambda p: (p, 0))],
        out_specs=col,
        out_shape=jax.ShapeDtypeStruct((rows, width), BF16),
        cost_estimate=cost(pairs * 60_000_000, 6 * rows * width * 2),
    )(
        acceptance_vector,
        lookup_vector_array,
        payload_vector_array,
        raw_forgetting_rate,
        raw_gating_signal,
        current_reward_vector[None, :],
        group_layernorm_scaling[None, :],
        entering,
    )

    mixed = lax.all_gather(mixed, "x", axis=0)
    mixed = mixed.reshape(nx, ny, nc, own, width).transpose(2, 1, 0, 3, 4)
    mixed = mixed.reshape(nc, ny * nx * own, width)
    theirs = mm(lax.dynamic_index_in_dim(mixed, 1 - ic, 0, False), proj)
    mine = mm(lax.dynamic_index_in_dim(mixed, ic, 0, False), proj)
    partial = mine + shifted(theirs, "c", 1)
    partial = partial.reshape(ny * nx, own, embed // nx)
    partial = lax.all_to_all(partial, ("y", "x"), 0, 0, tiled=True)
    projected = jnp.sum(partial.reshape(ny, nx, own, embed // nx), axis=0)
    projected = projected.transpose(1, 0, 2).reshape(own, embed)
    hidden = skip_stream_input.astype(F32) + projected
    hmean = jnp.mean(hidden, axis=-1, keepdims=True)
    hvar = jnp.mean((hidden - hmean) ** 2, axis=-1, keepdims=True)
    normed = ((hidden - hmean) / jnp.sqrt(hvar + 1e-05) * closing_layernorm_scaling).astype(BF16)

    tokens = lax.all_gather(normed, "y", axis=0, tiled=True)
    tokens = jnp.concatenate([tokens] + [shifted(tokens, "x", s) for s in range(1, nx)], axis=0)
    other = shifted(tokens, "c", 1)
    vocab_rows = lax.all_gather(vocab_share, "z", axis=0, tiled=True)

    facts = jnp.stack(
        [
            following_labels.astype(F32),
            response_indicator.astype(F32),
            baseline_logarithmic_likelihood,
        ]
    )
    facts, _ = lax.optimization_barrier((facts, other))
    facts = lax.all_gather(facts, ("x", "y", "c"), axis=0)
    facts = facts.reshape(nx, ny, nc, 3, own).transpose(3, 2, 0, 1, 4)
    labels = facts[0].astype(jnp.int32)
    back = (ix - jnp.arange(nx)) % nx

    index = jnp.arange(nz * share, dtype=jnp.int32)
    vocab_local = vocabulary_readout.shape[0]
    entry = (ix * nz + index // share) * vocab_local + head * share + index % share

    def score(toks, core):
        logits = mm_t(toks, vocab_rows)
        top = jnp.max(logits, axis=1)
        total = jnp.sum(jnp.exp(logits - top[:, None]), axis=1)
        wanted = lax.dynamic_index_in_dim(labels, core, 0, False)[back].reshape(-1)
        picked = jnp.sum(jnp.where(entry[None, :] == wanted[:, None], logits, 0.0), axis=1)
        both = jnp.stack([top + jnp.log(total), picked])
        return both.reshape(2, nx, ny * own)[:, back]

    first, second = score(tokens, ic), score(other, 1 - ic)
    both = jnp.where(
        ic == 0, jnp.stack([first, second], axis=1), jnp.stack([second, first], axis=1)
    )
    plane = nx * ny * nc
    count = plane * own
    both = jnp.broadcast_to(both.reshape(1, 2 * count // LANES, LANES), (plane, 2 * count // LANES, LANES))
    both = lax.all_to_all(both, ("x", "y", "c"), 0, 0, tiled=True).reshape(plane, 2, count)
    part, picked = both[:, 0], both[:, 1]
    peak = jnp.max(part, axis=0)
    logp = jnp.sum(picked, axis=0) - peak - jnp.log(jnp.sum(jnp.exp(part - peak), axis=0))
    ratio = facts[1] * (logp.reshape(nc, nx, ny, own) - facts[2])
    token_ratio = lax.dynamic_slice(ratio, (ic, ix, iy, 0), (1, 1, 1, own)).reshape(own)

    sums = jnp.sum(ratio, axis=(0, 2, 3))
    sums = jnp.broadcast_to(jnp.pad(sums, (0, LANES - nx)), (nz, 1, LANES))
    sums = lax.all_to_all(sums, "z", 0, 0, tiled=True)[:, 0, :nx]
    seq_of = rollout_for_segment.reshape(nx, nz).T
    marker = jnp.arange(query_text_for_rollout.shape[0])[:, None, None] == seq_of[None]
    seq_ratio = jnp.sum(jnp.where(marker, sums[None], 0.0), axis=(1, 2)) / TOK_BLK
    return (token_ratio, seq_ratio)


def solution(mesh):
    n_blk, n_head = mesh.devices.shape
    nx, nc = 4, 2
    fine = Mesh(
        mesh.devices.reshape(nx, n_blk // nx, n_head // nc, nc), ("x", "z", "y", "c")
    )
    blk, head = ("x", "z"), ("y", "c")
    placed = (
        P(blk, head),
        P(blk, head),
        P(blk, head),
        P(blk, head),
        P(blk, head),
        P(head),
        P(None, head, None),
        P(head),
        P(),
        P(blk + head, None),
        P(head, blk),
        P(blk, None),
        P(blk + head),
        P(blk + head),
        P(blk + head),
        P(),
        P(),
    )
    return jax.shard_map(
        per_device, mesh=fine, in_specs=placed, out_specs=(P(blk + head), P()), check_vma=False
    )
```

time: 978 us -> 256 us (0.26)
  blocking collectives: 373 us -> 67.1 us
  waiting for transfers between devices: 357 us -> 80.6 us
  starting transfers between devices: 163 us -> 54.8 us
  other arithmetic: 24 us -> 2.97 us
  Pallas kernels: 0 us -> 12.2 us
    psum x1 -> x0, blocking collectives: 161 us -> none  [per_device(): seq_ratio = lax.psum(partial_seq, ('blk', 'head'))]
    all_gather x3, blocking collectives: 188 us -> 45.3 us  [the longest x1 24.1 us: per_device(): facts = lax.all_gather(facts, ('x', 'y', 'c'), axis=0)]
    ppermute x31 -> x5, starting transfers between devices: 163 us -> 20.7 us  [shifted(): lax.ppermute(value, axis, [(i, (i + steps) % count) for i in range(count)])]
    all_gather x2, waiting for transfers between devices: 124 us -> 0.02 us  [the longest x1 0.02 us: per_device(): proj = lax.all_gather(closing_projection, 'z', axis=1, tiled=True)]
    ppermute x31 -> x5, waiting for transfers between devices: 134 us -> 26.4 us  [shifted(): lax.ppermute(value, axis, [(i, (i + steps) % count) for i in range(count)])]
    reduce_scatter x1 -> x0, waiting for transfers between devices: 98.3 us -> none  [per_device(): lax.psum_scatter(partial_out, 'head', scatter_dimension=0, tiled=True)]
    all_to_all x0 -> x4, waiting for transfers between devices: none -> 53.6 us  [the longest x1 19.7 us: per_device(): moved = lax.all_to_all(end, ('x', 'z'), 0, 0, tiled=True)]
    all_to_all x0 -> x4, starting transfers between devices: none -> 34.1 us  [the longest x1 19.1 us: per_device(): moved = lax.all_to_all(end, ('x', 'z'), 0, 0, tiled=True)]
  transfers between devices with their start and end apart: 34 -> 11, of which waited for: 33 -> 9; matrix products, arithmetic and copies ran while one was open for 4% -> 4% of each run, Pallas kernels for 0% -> 5%
where the time goes in v1:
time: 256 us; the launch traced here: 255 us
  waiting for transfers between devices  80.6 us (31%)
  blocking collectives  67.1 us (26%)
  starting transfers between devices  54.8 us (21%)
  between operations  14.5 us (6%)
  matrix products  12.5 us (5%)
  Pallas kernels  12.2 us (5%)
  local copies, waits for them, and re-layouts  10.4 us (4%)
  other arithmetic  2.97 us (1%)
    ppermute x5, waiting for transfers between devices, shifted(): lax.ppermute(value, axis, [(i, (i + steps) % count) for i in range(count)])  26.4 us
    all_gather x1, blocking collectives, per_device(): facts = lax.all_gather(facts, ('x', 'y', 'c'), axis=0)  24.1 us
    all_to_all x1, blocking collectives, per_device(): partial = lax.all_to_all(partial, ('y', 'x'), 0, 0, tiled=True)  21.9 us
    ppermute x5, starting transfers between devices, shifted(): lax.ppermute(value, axis, [(i, (i + steps) % count) for i in range(count)])  20.7 us
    all_to_all x1, waiting for transfers between devices, per_device(): moved = lax.all_to_all(end, ('x', 'z'), 0, 0, tiled=True)  19.7 us
    all_to_all x1, starting transfers between devices, per_device(): moved = lax.all_to_all(end, ('x', 'z'), 0, 0, tiled=True)  19.1 us
    all_to_all x1, waiting for transfers between devices, per_device(): entering = lax.all_to_all(entering, ('x', 'z'), 0, 0, tiled=True)  15.4 us
    all_gather x1, blocking collectives, per_device(): tokens = lax.all_gather(normed, 'y', axis=0, tiled=True)  11.1 us
  transfers between devices with their start and end apart: 11, of which 9 were waited for; matrix products, arithmetic and copies ran while one was open for 4% of the time, Pallas kernels for 5%

profile of v1, /device:TPU:1, one launch (start us, length us, event | category | flops | bytes accessed | tf_op | source)
XLA Modules:
  0.0 255.2 jit_solution(15966342224433148654)
XLA Ops:
  7.2 0.7 all-gather.6.cloned.1.call-update
  8.0 1.9 constant_dynamic-slice_fusion.1
  9.9 3.7 %shard_map.176 = f32[64,8,128]{2,1,0:T(8,128)} custom-call(bf16[128,512]{1,0:T(8,128)(2,1)} %k_ref.3, bf16[128,512]{1,0:T(8,128)(2,1)} %v_ref.3, bf16[128,512]{1,0:T(8,128)(2,1)} %w_ref.3), custom_call_target="tpu_custom_call" | custom-call | flops 80000000 | bytes 393216 | tf_op jit(solution)/shard_map/pallas_call | solution.py:176
  13.6 19.1 %all-to-all-start = ((f32[64,8,128]{2,1,0:T(8,128)}), f32[64,8,128]{2,1,0:T(8,128)S(1)}, u32[]{:S(2)}, u32[]{:S(2)}) async-start(f32[64,8,128]{2,1,0:T(8,128)} %shard_map.176), calls=%async_computation | async-start | bytes 524288 | tf_op jit(solution)/shard_map/all_to_all | solution.py:184
  32.8 0.2 reshape.215
  33.2 0.7 reshape.227.prompt_ref
  33.9 0.8 gather_fusion
  34.8 0.6 pad_add_fusion.meta_ref
  35.3 19.7 %all-to-all-done.moved_ref = f32[64,8,128]{2,1,0:T(8,128)S(1)} async-done(((f32[64,8,128]{2,1,0:T(8,128)}), f32[64,8,128]{2,1,0:T(8,128)S(1)}, u32[]{:S(2)}, u32[]{:S(2)}) %all-to-all-start) | async-done | bytes 262176 | tf_op jit(solution)/shard_map/all_to_all | solution.py:184
  55.1 0.7 copy-done.3
  55.8 1.9 shard_map.177
  57.7 6.8 %all-to-all-start.1 = ((f32[64,4,128]{2,1,0:T(4,128)}), f32[64,4,128]{2,1,0:T(4,128)S(1)}, u32[]{:S(2)}, u32[]{:S(2)}) async-start(f32[64,4,128]{2,1,0:T(4,128)} %shard_map.177), calls=%async_computation.1 | async-start | bytes 262144 | tf_op jit(solution)/shard_map/all_to_all | solution.py:204
  64.5 15.4 %all-to-all-done.1 = f32[64,4,128]{2,1,0:T(4,128)S(1)} async-done(((f32[64,4,128]{2,1,0:T(4,128)}), f32[64,4,128]{2,1,0:T(4,128)S(1)}, u32[]{:S(2)}, u32[]{:S(2)}) %all-to-all-start.1) | async-done | bytes 131104 | tf_op jit(solution)/shard_map/all_to_all | solution.py:204
  79.9 0.6 copy-done.4
  80.6 6.6 %shard_map.178 = bf16[128,512]{1,0:T(8,128)(2,1)} custom-call(bf16[128,512]{1,0:T(8,128)(2,1)} %r_ref.1, bf16[128,512]{1,0:T(8,128)(2,1)} %k_ref.3, bf16[128,512]{1,0:T(8,128)(2,1)} %v_ref.3, bf16[128,512]{1,0:T(8,128)(2,1)} %w_ref.3, bf16[128,512]{1,0:T(8,128)(2,1)} %g_ref.1, f32[1,512]{1,0:T(1,128)} %bitcast.100, f32[1,512]{1,0:T(1,128)} %bitcast.101, ...), custom_call_target="tpu_custom_call" | custom-call | flops 240000000 | bytes 786432 | tf_op jit(solution)/shard_map/pallas_call | solution.py:208
  87.2 10.1 %all-gather = bf16[512,512]{1,0:T(8,128)(2,1)S(1)} all-gather(bf16[128,512]{1,0:T(8,128)(2,1)} %shard_map.178), channel_id=2, replica_groups=mesh['x'=4,'z'=16,'y'=4,'c'=2] {'x'}, dimensions={0}, use_global_device_ids=true | all-gather | bytes 655360 | tf_op jit(solution)/shard_map/all_gather | solution.py:226
  97.3 1.8 fusion
  99.1 7.7 %collective-permute-start = (f32[256,1024]{1,0:T(8,128)S(1)}, f32[256,1024]{1,0:T(8,128)}, u32[]{:S(2)}, u32[]{:S(2)}) collective-permute-start(f32[256,1024]{1,0:T(8,128)S(1)} %fusion), channel_id=1, source_target_pairs={{0,1},{1,0},{2,3},{3,2},{4,5},{5,4},{6,7},{7,6},{8,9},{9,8},{10,11... | collective-permute-start | bytes 3145736 | tf_op jit(solution)/shard_map/ppermute | solution.py:138
  106.9 2.4 collective-permute-done
  109.3 1.7 convolution_add_fusion
  111.0 21.9 %all_to_all.25 = f32[16,16,1024]{2,1,0:T(8,128)S(1)} all-to-all(f32[16,16,1024]{2,1,0:T(8,128)S(1)} %bitcast.80), channel_id=1, replica_groups=mesh['x'=4,'z'=16,'y'=4,'c'=2] {'y','x'}, dimensions={0} | all-to-all | bytes 2097152 | tf_op jit(solution)/shard_map/all_to_all | solution.py:233
  133.0 0.2 fusion.5
  133.2 0.2 multiply_reduce_fusion
  133.5 11.1 %all_gather.24 = bf16[64,4096]{1,0:T(8,128)(2,1)S(1)} all-gather(bf16[16,4096]{1,0:T(8,128)(2,1)S(1)} %multiply_convert_fusion), channel_id=1, replica_groups=mesh['x'=4,'z'=16,'y'=4,'c'=2] {'y'}, dimensions={0}, use_global_device_ids=true | all-gather | bytes 655360 | tf_op jit(solution)/shard_map/all_gather | solution.py:241
  144.6 2.3 collective-permute-start.1
  146.9 3.2 %collective-permute-start.2 = (bf16[64,4096]{1,0:T(8,128)(2,1)S(1)}, bf16[64,4096]{1,0:T(8,128)(2,1)S(1)}, u32[]{:S(2)}, u32[]{:S(2)}) collective-permute-start(bf16[64,4096]{1,0:T(8,128)(2,1)S(1)} %all_gather.24), channel_id=1, source_target_pairs={{0,256},{128,384},{256,0},{384,128},{1,257},{129,385},{257,1},{385... | collective-permute-start | bytes 1572872 | tf_op jit(solution)/shard_map/ppermute | solution.py:138
  150.2 3.9 %collective-permute-start.3 = (bf16[64,4096]{1,0:T(8,128)(2,1)S(1)}, bf16[64,4096]{1,0:T(8,128)(2,1)S(1)}, u32[]{:S(2)}, u32[]{:S(2)}) collective-permute-start(bf16[64,4096]{1,0:T(8,128)(2,1)S(1)} %all_gather.24), channel_id=1, source_target_pairs={{0,384},{128,0},{256,128},{384,256},{1,385},{129,1},{257,129},{385... | collective-permute-start | bytes 1572872 | tf_op jit(solution)/shard_map/ppermute | solution.py:138
  154.0 4.1 %collective-permute-done.1 = bf16[64,4096]{1,0:T(8,128)(2,1)S(1)} collective-permute-done((bf16[64,4096]{1,0:T(8,128)(2,1)S(1)}, bf16[64,4096]{1,0:T(8,128)(2,1)S(1)}, u32[]{:S(2)}, u32[]{:S(2)}) %collective-permute-start.1) | collective-permute-done | bytes 524320 | tf_op jit(solution)/shard_map/ppermute | solution.py:138
  158.1 9.4 %collective-permute-done.2 = bf16[64,4096]{1,0:T(8,128)(2,1)S(1)} collective-permute-done((bf16[64,4096]{1,0:T(8,128)(2,1)S(1)}, bf16[64,4096]{1,0:T(8,128)(2,1)S(1)}, u32[]{:S(2)}, u32[]{:S(2)}) %collective-permute-start.2) | collective-permute-done | bytes 524320 | tf_op jit(solution)/shard_map/ppermute | solution.py:138
  167.6 6.7 %collective-permute-done.3 = bf16[64,4096]{1,0:T(8,128)(2,1)S(1)} collective-permute-done((bf16[64,4096]{1,0:T(8,128)(2,1)S(1)}, bf16[64,4096]{1,0:T(8,128)(2,1)S(1)}, u32[]{:S(2)}, u32[]{:S(2)}) %collective-permute-start.3) | collective-permute-done | bytes 524320 | tf_op jit(solution)/shard_map/ppermute | solution.py:138
  174.3 3.6 %collective-permute-start.4 = (bf16[256,4096]{1,0:T(8,128)(2,1)S(1)}, bf16[256,4096]{1,0:T(8,128)(2,1)}, u32[]{:S(2)}, u32[]{:S(2)}) collective-permute-start(bf16[256,4096]{1,0:T(8,128)(2,1)S(1)} %constant_dynamic-update-slice_fusion), channel_id=1, source_target_pairs={{0,1},{1,0},{2,3},{3,2},{4,5},{5,4},{6,7},{7,6},{8,9},{9,8},{10,11... | collective-permute-start | bytes 6291464 | tf_op jit(solution)/shard_map/ppermute | solution.py:138
  178.0 3.8 %collective-permute-done.4 = bf16[256,4096]{1,0:T(8,128)(2,1)} collective-permute-done((bf16[256,4096]{1,0:T(8,128)(2,1)S(1)}, bf16[256,4096]{1,0:T(8,128)(2,1)}, u32[]{:S(2)}, u32[]{:S(2)}) %collective-permute-start.4) | collective-permute-done | bytes 2097184 | tf_op jit(solution)/shard_map/ppermute | solution.py:138
  181.8 24.1 %all-gather.2 = f32[32,3,16]{2,1,0:T(4,128)S(1)} all-gather(f32[1,3,16]{2,1,0:T(4,128)S(1)} %bitcast.96), channel_id=3, replica_groups=mesh['x'=4,'z'=16,'y'=4,'c'=2] {'x','y','c'}, dimensions={0}, use_global_device_ids=true | all-gather | bytes 6336 | tf_op jit(solution)/shard_map/all_gather | solution.py:254
  206.0 0.6 gather_fusion.1
  206.6 0.6 gather_fusion.3
  207.3 6.6 %fusion.30 = (f32[256]{0:T(256)S(1)}, f32[256,1024]{1,0:T(8,128)S(1)}) fusion(bf16[256,4096]{1,0:T(8,128)(2,1)} %collective-permute-done.4, bf16[1024,4096]{1,0:T(8,128)(2,1)} %all-gather.8.cloned.1.call-done), kind=kOutput, calls=%fused_computation.86 | convolution fusion | flops 2147745536 | bytes 11535360 | tf_op jit(solution)/shard_map/dot_general | solution.py:36
  213.9 2.4 fusion.29
  216.3 0.7 exponential_reduce_fusion.1
  217.2 0.6 gather_fusion.2
  218.0 0.6 gather_fusion.4
  218.7 0.6 broadcast_in_dim.54
  219.3 4.3 %all-to-all-start.3 = ((f32[32,8,128]{2,1,0:T(8,128)}), f32[32,8,128]{2,1,0:T(8,128)S(1)}, u32[]{:S(2)}, u32[]{:S(2)}) async-start(f32[32,8,128]{2,1,0:T(8,128)} %broadcast_in_dim.54), calls=%async_computation.3 | async-start | bytes 262144 | tf_op jit(solution)/shard_map/all_to_all | solution.py:279
  223.7 7.6 %all-to-all-done.3 = f32[32,8,128]{2,1,0:T(8,128)S(1)} async-done(((f32[32,8,128]{2,1,0:T(8,128)}), f32[32,8,128]{2,1,0:T(8,128)S(1)}, u32[]{:S(2)}, u32[]{:S(2)}) %all-to-all-start.3) | async-done | bytes 131104 | tf_op jit(solution)/shard_map/all_to_all | solution.py:279
  231.8 0.6 broadcast_in_dim.55
  232.4 3.9 %all-to-all-start.4 = ((f32[16,1,128]{2,1,0:T(1,128)}), f32[16,1,128]{2,1,0:T(1,128)S(1)}, u32[]{:S(2)}, u32[]{:S(2)}) async-start(f32[16,1,128]{2,1,0:T(1,128)} %broadcast_in_dim.55), calls=%async_computation.4 | async-start | bytes 16384 | tf_op jit(solution)/shard_map/all_to_all | solution.py:288
  236.3 0.5 fusion.23
  236.8 10.8 %all-to-all-done.4 = f32[16,1,128]{2,1,0:T(1,128)S(1)} async-done(((f32[16,1,128]{2,1,0:T(1,128)}), f32[16,1,128]{2,1,0:T(1,128)S(1)}, u32[]{:S(2)}, u32[]{:S(2)}) %all-to-all-start.4) | async-done | bytes 8224 | tf_op jit(solution)/shard_map/all_to_all | solution.py:288
  247.8 0.5 broadcast_multiply_fusion
  (74 shorter events, 2.4 us)
Async XLA Ops:
  7.2 26.8 %copy-start = (s32[16]{0:T(128)S(1)}, s32[16]{0:T(128)}, u32[]{:S(2)}) copy-start(s32[16]{0:T(128)} %param.33) | copy-start | bytes 196
  7.2 25.6 %copy-start.5 = (bf16[2,512,64]{1,2,0:T(8,128)(2,1)S(1)}, bf16[2,512,64]{1,2,0:T(8,128)(2,1)}, u32[]{:S(2)}) copy-start(bf16[2,512,64]{1,2,0:T(8,128)(2,1)} %param.23) | copy-start | bytes 393220
  7.2 26.7 %copy-start.7 = (s32[64]{0:T(128)S(1)}, s32[64]{0:T(128)}, u32[]{:S(2)}) copy-start(s32[64]{0:T(128)} %param.32) | copy-start | bytes 772
  7.2 90.1 %all-gather.6.cloned.1.call-start = ((), (), s32[]{:S(2)}) async-start(), calls=%async_computation.5 | async-start | bytes 1114112 | tf_op jit(solution)/shard_map/all_gather | solution.py:169
  7.9 199.3 %all-gather.8.cloned.1.call-start = ((), (), s32[]{:S(2)}) async-start(), calls=%async_computation.6 | async-start | bytes 8912896 | tf_op jit(solution)/shard_map/all_gather | solution.py:244
  13.6 41.5 %all-to-all-start = ((f32[64,8,128]{2,1,0:T(8,128)}), f32[64,8,128]{2,1,0:T(8,128)S(1)}, u32[]{:S(2)}, u32[]{:S(2)}) async-start(f32[64,8,128]{2,1,0:T(8,128)} %shard_map.176), calls=%async_computation | async-start | bytes 524288 | tf_op jit(solution)/shard_map/all_to_all | solution.py:184
  55.1 0.7 copy-start.3
  57.7 22.2 %all-to-all-start.1 = ((f32[64,4,128]{2,1,0:T(4,128)}), f32[64,4,128]{2,1,0:T(4,128)S(1)}, u32[]{:S(2)}, u32[]{:S(2)}) async-start(f32[64,4,128]{2,1,0:T(4,128)} %shard_map.177), calls=%async_computation.1 | async-start | bytes 262144 | tf_op jit(solution)/shard_map/all_to_all | solution.py:204
  79.9 0.7 copy-start.4
  97.3 11.9 %copy-start.1 = (bf16[512,1024]{0,1:T(8,128)(2,1)S(1)}, bf16[512,1024]{0,1:T(8,128)(2,1)}, u32[]{:S(2)}) copy-start(bf16[512,1024]{0,1:T(8,128)(2,1)} %all-gather.6.cloned.1.call-done) | copy-start | bytes 3145732
  99.1 10.1 %collective-permute-start = (f32[256,1024]{1,0:T(8,128)S(1)}, f32[256,1024]{1,0:T(8,128)}, u32[]{:S(2)}, u32[]{:S(2)}) collective-permute-start(f32[256,1024]{1,0:T(8,128)S(1)} %fusion), channel_id=1, source_target_pairs={{0,1},{1,0},{2,3},{3,2},{4,5},{5,4},{6,7},{7,6},{8,9},{9,8},{10,11... | collective-permute-start | bytes 3145736 | tf_op jit(solution)/shard_map/ppermute | solution.py:138
  111.0 22.0 %copy-start.2 = (bf16[16,4096]{1,0:T(8,128)(2,1)S(1)}, bf16[16,4096]{1,0:T(8,128)(2,1)}, u32[]{:S(2)}) copy-start(bf16[16,4096]{1,0:T(8,128)(2,1)} %param.26) | copy-start | bytes 393220
  111.0 22.4 %copy-start.6 = (f32[4096]{0:T(1024)S(1)}, f32[4096]{0:T(1024)}, u32[]{:S(2)}) copy-start(f32[4096]{0:T(1024)} %param.25) | copy-start | bytes 49156
  144.6 33.3 %copy-start.9 = (s32[16]{0:T(128)S(1)}, s32[16]{0:T(128)}, u32[]{:S(2)}) copy-start(s32[16]{0:T(128)} %param.30) | copy-start | bytes 196
  144.6 33.3 %copy-start.10 = (s32[16]{0:T(128)S(1)}, s32[16]{0:T(128)}, u32[]{:S(2)}) copy-start(s32[16]{0:T(128)} %param.29) | copy-start | bytes 196
  144.6 33.4 %copy-start.8 = (f32[16]{0:T(128)S(1)}, f32[16]{0:T(128)}, u32[]{:S(2)}) copy-start(f32[16]{0:T(128)} %param.31) | copy-start | bytes 196
  144.6 13.5 %collective-permute-start.1 = (bf16[64,4096]{1,0:T(8,128)(2,1)S(1)}, bf16[64,4096]{1,0:T(8,128)(2,1)S(1)}, u32[]{:S(2)}, u32[]{:S(2)}) collective-permute-start(bf16[64,4096]{1,0:T(8,128)(2,1)S(1)} %all_gather.24), channel_id=1, source_target_pairs={{0,128},{128,256},{256,384},{384,0},{1,129},{129,257},{257,385},{3... | collective-permute-start | bytes 1572872 | tf_op jit(solution)/shard_map/ppermute | solution.py:138
  146.9 20.6 %collective-permute-start.2 = (bf16[64,4096]{1,0:T(8,128)(2,1)S(1)}, bf16[64,4096]{1,0:T(8,128)(2,1)S(1)}, u32[]{:S(2)}, u32[]{:S(2)}) collective-permute-start(bf16[64,4096]{1,0:T(8,128)(2,1)S(1)} %all_gather.24), channel_id=1, source_target_pairs={{0,256},{128,384},{256,0},{384,128},{1,257},{129,385},{257,1},{385... | collective-permute-start | bytes 1572872 | tf_op jit(solution)/shard_map/ppermute | solution.py:138
  150.2 24.1 %collective-permute-start.3 = (bf16[64,4096]{1,0:T(8,128)(2,1)S(1)}, bf16[64,4096]{1,0:T(8,128)(2,1)S(1)}, u32[]{:S(2)}, u32[]{:S(2)}) collective-permute-start(bf16[64,4096]{1,0:T(8,128)(2,1)S(1)} %all_gather.24), channel_id=1, source_target_pairs={{0,384},{128,0},{256,128},{384,256},{1,385},{129,1},{257,129},{385... | collective-permute-start | bytes 1572872 | tf_op jit(solution)/shard_map/ppermute | solution.py:138
  174.3 7.5 %collective-permute-start.4 = (bf16[256,4096]{1,0:T(8,128)(2,1)S(1)}, bf16[256,4096]{1,0:T(8,128)(2,1)}, u32[]{:S(2)}, u32[]{:S(2)}) collective-permute-start(bf16[256,4096]{1,0:T(8,128)(2,1)S(1)} %constant_dynamic-update-slice_fusion), channel_id=1, source_target_pairs={{0,1},{1,0},{2,3},{3,2},{4,5},{5,4},{6,7},{7,6},{8,9},{9,8},{10,11... | collective-permute-start | bytes 6291464 | tf_op jit(solution)/shard_map/ppermute | solution.py:138
  207.3 6.6 %copy-start.11 = (bf16[1024,4096]{1,0:T(8,128)(2,1)S(1)}, bf16[1024,4096]{1,0:T(8,128)(2,1)}, u32[]{:S(2)}) copy-start(bf16[1024,4096]{1,0:T(8,128)(2,1)} %all-gather.8.cloned.1.call-done) | copy-start | bytes 25165828
  219.3 12.0 %all-to-all-start.3 = ((f32[32,8,128]{2,1,0:T(8,128)}), f32[32,8,128]{2,1,0:T(8,128)S(1)}, u32[]{:S(2)}, u32[]{:S(2)}) async-start(f32[32,8,128]{2,1,0:T(8,128)} %broadcast_in_dim.54), calls=%async_computation.3 | async-start | bytes 262144 | tf_op jit(solution)/shard_map/all_to_all | solution.py:279
  232.4 15.2 %all-to-all-start.4 = ((f32[16,1,128]{2,1,0:T(1,128)}), f32[16,1,128]{2,1,0:T(1,128)S(1)}, u32[]{:S(2)}, u32[]{:S(2)}) async-start(f32[16,1,128]{2,1,0:T(1,128)} %broadcast_in_dim.55), calls=%async_computation.4 | async-start | bytes 16384 | tf_op jit(solution)/shard_map/all_to_all | solution.py:288
Sparse Core Ops, SparseCore 0:
  10.1 72.5 all-gather.5
  84.8 110.0 all-gather.7

commit v2 on v1

--- a/solution.py
+++ b/solution.py
@@ -81,7 +81,7 @@
     )
 
 
-def mix_kernel(r_ref, k_ref, v_ref, w_ref, g_ref, u_ref, scale_ref, state_ref, out_ref):
+def within_kernel(r_ref, k_ref, v_ref, w_ref, u_ref, wkv_ref, high_ref, low_ref):
     r = r_ref[...].astype(F32)
     k = k_ref[...].astype(F32)
     v = v_ref[...]
@@ -105,22 +105,27 @@
         sh, sl = parts2(jnp.where(s < t, scores, 0.0))
         both = mm(sh, v[:b]) + mm(sl, v[:b])
         pieces.append(jnp.where(left, both[:SUB], both[SUB:]))
-    wkv = jnp.concatenate(pieces, axis=0)
+    now = mm(jnp.concatenate(parts2(r * k * u_ref[...]), axis=1), same_head(1.0))
+    wkv_ref[...] = jnp.concatenate(pieces, axis=0) + now * v.astype(F32)
+    high_ref[...], low_ref[...] = parts2(r * jnp.exp(exclusive))
+
+
+def same_head(value):
     i = lax.broadcasted_iota(jnp.int32, (LANES, LANES), 0) // CHAN
     j = lax.broadcasted_iota(jnp.int32, (LANES, LANES), 1) // CHAN
-    same = (i == j).astype(F32)
-    ones = jnp.concatenate([same.astype(BF16)] * 2, axis=0)
-    mean_of = jnp.concatenate([(same / CHAN).astype(BF16)] * 2, axis=0)
-    now = mm(jnp.concatenate(parts2(r * k * u_ref[...]), axis=1), ones)
-    wkv = wkv + now * v.astype(F32)
+    return jnp.concatenate([jnp.where(i == j, value, 0.0).astype(BF16)] * 2, axis=0)
+
+
+def mix_kernel(wkv_ref, high_ref, low_ref, g_ref, scale_ref, state_ref, out_ref):
     state = state_ref[...]
     left = left_lanes(CHAN)
     state = jnp.concatenate([jnp.where(left, state, 0.0), jnp.where(left, 0.0, state)], axis=0)
-    rh, rl = parts2(r * jnp.exp(exclusive))
     sh, sl = parts2(state)
-    wkv = wkv + mm(
-        jnp.concatenate([rh, rl, rh], axis=1), jnp.concatenate([sh, sh, sl], axis=0)
-    )
+    high = high_ref[...]
+    wkv = wkv_ref[...] + mm(
+        jnp.concatenate([high, low_ref[...], high], axis=1), jnp.concatenate([sh, sh, sl], axis=0)
+    )
+    mean_of = same_head(1.0 / CHAN)
     mean = mm(jnp.concatenate(parts2(wkv), axis=1), mean_of)
     off = wkv - mean
     var = mm(jnp.concatenate(parts2(off * off), axis=1), mean_of)
@@ -129,6 +134,40 @@
     out_ref[...] = (y * (g / (1.0 + jnp.exp(-g)))).astype(out_ref.dtype)
 
 
+def score_kernel(share_bits, vocab_bits, place_ref, mine_ref, theirs_ref, label_ref, vocab_ref, out_ref, top_ref, sum_ref, pick_ref):
+    step = pl.program_id(0)
+    tile, half = vocab_ref.shape[0], mine_ref.shape[0]
+    core = place_ref[0]
+
+    @pl.when(step == 0)
+    def _():
+        top_ref[...] = jnp.full_like(top_ref, -3.0e38)
+        sum_ref[...] = jnp.zeros_like(sum_ref)
+        pick_ref[...] = jnp.zeros_like(pick_ref)
+
+    index = step * tile + lax.broadcasted_iota(jnp.int32, (tile, half), 0)
+    group = lax.shift_right_logical(index, share_bits)
+    entry = place_ref[1] + lax.shift_left(group, vocab_bits) + (index & ((1 << share_bits) - 1))
+    for part, tokens in enumerate((mine_ref, theirs_ref)):
+        at = slice(part * half, (part + 1) * half)
+        label = jnp.where(core == part, label_ref[:, :half], label_ref[:, half:])
+        logits = mm_t(vocab_ref[...], tokens[...])
+        old = top_ref[:, at]
+        top = jnp.maximum(old, jnp.max(logits, axis=0, keepdims=True))
+        fresh = jnp.sum(jnp.exp(logits - top), axis=0, keepdims=True)
+        sum_ref[:, at] = sum_ref[:, at] * jnp.exp(old - top) + fresh
+        pick_ref[:, at] += jnp.sum(jnp.where(entry == label, logits, 0.0), axis=0, keepdims=True)
+        top_ref[:, at] = top
+
+    @pl.when(step == pl.num_programs(0) - 1)
+    def _():
+        part = top_ref[...] + jnp.log(sum_ref[...])
+        for row, value in enumerate((part, pick_ref[...])):
+            first, second = value[:, :half], value[:, half:]
+            out_ref[row : row + 1, :half] = jnp.where(core == 0, first, second)
+            out_ref[row : row + 1, half:] = jnp.where(core == 0, second, first)
+
+
 def cost(flops, nbytes):
     return pl.CostEstimate(flops=flops, bytes_accessed=nbytes, transcendentals=0)
 
@@ -136,6 +175,27 @@
 def shifted(value, axis, steps):
     count = lax.axis_size(axis)
     return lax.ppermute(value, axis, [(i, (i + steps) % count) for i in range(count)])
+
+
+def copies(value, axes):
+    count = lax.axis_size(axes)
+    sent = jnp.broadcast_to(value[None], (count, *value.shape))
+    return lax.all_to_all(sent, axes, 0, 0, tiled=True)
+
+
+def spread(value, axis, groups):
+    count = len(groups[0])
+    place = sum(
+        jnp.where(lax.axis_index(axis) == source, i, 0)
+        for group in groups
+        for i, source in enumerate(group)
+    )
+    out = jnp.zeros((count, *value.shape), value.dtype)
+    for step in range(count):
+        pairs = [(g[i], g[(i + step) % count]) for g in groups for i in range(count)]
+        piece = lax.ppermute(value, axis, pairs) if step else value
+        out = lax.dynamic_update_index_in_dim(out, piece, (place - step) % count, 0)
+    return out
 
 
 def per_device(
@@ -166,9 +226,10 @@
     pairs = width // LANES
     own = rows // n_head
 
-    proj = lax.all_gather(closing_projection, "z", axis=1, tiled=True)
-    share = vocabulary_readout.shape[0] // n_head
+    vocab_local = vocabulary_readout.shape[0]
+    share = vocab_local // n_head
     vocab_share = lax.dynamic_slice_in_dim(vocabulary_readout, head * share, share)
+    vocab_rows = lax.all_gather(vocab_share, "z", axis=0, tiled=True)
 
     chunks = n_blk // pairs
     chunk_rows = CHAN // chunks
@@ -183,6 +244,39 @@
     )(lookup_vector_array, payload_vector_array, raw_forgetting_rate)
     moved = lax.all_to_all(end, ("x", "z"), 0, 0, tiled=True)
 
+    columns, facts, bonus, _ = lax.optimization_barrier(
+        (
+            closing_projection.T,
+            jnp.concatenate(
+                [
+                    following_labels.astype(F32),
+                    response_indicator.astype(F32),
+                    baseline_logarithmic_likelihood,
+                ]
+            ),
+            current_reward_vector[None, :],
+            end,
+        )
+    )
+    far = [[i + j * 4 for j in range(nz // 4)] for i in range(4)]
+    near = [[i * 4 + j for j in range(4)] for i in range(nz // 4)]
+    columns = spread(columns, "z", far)
+    plane = nx * ny * nc
+    facts = jnp.pad(facts, (0, LANES - 3 * own)).reshape(1, LANES)
+    facts = spread(facts, "c", [list(range(nc))])
+    row = pl.BlockSpec((1, LANES), lambda p: (0, p))
+    within, high, low = pl.pallas_call(
+        within_kernel,
+        grid=(pairs,),
+        in_specs=[col] * 4 + [row],
+        out_specs=[col] * 3,
+        out_shape=[jax.ShapeDtypeStruct((rows, width), t) for t in (F32, BF16, BF16)],
+        cost_estimate=cost(pairs * 60_000_000, 8 * rows * width * 2),
+    )(acceptance_vector, lookup_vector_array, payload_vector_array, raw_forgetting_rate, bonus)
+
+    moved, within, high, low, columns, facts = lax.optimization_barrier(
+        (moved, within, high, low, columns, facts)
+    )
     prev_seq = jnp.concatenate([jnp.full((1,), -1, jnp.int32), rollout_for_segment[:-1]])
     starts = (rollout_for_segment != prev_seq).astype(jnp.int32)
     meta = jnp.stack([starts, query_text_for_rollout[rollout_for_segment]])
@@ -201,35 +295,31 @@
         out_shape=jax.ShapeDtypeStruct((n_blk, chunk_rows, LANES), F32),
         cost_estimate=cost(1_000_000, 500_000),
     )(meta, moved, prompt)
+    columns, facts, _ = lax.optimization_barrier((columns, facts, entering))
     entering = lax.all_to_all(entering, ("x", "z"), 0, 0, tiled=True)
+    columns = spread(columns, "z", near).transpose(1, 0, 2, 3).reshape(-1, width)
+    facts = spread(facts, "y", [list(range(ny))])
+    entering, facts = lax.optimization_barrier((entering, facts))
     entering = entering.reshape(pairs * CHAN, LANES)
 
-    row = pl.BlockSpec((1, LANES), lambda p: (0, p))
     mixed = pl.pallas_call(
         mix_kernel,
         grid=(pairs,),
-        in_specs=[col] * 5 + [row] * 2 + [pl.BlockSpec((CHAN, LANES), lambda p: (p, 0))],
+        in_specs=[col] * 4 + [row, pl.BlockSpec((CHAN, LANES), lambda p: (p, 0))],
         out_specs=col,
         out_shape=jax.ShapeDtypeStruct((rows, width), BF16),
-        cost_estimate=cost(pairs * 60_000_000, 6 * rows * width * 2),
-    )(
-        acceptance_vector,
-        lookup_vector_array,
-        payload_vector_array,
-        raw_forgetting_rate,
-        raw_gating_signal,
-        current_reward_vector[None, :],
-        group_layernorm_scaling[None, :],
-        entering,
-    )
+        cost_estimate=cost(pairs * 20_000_000, 6 * rows * width * 2),
+    )(within, high, low, raw_gating_signal, group_layernorm_scaling[None, :], entering)
 
     mixed = lax.all_gather(mixed, "x", axis=0)
     mixed = mixed.reshape(nx, ny, nc, own, width).transpose(2, 1, 0, 3, 4)
     mixed = mixed.reshape(nc, ny * nx * own, width)
-    theirs = mm(lax.dynamic_index_in_dim(mixed, 1 - ic, 0, False), proj)
-    mine = mm(lax.dynamic_index_in_dim(mixed, ic, 0, False), proj)
+    theirs = mm_t(lax.dynamic_index_in_dim(mixed, 1 - ic, 0, False), columns)
+    mine = mm_t(lax.dynamic_index_in_dim(mixed, ic, 0, False), columns)
     partial = mine + shifted(theirs, "c", 1)
     partial = partial.reshape(ny * nx, own, embed // nx)
+    partial, facts = lax.optimization_barrier((partial, facts))
+    facts = spread(facts, "x", [list(range(nx))])
     partial = lax.all_to_all(partial, ("y", "x"), 0, 0, tiled=True)
     projected = jnp.sum(partial.reshape(ny, nx, own, embed // nx), axis=0)
     projected = projected.transpose(1, 0, 2).reshape(own, embed)
@@ -238,54 +328,41 @@
     hvar = jnp.mean((hidden - hmean) ** 2, axis=-1, keepdims=True)
     normed = ((hidden - hmean) / jnp.sqrt(hvar + 1e-05) * closing_layernorm_scaling).astype(BF16)
 
-    tokens = lax.all_gather(normed, "y", axis=0, tiled=True)
-    tokens = jnp.concatenate([tokens] + [shifted(tokens, "x", s) for s in range(1, nx)], axis=0)
+    normed, facts = lax.optimization_barrier((normed, facts))
+    facts = facts[..., 0, : 3 * own].reshape(nx, ny, nc, 3, own).transpose(3, 2, 1, 0, 4)
+
+    tokens = copies(normed, ("y", "x")).reshape(ny * nx * own, embed)
     other = shifted(tokens, "c", 1)
-    vocab_rows = lax.all_gather(vocab_share, "z", axis=0, tiled=True)
-
-    facts = jnp.stack(
-        [
-            following_labels.astype(F32),
-            response_indicator.astype(F32),
-            baseline_logarithmic_likelihood,
-        ]
-    )
-    facts, _ = lax.optimization_barrier((facts, other))
-    facts = lax.all_gather(facts, ("x", "y", "c"), axis=0)
-    facts = facts.reshape(nx, ny, nc, 3, own).transpose(3, 2, 0, 1, 4)
-    labels = facts[0].astype(jnp.int32)
-    back = (ix - jnp.arange(nx)) % nx
-
-    index = jnp.arange(nz * share, dtype=jnp.int32)
-    vocab_local = vocabulary_readout.shape[0]
-    entry = (ix * nz + index // share) * vocab_local + head * share + index % share
-
-    def score(toks, core):
-        logits = mm_t(toks, vocab_rows)
-        top = jnp.max(logits, axis=1)
-        total = jnp.sum(jnp.exp(logits - top[:, None]), axis=1)
-        wanted = lax.dynamic_index_in_dim(labels, core, 0, False)[back].reshape(-1)
-        picked = jnp.sum(jnp.where(entry[None, :] == wanted[:, None], logits, 0.0), axis=1)
-        both = jnp.stack([top + jnp.log(total), picked])
-        return both.reshape(2, nx, ny * own)[:, back]
-
-    first, second = score(tokens, ic), score(other, 1 - ic)
-    both = jnp.where(
-        ic == 0, jnp.stack([first, second], axis=1), jnp.stack([second, first], axis=1)
-    )
-    plane = nx * ny * nc
     count = plane * own
-    both = jnp.broadcast_to(both.reshape(1, 2 * count // LANES, LANES), (plane, 2 * count // LANES, LANES))
-    both = lax.all_to_all(both, ("x", "y", "c"), 0, 0, tiled=True).reshape(plane, 2, count)
+    labels = facts[0].reshape(1, count).astype(jnp.int32)
+    tile = min(256, nz * share)
+    place = jnp.stack([ic, ix * nz * vocab_local + head * share]).astype(jnp.int32)
+    whole = lambda *shape: pl.BlockSpec(shape, lambda i: (0,) * len(shape))
+    both = pl.pallas_call(
+        functools.partial(score_kernel, share.bit_length() - 1, vocab_local.bit_length() - 1),
+        grid=(nz * share // tile,),
+        in_specs=[
+            pl.BlockSpec(memory_space=pltpu.SMEM),
+            whole(count // nc, embed),
+            whole(count // nc, embed),
+            whole(1, count),
+            pl.BlockSpec((tile, embed), lambda i: (i, 0)),
+        ],
+        out_specs=whole(2, count),
+        out_shape=jax.ShapeDtypeStruct((2, count), F32),
+        scratch_shapes=[pltpu.VMEM((1, count), F32)] * 3,
+        compiler_params=pltpu.CompilerParams(vmem_limit_bytes=40 * 1024 * 1024),
+        cost_estimate=cost(2 * count * nz * share * embed, (count + nz * share) * embed * 2),
+    )(place, tokens, other, labels, vocab_rows)
+    both = copies(both, ("x", "y", "c"))
     part, picked = both[:, 0], both[:, 1]
     peak = jnp.max(part, axis=0)
     logp = jnp.sum(picked, axis=0) - peak - jnp.log(jnp.sum(jnp.exp(part - peak), axis=0))
-    ratio = facts[1] * (logp.reshape(nc, nx, ny, own) - facts[2])
-    token_ratio = lax.dynamic_slice(ratio, (ic, ix, iy, 0), (1, 1, 1, own)).reshape(own)
-
-    sums = jnp.sum(ratio, axis=(0, 2, 3))
-    sums = jnp.broadcast_to(jnp.pad(sums, (0, LANES - nx)), (nz, 1, LANES))
-    sums = lax.all_to_all(sums, "z", 0, 0, tiled=True)[:, 0, :nx]
+    ratio = facts[1] * (logp.reshape(nc, ny, nx, own) - facts[2])
+    token_ratio = lax.dynamic_slice(ratio, (ic, iy, ix, 0), (1, 1, 1, own)).reshape(own)
+
+    sums = jnp.sum(ratio, axis=(0, 1, 3))
+    sums = copies(jnp.pad(sums, (0, LANES - nx)).reshape(1, LANES), "z")[:, 0, :nx]
     seq_of = rollout_for_segment.reshape(nx, nz).T
     marker = jnp.arange(query_text_for_rollout.shape[0])[:, None, None] == seq_of[None]
     seq_ratio = jnp.sum(jnp.where(marker, sums[None], 0.0), axis=(1, 2)) / TOK_BLK

time: 256 us -> 274 us (1.070)
  starting transfers between devices: 54.8 us -> 112 us
  blocking collectives: 67.1 us -> 43.1 us
  waiting for transfers between devices: 80.6 us -> 60.3 us
  Pallas kernels: 12.2 us -> 21.6 us
  matrix products: 12.5 us -> 3.16 us
    ppermute x0 -> x13, starting transfers between devices: none -> 52.8 us  [spread(): piece = lax.ppermute(value, axis, pairs) if step else value]
    all_gather x2 -> x0, blocking collectives: 35.2 us -> none  [the longest x1 24.1 us: per_device(): facts = lax.all_gather(facts, ('x', 'y', 'c'), axis=0)]
    ppermute x0 -> x13, waiting for transfers between devices: none -> 33.9 us  [spread(): piece = lax.ppermute(value, axis, pairs) if step else value]
    ppermute x5 -> x2, waiting for transfers between devices: 26.4 us -> 5.96 us  [shifted(): lax.ppermute(value, axis, [(i, (i + steps) % count) for i in range(count)])]
    all_to_all x1, waiting for transfers between devices: 19.7 us -> 0.01 us  [per_device(): moved = lax.all_to_all(end, ('x', 'z'), 0, 0, tiled=True)]
    all_to_all x1, waiting for transfers between devices: 15.4 us -> 0.01 us  [per_device(): entering = lax.all_to_all(entering, ('x', 'z'), 0, 0, tiled=True)]
    all_to_all x2 -> x3, starting transfers between devices: 8.18 us -> 19 us  [the longest x2 13.7 us: copies(): return lax.all_to_all(sent, axes, 0, 0, tiled=True)]
    all_to_all x1, blocking collectives: 21.9 us -> 31.7 us  [copies(): return lax.all_to_all(sent, axes, 0, 0, tiled=True)]
  transfers between devices with their start and end apart: 11 -> 21, of which waited for: 9 -> 8; matrix products, arithmetic and copies ran while one was open for 4% -> 4% of each run, Pallas kernels for 5% -> 5%
where the time goes in v2:
time: 274 us; the launch traced here: 273 us
  starting transfers between devices  112 us (41%)
  waiting for transfers between devices  60.3 us (22%)
  blocking collectives  43.1 us (16%)
  Pallas kernels  21.6 us (8%)
  between operations  14.8 us (5%)
  local copies, waits for them, and re-layouts  12.5 us (5%)
  other arithmetic  4.95 us (2%)
  matrix products  3.16 us (1%)
    ppermute x13, starting transfers between devices, spread(): piece = lax.ppermute(value, axis, pairs) if step else value  52.8 us
    ppermute x13, waiting for transfers between devices, spread(): piece = lax.ppermute(value, axis, pairs) if step else value  33.9 us
    all_to_all x1, blocking collectives, copies(): return lax.all_to_all(sent, axes, 0, 0, tiled=True)  31.7 us
    all_to_all x1, starting transfers between devices, per_device(): moved = lax.all_to_all(end, ('x', 'z'), 0, 0, tiled=True)  19.1 us
    all_to_all x2, waiting for transfers between devices, copies(): return lax.all_to_all(sent, axes, 0, 0, tiled=True)  18.4 us
    all_to_all x2, starting transfers between devices, copies(): return lax.all_to_all(sent, axes, 0, 0, tiled=True)  13.7 us
    ppermute x2, starting transfers between devices, shifted(): lax.ppermute(value, axis, [(i, (i + steps) % count) for i in range(count)])  11.7 us
    all_gather x1, blocking collectives, per_device(): mixed = lax.all_gather(mixed, 'x', axis=0)  11.3 us
  transfers between devices with their start and end apart: 21, of which 8 were waited for; matrix products, arithmetic and copies ran while one was open for 4% of the time, Pallas kernels for 5%

profile of v2, /device:TPU:1, one launch (start us, length us, event | category | flops | bytes accessed | tf_op | source)
XLA Modules:
  0.0 272.7 jit_solution(12108351708457645871)
XLA Ops:
  7.3 1.9 constant_dynamic-slice_fusion.1
  9.2 3.7 %shard_map.176 = f32[64,8,128]{2,1,0:T(8,128)} custom-call(bf16[128,512]{1,0:T(8,128)(2,1)} %k_ref.3, bf16[128,512]{1,0:T(8,128)(2,1)} %v_ref.3, bf16[128,512]{1,0:T(8,128)(2,1)} %w_ref.3), custom_call_target="tpu_custom_call" | custom-call | flops 80000000 | bytes 393216 | tf_op jit(solution)/shard_map/pallas_call | solution.py:237
  12.9 19.1 %all-to-all-start = ((f32[64,8,128]{2,1,0:T(8,128)}), f32[64,8,128]{2,1,0:T(8,128)S(1)}, u32[]{:S(2)}, u32[]{:S(2)}) async-start(f32[64,8,128]{2,1,0:T(8,128)} %shard_map.176), calls=%async_computation | async-start | bytes 524288 | tf_op jit(solution)/shard_map/all_to_all | solution.py:245
  32.0 0.7 convert_element_type.32
  32.6 0.7 convert_element_type.33
  33.3 0.7 pad_maximum_fusion
  34.0 6.8 %collective-permute-start.2 = (bf16[64,512]{1,0:T(8,128)(2,1)}, bf16[64,512]{1,0:T(8,128)(2,1)S(1)}, u32[]{:S(2)}, u32[]{:S(2)}) collective-permute-start(bf16[64,512]{1,0:T(8,128)(2,1)} %bitcast.142), channel_id=1, source_target_pairs={{0,96},{32,0},{64,32},{96,64},{8,104},{40,8},{72,40},{104,72},{16,... | collective-permute-start | bytes 196616 | tf_op jit(solution)/shard_map/ppermute | solution.py:196
  40.9 7.0 %collective-permute-start.1 = (bf16[64,512]{1,0:T(8,128)(2,1)}, bf16[64,512]{1,0:T(8,128)(2,1)S(1)}, u32[]{:S(2)}, u32[]{:S(2)}) collective-permute-start(bf16[64,512]{1,0:T(8,128)(2,1)} %bitcast.143), channel_id=1, source_target_pairs={{0,64},{32,96},{64,0},{96,32},{8,72},{40,104},{72,8},{104,40},{16,... | collective-permute-start | bytes 196616 | tf_op jit(solution)/shard_map/ppermute | solution.py:196
  47.9 7.0 %collective-permute-start = (bf16[64,512]{1,0:T(8,128)(2,1)}, bf16[64,512]{1,0:T(8,128)(2,1)S(1)}, u32[]{:S(2)}, u32[]{:S(2)}) collective-permute-start(bf16[64,512]{1,0:T(8,128)(2,1)} %bitcast.144), channel_id=1, source_target_pairs={{0,32},{32,64},{64,96},{96,0},{8,40},{40,72},{72,104},{104,8},{16,... | collective-permute-start | bytes 196616 | tf_op jit(solution)/shard_map/ppermute | solution.py:196
  54.9 4.0 %collective-permute-start.3 = (f32[1,128]{1,0:T(1,128)S(1)}, f32[1,128]{1,0:T(1,128)S(1)}, u32[]{:S(2)}, u32[]{:S(2)}) collective-permute-start(f32[1,128]{1,0:T(1,128)S(1)} %get-tuple-element.47), channel_id=1, source_target_pairs={{0,1},{1,0},{2,3},{3,2},{4,5},{5,4},{6,7},{7,6},{8,9},{9,8},{10,11... | collective-permute-start | bytes 1544 | tf_op jit(solution)/shard_map/ppermute | solution.py:196
  59.0 1.1 reshape.88
  60.4 0.7 compare_select_fusion
  61.1 0.8 gather_fusion
  62.5 0.7 reshape.100.prompt_ref
  63.2 4.8 %shard_map.177 = (f32[128,512]{1,0:T(8,128)}, bf16[128,512]{1,0:T(8,128)(2,1)}, bf16[128,512]{1,0:T(8,128)(2,1)}) custom-call(bf16[128,512]{1,0:T(8,128)(2,1)} %r_ref.1, bf16[128,512]{1,0:T(8,128)(2,1)} %k_ref.3, bf16[128,512]{1,0:T(8,128)(2,1)} %v_ref.3, bf16[128,512]{1,0:T(8,128)(2,1)} %w_ref.3, f32[1,512]{1,0:T(1,128)} %bitcast.153), custom_call_target="tpu_custom_call" | custom-call | flops 240000000 | bytes 1048576 | tf_op jit(solution)/shard_map/pallas_call | solution.py:268
  68.2 0.7 copy-done.3
  68.9 1.9 shard_map.178
  70.8 9.7 %all-to-all-start.1 = ((f32[64,4,128]{2,1,0:T(4,128)}), f32[64,4,128]{2,1,0:T(4,128)S(1)}, u32[]{:S(2)}, u32[]{:S(2)}) async-start(f32[64,4,128]{2,1,0:T(4,128)} %shard_map.178), calls=%async_computation.1 | async-start | bytes 262144 | tf_op jit(solution)/shard_map/all_to_all | solution.py:299
  80.5 4.7 %collective-permute-start.6 = (f32[2,1,128]{2,0,1:T(2,128)S(1)}, f32[2,1,128]{2,0,1:T(2,128)S(1)}, u32[]{:S(2)}, u32[]{:S(2)}) collective-permute-start(f32[2,1,128]{2,0,1:T(2,128)S(1)} %dynamic_update_slice.64), channel_id=1, source_target_pairs={{0,6},{2,0},{4,2},{6,4},{1,7},{3,1},{5,3},{7,5},{8,14},{10,8},{12,... | collective-permute-start | bytes 3080 | tf_op jit(solution)/shard_map/ppermute | solution.py:196
  85.1 2.2 collective-permute-start.5
  87.4 2.6 collective-permute-start.4
  90.0 4.7 %collective-permute-start.9 = (bf16[4,64,512]{2,1,0:T(8,128)(2,1)S(1)}, bf16[4,64,512]{2,1,0:T(8,128)(2,1)S(1)}, u32[]{:S(2)}, u32[]{:S(2)}) collective-permute-start(bf16[4,64,512]{2,1,0:T(8,128)(2,1)S(1)} %bitcast_dynamic-update-slice_fusion.4), channel_id=1, source_target_pairs={{0,24},{8,0},{16,8},{24,16},{32,56},{40,32},{48,40},{56,48},{64,88... | collective-permute-start | bytes 786440 | tf_op jit(solution)/shard_map/ppermute | solution.py:196
  94.8 1.9 collective-permute-start.8
  96.9 2.5 collective-permute-start.7
  99.4 29.1 %collective-permute-done.7 = bf16[4,64,512]{2,1,0:T(8,128)(2,1)S(1)} collective-permute-done((bf16[4,64,512]{2,1,0:T(8,128)(2,1)S(1)}, bf16[4,64,512]{2,1,0:T(8,128)(2,1)S(1)}, u32[]{:S(2)}, u32[]{:S(2)}) %collective-permute-start.7) | collective-permute-done | bytes 262176 | tf_op jit(solution)/shard_map/ppermute | solution.py:196
  128.6 0.6 copy-done.4
  129.3 3.9 %shard_map.179 = bf16[128,512]{1,0:T(8,128)(2,1)} custom-call(f32[128,512]{1,0:T(8,128)} %get-tuple-element.28.wkv_ref, bf16[128,512]{1,0:T(8,128)(2,1)} %get-tuple-element.29.high_ref, bf16[128,512]{1,0:T(8,128)(2,1)} %get-tuple-element.30.low_ref, bf16[128,512]{1,0:T(8,128)(2,1)} %g_ref.1, f32[1,512]{1,0:T(1,128)} %bitcast.150, f32[256,128]{1,0:T(8,128)} %bitcast.138), custom_call_target="tpu_custom_call" | custom-call | flops 80000000 | bytes 786432 | tf_op jit(solution)/shard_map/pallas_call | solution.py:305
  133.2 11.3 %all-gather = bf16[512,512]{1,0:T(8,128)(2,1)S(1)} all-gather(bf16[128,512]{1,0:T(8,128)(2,1)} %shard_map.179), channel_id=2, replica_groups=mesh['x'=4,'z'=16,'y'=4,'c'=2] {'x'}, dimensions={0}, use_global_device_ids=true | all-gather | bytes 655360 | tf_op jit(solution)/shard_map/all_gather | solution.py:314
  145.1 7.9 %collective-permute-start.10 = (f32[256,1024]{1,0:T(8,128)S(1)}, f32[256,1024]{1,0:T(8,128)}, u32[]{:S(2)}, u32[]{:S(2)}) collective-permute-start(f32[256,1024]{1,0:T(8,128)S(1)} %fusion), channel_id=1, source_target_pairs={{0,1},{1,0},{2,3},{3,2},{4,5},{5,4},{6,7},{7,6},{8,9},{9,8},{10,11... | collective-permute-start | bytes 3145736 | tf_op jit(solution)/shard_map/ppermute | solution.py:177
  153.0 2.4 collective-permute-done.10
  155.4 2.7 convolution_add_fusion
  158.0 5.2 %all-to-all-start.2 = ((f32[16,16,1024]{2,1,0:T(8,128)}), f32[16,16,1024]{2,1,0:T(8,128)S(1)}, u32[]{:S(2)}, u32[]{:S(2)}) async-start(f32[16,16,1024]{2,1,0:T(8,128)} %bitcast.40), calls=%async_computation.2 | async-start | bytes 2097152 | tf_op jit(solution)/shard_map/all_to_all | solution.py:323
  163.4 4.4 %collective-permute-start.13 = (f32[4,2,1,128]{3,1,0,2:T(2,128)S(1)}, f32[4,2,1,128]{3,1,0,2:T(2,128)S(1)}, u32[]{:S(2)}, u32[]{:S(2)}) collective-permute-start(f32[4,2,1,128]{3,1,0,2:T(2,128)S(1)} %constant_dynamic-update-slice_fusion.4), channel_id=1, source_target_pairs={{0,384},{128,0},{256,128},{384,256},{1,385},{129,1},{257,129},{385... | collective-permute-start | bytes 12296 | tf_op jit(solution)/shard_map/ppermute | solution.py:196
  167.7 2.5 collective-permute-start.12
  170.2 2.5 collective-permute-start.11
  172.8 4.5 %collective-permute-done.11 = f32[4,2,1,128]{3,1,0,2:T(2,128)S(1)} collective-permute-done((f32[4,2,1,128]{3,1,0,2:T(2,128)S(1)}, f32[4,2,1,128]{3,1,0,2:T(2,128)S(1)}, u32[]{:S(2)}, u32[]{:S(2)}) %collective-permute-start.11) | collective-permute-done | bytes 4128 | tf_op jit(solution)/shard_map/ppermute | solution.py:196
  177.6 2.0 all-to-all-done.2
  180.4 31.7 %all_to_all.30 = bf16[16,16,4096]{2,1,0:T(8,128)(2,1)S(1)} all-to-all(bf16[16,16,4096]{2,1,0:T(8,128)(2,1)S(1)} %broadcast_in_dim.146), channel_id=1, replica_groups=mesh['x'=4,'z'=16,'y'=4,'c'=2] {'y','x'}, dimensions={0} | all-to-all | bytes 4194304 | tf_op jit(solution)/shard_map/all_to_all | solution.py:183
  212.2 3.9 %collective-permute-start.14 = (bf16[256,4096]{1,0:T(8,128)(2,1)S(1)}, bf16[256,4096]{1,0:T(8,128)(2,1)}, u32[]{:S(2)}, u32[]{:S(2)}) collective-permute-start(bf16[256,4096]{1,0:T(8,128)(2,1)S(1)} %bitcast.126), channel_id=1, source_target_pairs={{0,1},{1,0},{2,3},{3,2},{4,5},{5,4},{6,7},{7,6},{8,9},{9,8},{10,11... | collective-permute-start | bytes 6291464 | tf_op jit(solution)/shard_map/ppermute | solution.py:177
  216.4 3.6 %collective-permute-done.14.theirs_ref = bf16[256,4096]{1,0:T(8,128)(2,1)} collective-permute-done((bf16[256,4096]{1,0:T(8,128)(2,1)S(1)}, bf16[256,4096]{1,0:T(8,128)(2,1)}, u32[]{:S(2)}, u32[]{:S(2)}) %collective-permute-start.14) | collective-permute-done | bytes 2097184 | tf_op jit(solution)/shard_map/ppermute | solution.py:177
  219.9 3.4 %copy-done.1 = bf16[1024,4096]{1,0:T(8,128)(2,1)S(1)} copy-done((bf16[1024,4096]{1,0:T(8,128)(2,1)S(1)}, bf16[1024,4096]{1,0:T(8,128)(2,1)}, u32[]{:S(2)}) %copy-start.1) | copy-done | bytes 8388632
  223.3 7.3 %shard_map.180 = f32[2,512]{1,0:T(2,128)S(1)} custom-call(s32[2]{0:T(128)S(1)} %pad_add_fusion.1.place_ref, bf16[256,4096]{1,0:T(8,128)(2,1)S(1)} %bitcast.127, bf16[256,4096]{1,0:T(8,128)(2,1)} %collective-permute-done.14.theirs_ref, s32[1,512]{1,0:T(1,128)S(1)} %convert_element_type.40.label_ref, bf16[1024,4096]{1,0:T(8,128)(2,1)S(1)} %copy-done.1), custom_call_target="tpu_custom_call" | custom-call | flops 4294967296 | bytes 12582912 | tf_op jit(solution)/shard_map/pallas_call | solution.py:341
  230.6 0.7 broadcast_in_dim.147
  231.3 3.9 %all-to-all-start.4 = ((f32[32,2,512]{2,1,0:T(2,128)}), f32[32,2,512]{2,1,0:T(2,128)S(1)}, u32[]{:S(2)}, u32[]{:S(2)}) async-start(f32[32,2,512]{2,1,0:T(2,128)} %broadcast_in_dim.147), calls=%async_computation.4 | async-start | bytes 262144 | tf_op jit(solution)/shard_map/all_to_all | solution.py:183
  235.2 7.7 %all-to-all-done.4 = f32[32,2,512]{2,1,0:T(2,128)S(1)} async-done(((f32[32,2,512]{2,1,0:T(2,128)}), f32[32,2,512]{2,1,0:T(2,128)S(1)}, u32[]{:S(2)}, u32[]{:S(2)}) %all-to-all-start.4) | async-done | bytes 131104 | tf_op jit(solution)/shard_map/all_to_all | solution.py:183
  243.4 0.6 broadcast_in_dim.148
  244.0 9.9 %all-to-all-start.5 = ((f32[16,1,128]{2,1,0:T(1,128)}), f32[16,1,128]{2,1,0:T(1,128)S(1)}, u32[]{:S(2)}, u32[]{:S(2)}) async-start(f32[16,1,128]{2,1,0:T(1,128)} %broadcast_in_dim.148), calls=%async_computation.5 | async-start | bytes 16384 | tf_op jit(solution)/shard_map/all_to_all | solution.py:183
  254.4 10.7 %all-to-all-done.5 = f32[16,1,128]{2,1,0:T(1,128)S(1)} async-done(((f32[16,1,128]{2,1,0:T(1,128)}), f32[16,1,128]{2,1,0:T(1,128)S(1)}, u32[]{:S(2)}, u32[]{:S(2)}) %all-to-all-start.5) | async-done | bytes 8224 | tf_op jit(solution)/shard_map/all_to_all | solution.py:183
  (85 shorter events, 5.1 us)
Async XLA Ops:
  7.2 53.9 %copy-start = (s32[16]{0:T(128)S(1)}, s32[16]{0:T(128)}, u32[]{:S(2)}) copy-start(s32[16]{0:T(128)} %param.33) | copy-start | bytes 196
  7.2 54.7 %copy-start.5 = (bf16[512,64]{0,1:T(8,128)(2,1)S(1)}, bf16[512,64]{0,1:T(8,128)(2,1)}, u32[]{:S(2)}) copy-start(bf16[512,64]{0,1:T(8,128)(2,1)} %param.27) | copy-start | bytes 196612
  7.2 54.7 %copy-start.7 = (s32[64]{0:T(128)S(1)}, s32[64]{0:T(128)}, u32[]{:S(2)}) copy-start(s32[64]{0:T(128)} %param.32) | copy-start | bytes 772
  7.2 212.7 %all-gather.3.cloned.1.call-start = ((), (), s32[]{:S(2)}) async-start(), calls=%async_computation.6 | async-start | bytes 8912896 | tf_op jit(solution)/shard_map/all_gather | solution.py:232
  12.9 55.3 %all-to-all-start = ((f32[64,8,128]{2,1,0:T(8,128)}), f32[64,8,128]{2,1,0:T(8,128)S(1)}, u32[]{:S(2)}, u32[]{:S(2)}) async-start(f32[64,8,128]{2,1,0:T(8,128)} %shard_map.176), calls=%async_computation | async-start | bytes 524288 | tf_op jit(solution)/shard_map/all_to_all | solution.py:245
  34.0 34.1 %collective-permute-start.2 = (bf16[64,512]{1,0:T(8,128)(2,1)}, bf16[64,512]{1,0:T(8,128)(2,1)S(1)}, u32[]{:S(2)}, u32[]{:S(2)}) collective-permute-start(bf16[64,512]{1,0:T(8,128)(2,1)} %bitcast.142), channel_id=1, source_target_pairs={{0,96},{32,0},{64,32},{96,64},{8,104},{40,8},{72,40},{104,72},{16,... | collective-permute-start | bytes 196616 | tf_op jit(solution)/shard_map/ppermute | solution.py:196
  40.9 27.2 %collective-permute-start.1 = (bf16[64,512]{1,0:T(8,128)(2,1)}, bf16[64,512]{1,0:T(8,128)(2,1)S(1)}, u32[]{:S(2)}, u32[]{:S(2)}) collective-permute-start(bf16[64,512]{1,0:T(8,128)(2,1)} %bitcast.143), channel_id=1, source_target_pairs={{0,64},{32,96},{64,0},{96,32},{8,72},{40,104},{72,8},{104,40},{16,... | collective-permute-start | bytes 196616 | tf_op jit(solution)/shard_map/ppermute | solution.py:196
  47.9 20.2 %collective-permute-start = (bf16[64,512]{1,0:T(8,128)(2,1)}, bf16[64,512]{1,0:T(8,128)(2,1)S(1)}, u32[]{:S(2)}, u32[]{:S(2)}) collective-permute-start(bf16[64,512]{1,0:T(8,128)(2,1)} %bitcast.144), channel_id=1, source_target_pairs={{0,32},{32,64},{64,96},{96,0},{8,40},{40,72},{72,104},{104,8},{16,... | collective-permute-start | bytes 196616 | tf_op jit(solution)/shard_map/ppermute | solution.py:196
  54.9 13.1 %collective-permute-start.3 = (f32[1,128]{1,0:T(1,128)S(1)}, f32[1,128]{1,0:T(1,128)S(1)}, u32[]{:S(2)}, u32[]{:S(2)}) collective-permute-start(f32[1,128]{1,0:T(1,128)S(1)} %get-tuple-element.47), channel_id=1, source_target_pairs={{0,1},{1,0},{2,3},{3,2},{4,5},{5,4},{6,7},{7,6},{8,9},{9,8},{10,11... | collective-permute-start | bytes 1544 | tf_op jit(solution)/shard_map/ppermute | solution.py:196
  68.2 0.7 copy-start.3
  70.8 57.8 %all-to-all-start.1 = ((f32[64,4,128]{2,1,0:T(4,128)}), f32[64,4,128]{2,1,0:T(4,128)S(1)}, u32[]{:S(2)}, u32[]{:S(2)}) async-start(f32[64,4,128]{2,1,0:T(4,128)} %shard_map.178), calls=%async_computation.1 | async-start | bytes 262144 | tf_op jit(solution)/shard_map/all_to_all | solution.py:299
  80.5 18.9 %collective-permute-start.6 = (f32[2,1,128]{2,0,1:T(2,128)S(1)}, f32[2,1,128]{2,0,1:T(2,128)S(1)}, u32[]{:S(2)}, u32[]{:S(2)}) collective-permute-start(f32[2,1,128]{2,0,1:T(2,128)S(1)} %dynamic_update_slice.64), channel_id=1, source_target_pairs={{0,6},{2,0},{4,2},{6,4},{1,7},{3,1},{5,3},{7,5},{8,14},{10,8},{12,... | collective-permute-start | bytes 3080 | tf_op jit(solution)/shard_map/ppermute | solution.py:196
  85.1 14.2 %collective-permute-start.5 = (f32[2,1,128]{2,0,1:T(2,128)S(1)}, f32[2,1,128]{2,0,1:T(2,128)S(1)}, u32[]{:S(2)}, u32[]{:S(2)}) collective-permute-start(f32[2,1,128]{2,0,1:T(2,128)S(1)} %dynamic_update_slice.64), channel_id=1, source_target_pairs={{0,4},{2,6},{4,0},{6,2},{1,5},{3,7},{5,1},{7,3},{8,12},{10,14},{12... | collective-permute-start | bytes 3080 | tf_op jit(solution)/shard_map/ppermute | solution.py:196
  87.4 9.5 %collective-permute-start.4 = (f32[2,1,128]{2,0,1:T(2,128)S(1)}, f32[2,1,128]{2,0,1:T(2,128)S(1)}, u32[]{:S(2)}, u32[]{:S(2)}) collective-permute-start(f32[2,1,128]{2,0,1:T(2,128)S(1)} %dynamic_update_slice.64), channel_id=1, source_target_pairs={{0,2},{2,4},{4,6},{6,0},{1,3},{3,5},{5,7},{7,1},{8,10},{10,12},{12... | collective-permute-start | bytes 3080 | tf_op jit(solution)/shard_map/ppermute | solution.py:196
  90.0 38.6 %collective-permute-start.9 = (bf16[4,64,512]{2,1,0:T(8,128)(2,1)S(1)}, bf16[4,64,512]{2,1,0:T(8,128)(2,1)S(1)}, u32[]{:S(2)}, u32[]{:S(2)}) collective-permute-start(bf16[4,64,512]{2,1,0:T(8,128)(2,1)S(1)} %bitcast_dynamic-update-slice_fusion.4), channel_id=1, source_target_pairs={{0,24},{8,0},{16,8},{24,16},{32,56},{40,32},{48,40},{56,48},{64,88... | collective-permute-start | bytes 786440 | tf_op jit(solution)/shard_map/ppermute | solution.py:196
  94.8 33.8 %collective-permute-start.8 = (bf16[4,64,512]{2,1,0:T(8,128)(2,1)S(1)}, bf16[4,64,512]{2,1,0:T(8,128)(2,1)S(1)}, u32[]{:S(2)}, u32[]{:S(2)}) collective-permute-start(bf16[4,64,512]{2,1,0:T(8,128)(2,1)S(1)} %bitcast_dynamic-update-slice_fusion.4), channel_id=1, source_target_pairs={{0,16},{8,24},{16,0},{24,8},{32,48},{40,56},{48,32},{56,40},{64,80... | collective-permute-start | bytes 786440 | tf_op jit(solution)/shard_map/ppermute | solution.py:196
  96.9 31.7 %collective-permute-start.7 = (bf16[4,64,512]{2,1,0:T(8,128)(2,1)S(1)}, bf16[4,64,512]{2,1,0:T(8,128)(2,1)S(1)}, u32[]{:S(2)}, u32[]{:S(2)}) collective-permute-start(bf16[4,64,512]{2,1,0:T(8,128)(2,1)S(1)} %bitcast_dynamic-update-slice_fusion.4), channel_id=1, source_target_pairs={{0,8},{8,16},{16,24},{24,0},{32,40},{40,48},{48,56},{56,32},{64,72... | collective-permute-start | bytes 786440 | tf_op jit(solution)/shard_map/ppermute | solution.py:196
  128.6 0.7 copy-start.4
  145.1 34.6 %copy-start.2 = (bf16[16,4096]{1,0:T(8,128)(2,1)S(1)}, bf16[16,4096]{1,0:T(8,128)(2,1)}, u32[]{:S(2)}) copy-start(bf16[16,4096]{1,0:T(8,128)(2,1)} %param.26) | copy-start | bytes 393220
  145.1 35.0 %copy-start.6 = (f32[4096]{0:T(1024)S(1)}, f32[4096]{0:T(1024)}, u32[]{:S(2)}) copy-start(f32[4096]{0:T(1024)} %param.25) | copy-start | bytes 49156
  145.1 10.3 %collective-permute-start.10 = (f32[256,1024]{1,0:T(8,128)S(1)}, f32[256,1024]{1,0:T(8,128)}, u32[]{:S(2)}, u32[]{:S(2)}) collective-permute-start(f32[256,1024]{1,0:T(8,128)S(1)} %fusion), channel_id=1, source_target_pairs={{0,1},{1,0},{2,3},{3,2},{4,5},{5,4},{6,7},{7,6},{8,9},{9,8},{10,11... | collective-permute-start | bytes 3145736 | tf_op jit(solution)/shard_map/ppermute | solution.py:177
  158.0 21.5 %all-to-all-start.2 = ((f32[16,16,1024]{2,1,0:T(8,128)}), f32[16,16,1024]{2,1,0:T(8,128)S(1)}, u32[]{:S(2)}, u32[]{:S(2)}) async-start(f32[16,16,1024]{2,1,0:T(8,128)} %bitcast.40), calls=%async_computation.2 | async-start | bytes 2097152 | tf_op jit(solution)/shard_map/all_to_all | solution.py:323
  163.4 14.2 %collective-permute-start.13 = (f32[4,2,1,128]{3,1,0,2:T(2,128)S(1)}, f32[4,2,1,128]{3,1,0,2:T(2,128)S(1)}, u32[]{:S(2)}, u32[]{:S(2)}) collective-permute-start(f32[4,2,1,128]{3,1,0,2:T(2,128)S(1)} %constant_dynamic-update-slice_fusion.4), channel_id=1, source_target_pairs={{0,384},{128,0},{256,128},{384,256},{1,385},{129,1},{257,129},{385... | collective-permute-start | bytes 12296 | tf_op jit(solution)/shard_map/ppermute | solution.py:196
  167.7 9.8 %collective-permute-start.12 = (f32[4,2,1,128]{3,1,0,2:T(2,128)S(1)}, f32[4,2,1,128]{3,1,0,2:T(2,128)S(1)}, u32[]{:S(2)}, u32[]{:S(2)}) collective-permute-start(f32[4,2,1,128]{3,1,0,2:T(2,128)S(1)} %constant_dynamic-update-slice_fusion.4), channel_id=1, source_target_pairs={{0,256},{128,384},{256,0},{384,128},{1,257},{129,385},{257,1},{385... | collective-permute-start | bytes 12296 | tf_op jit(solution)/shard_map/ppermute | solution.py:196
  170.2 7.0 %collective-permute-start.11 = (f32[4,2,1,128]{3,1,0,2:T(2,128)S(1)}, f32[4,2,1,128]{3,1,0,2:T(2,128)S(1)}, u32[]{:S(2)}, u32[]{:S(2)}) collective-permute-start(f32[4,2,1,128]{3,1,0,2:T(2,128)S(1)} %constant_dynamic-update-slice_fusion.4), channel_id=1, source_target_pairs={{0,128},{128,256},{256,384},{384,0},{1,129},{129,257},{257,385},{3... | collective-permute-start | bytes 12296 | tf_op jit(solution)/shard_map/ppermute | solution.py:196
  212.2 7.8 %collective-permute-start.14 = (bf16[256,4096]{1,0:T(8,128)(2,1)S(1)}, bf16[256,4096]{1,0:T(8,128)(2,1)}, u32[]{:S(2)}, u32[]{:S(2)}) collective-permute-start(bf16[256,4096]{1,0:T(8,128)(2,1)S(1)} %bitcast.126), channel_id=1, source_target_pairs={{0,1},{1,0},{2,3},{3,2},{4,5},{5,4},{6,7},{7,6},{8,9},{9,8},{10,11... | collective-permute-start | bytes 6291464 | tf_op jit(solution)/shard_map/ppermute | solution.py:177
  219.9 3.4 %copy-start.1 = (bf16[1024,4096]{1,0:T(8,128)(2,1)S(1)}, bf16[1024,4096]{1,0:T(8,128)(2,1)}, u32[]{:S(2)}) copy-start(bf16[1024,4096]{1,0:T(8,128)(2,1)} %all-gather.3.cloned.1.call-done.vocab_ref) | copy-start | bytes 25165828
  231.3 11.7 %all-to-all-start.4 = ((f32[32,2,512]{2,1,0:T(2,128)}), f32[32,2,512]{2,1,0:T(2,128)S(1)}, u32[]{:S(2)}, u32[]{:S(2)}) async-start(f32[32,2,512]{2,1,0:T(2,128)} %broadcast_in_dim.147), calls=%async_computation.4 | async-start | bytes 262144 | tf_op jit(solution)/shard_map/all_to_all | solution.py:183
  244.0 21.1 %all-to-all-start.5 = ((f32[16,1,128]{2,1,0:T(1,128)}), f32[16,1,128]{2,1,0:T(1,128)S(1)}, u32[]{:S(2)}, u32[]{:S(2)}) async-start(f32[16,1,128]{2,1,0:T(1,128)} %broadcast_in_dim.148), calls=%async_computation.5 | async-start | bytes 16384 | tf_op jit(solution)/shard_map/all_to_all | solution.py:183
Sparse Core Ops, SparseCore 0:
  10.1 157.7 all-gather.2

commit v3 on v2

--- a/solution.py
+++ b/solution.py
@@ -134,38 +134,53 @@
     out_ref[...] = (y * (g / (1.0 + jnp.exp(-g)))).astype(out_ref.dtype)
 
 
-def score_kernel(share_bits, vocab_bits, place_ref, mine_ref, theirs_ref, label_ref, vocab_ref, out_ref, top_ref, sum_ref, pick_ref):
+def score_kernel(
+    layout, first, final, place_ref, mine_ref, theirs_ref, label_ref, vocab_ref, *refs
+):
+    group, skipped, offset, vocab_local = layout
+    known_ref, (out_ref, state_ref) = (None, refs) if first else (refs[0], refs[1:])
     step = pl.program_id(0)
     tile, half = vocab_ref.shape[0], mine_ref.shape[0]
     core = place_ref[0]
 
     @pl.when(step == 0)
     def _():
-        top_ref[...] = jnp.full_like(top_ref, -3.0e38)
-        sum_ref[...] = jnp.zeros_like(sum_ref)
-        pick_ref[...] = jnp.zeros_like(pick_ref)
-
-    index = step * tile + lax.broadcasted_iota(jnp.int32, (tile, half), 0)
-    group = lax.shift_right_logical(index, share_bits)
-    entry = place_ref[1] + lax.shift_left(group, vocab_bits) + (index & ((1 << share_bits) - 1))
+        if first:
+            state_ref[0:1] = jnp.full((1, 2 * half), -3.0e38, F32)
+            state_ref[1:3] = jnp.zeros((2, 2 * half), F32)
+        else:
+            state_ref[...] = known_ref[...]
+
+    index = step * tile + lax.broadcasted_iota(jnp.int32, (tile, 1), 0)
+    source = lax.div(index, jnp.int32(group))
+    row = index - source * group
+    entry = jnp.where(
+        row < skipped, -1, place_ref[1] + source * vocab_local + (row - skipped + offset)
+    )
     for part, tokens in enumerate((mine_ref, theirs_ref)):
         at = slice(part * half, (part + 1) * half)
         label = jnp.where(core == part, label_ref[:, :half], label_ref[:, half:])
         logits = mm_t(vocab_ref[...], tokens[...])
-        old = top_ref[:, at]
+        found = jnp.where(entry == label, logits, 0.0)
+        if skipped:
+            logits = jnp.where(entry < 0, -3.0e38, logits)
+        old = state_ref[0:1, at]
         top = jnp.maximum(old, jnp.max(logits, axis=0, keepdims=True))
         fresh = jnp.sum(jnp.exp(logits - top), axis=0, keepdims=True)
-        sum_ref[:, at] = sum_ref[:, at] * jnp.exp(old - top) + fresh
-        pick_ref[:, at] += jnp.sum(jnp.where(entry == label, logits, 0.0), axis=0, keepdims=True)
-        top_ref[:, at] = top
+        state_ref[1:2, at] = state_ref[1:2, at] * jnp.exp(old - top) + fresh
+        state_ref[2:3, at] += jnp.sum(found, axis=0, keepdims=True)
+        state_ref[0:1, at] = top
 
     @pl.when(step == pl.num_programs(0) - 1)
     def _():
-        part = top_ref[...] + jnp.log(sum_ref[...])
-        for row, value in enumerate((part, pick_ref[...])):
-            first, second = value[:, :half], value[:, half:]
-            out_ref[row : row + 1, :half] = jnp.where(core == 0, first, second)
-            out_ref[row : row + 1, half:] = jnp.where(core == 0, second, first)
+        if not final:
+            out_ref[...] = state_ref[...]
+            return
+        part = state_ref[0:1] + jnp.log(state_ref[1:2])
+        for row, value in enumerate((part, state_ref[2:3])):
+            left, right = value[:, :half], value[:, half:]
+            out_ref[row : row + 1, :half] = jnp.where(core == 0, left, right)
+            out_ref[row : row + 1, half:] = jnp.where(core == 0, right, left)
 
 
 def cost(flops, nbytes):
@@ -228,8 +243,18 @@
 
     vocab_local = vocabulary_readout.shape[0]
     share = vocab_local // n_head
-    vocab_share = lax.dynamic_slice_in_dim(vocabulary_readout, head * share, share)
-    vocab_rows = lax.all_gather(vocab_share, "z", axis=0, tiled=True)
+    own_columns = closing_projection.shape[1]
+    fold = embed // width
+    held = own_columns // fold
+    early = share * 3 // 8
+    block = closing_projection.T.reshape(fold, held, width).transpose(1, 0, 2).reshape(held, embed)
+    rows_1 = jnp.concatenate(
+        [block, lax.dynamic_slice_in_dim(vocabulary_readout, head * share, early)], axis=0
+    )
+    gathered_1 = lax.all_gather(rows_1, "z", axis=0, tiled=True)
+    rows_2 = lax.dynamic_slice_in_dim(vocabulary_readout, head * share + early, share - early)
+    rows_2, _ = lax.optimization_barrier((rows_2, rows_1))
+    gathered_2 = lax.all_gather(rows_2, "z", axis=0, tiled=True)
 
     chunks = n_blk // pairs
     chunk_rows = CHAN // chunks
@@ -244,9 +269,8 @@
     )(lookup_vector_array, payload_vector_array, raw_forgetting_rate)
     moved = lax.all_to_all(end, ("x", "z"), 0, 0, tiled=True)
 
-    columns, facts, bonus, _ = lax.optimization_barrier(
+    facts, bonus, _ = lax.optimization_barrier(
         (
-            closing_projection.T,
             jnp.concatenate(
                 [
                     following_labels.astype(F32),
@@ -258,12 +282,10 @@
             end,
         )
     )
-    far = [[i + j * 4 for j in range(nz // 4)] for i in range(4)]
-    near = [[i * 4 + j for j in range(4)] for i in range(nz // 4)]
-    columns = spread(columns, "z", far)
     plane = nx * ny * nc
     facts = jnp.pad(facts, (0, LANES - 3 * own)).reshape(1, LANES)
     facts = spread(facts, "c", [list(range(nc))])
+    facts = spread(facts, "y", [list(range(ny))])
     row = pl.BlockSpec((1, LANES), lambda p: (0, p))
     within, high, low = pl.pallas_call(
         within_kernel,
@@ -274,9 +296,7 @@
         cost_estimate=cost(pairs * 60_000_000, 8 * rows * width * 2),
     )(acceptance_vector, lookup_vector_array, payload_vector_array, raw_forgetting_rate, bonus)
 
-    moved, within, high, low, columns, facts = lax.optimization_barrier(
-        (moved, within, high, low, columns, facts)
-    )
+    moved, within, high, low, facts = lax.optimization_barrier((moved, within, high, low, facts))
     prev_seq = jnp.concatenate([jnp.full((1,), -1, jnp.int32), rollout_for_segment[:-1]])
     starts = (rollout_for_segment != prev_seq).astype(jnp.int32)
     meta = jnp.stack([starts, query_text_for_rollout[rollout_for_segment]])
@@ -295,11 +315,7 @@
         out_shape=jax.ShapeDtypeStruct((n_blk, chunk_rows, LANES), F32),
         cost_estimate=cost(1_000_000, 500_000),
     )(meta, moved, prompt)
-    columns, facts, _ = lax.optimization_barrier((columns, facts, entering))
     entering = lax.all_to_all(entering, ("x", "z"), 0, 0, tiled=True)
-    columns = spread(columns, "z", near).transpose(1, 0, 2, 3).reshape(-1, width)
-    facts = spread(facts, "y", [list(range(ny))])
-    entering, facts = lax.optimization_barrier((entering, facts))
     entering = entering.reshape(pairs * CHAN, LANES)
 
     mixed = pl.pallas_call(
@@ -310,6 +326,10 @@
         out_shape=jax.ShapeDtypeStruct((rows, width), BF16),
         cost_estimate=cost(pairs * 20_000_000, 6 * rows * width * 2),
     )(within, high, low, raw_gating_signal, group_layernorm_scaling[None, :], entering)
+
+    columns = gathered_1.reshape(nz, held + early, embed)[:, :held]
+    columns = jnp.concatenate(jnp.split(columns, fold, axis=2), axis=1)
+    columns = columns.reshape(nz * own_columns, width)
 
     mixed = lax.all_gather(mixed, "x", axis=0)
     mixed = mixed.reshape(nx, ny, nc, own, width).transpose(2, 1, 0, 3, 4)
@@ -335,25 +355,36 @@
     other = shifted(tokens, "c", 1)
     count = plane * own
     labels = facts[0].reshape(1, count).astype(jnp.int32)
-    tile = min(256, nz * share)
     place = jnp.stack([ic, ix * nz * vocab_local + head * share]).astype(jnp.int32)
-    whole = lambda *shape: pl.BlockSpec(shape, lambda i: (0,) * len(shape))
-    both = pl.pallas_call(
-        functools.partial(score_kernel, share.bit_length() - 1, vocab_local.bit_length() - 1),
-        grid=(nz * share // tile,),
-        in_specs=[
-            pl.BlockSpec(memory_space=pltpu.SMEM),
-            whole(count // nc, embed),
-            whole(count // nc, embed),
-            whole(1, count),
-            pl.BlockSpec((tile, embed), lambda i: (i, 0)),
-        ],
-        out_specs=whole(2, count),
-        out_shape=jax.ShapeDtypeStruct((2, count), F32),
-        scratch_shapes=[pltpu.VMEM((1, count), F32)] * 3,
-        compiler_params=pltpu.CompilerParams(vmem_limit_bytes=40 * 1024 * 1024),
-        cost_estimate=cost(2 * count * nz * share * embed, (count + nz * share) * embed * 2),
-    )(place, tokens, other, labels, vocab_rows)
+
+    def whole(*shape):
+        return pl.BlockSpec(shape, lambda i: (0,) * len(shape))
+
+    def score(vocab, layout, tile, known=None):
+        first, height = known is None, 3 if known is None else 2
+        return pl.pallas_call(
+            functools.partial(score_kernel, layout, first, not first),
+            grid=(vocab.shape[0] // tile,),
+            in_specs=[
+                pl.BlockSpec(memory_space=pltpu.SMEM),
+                whole(count // nc, embed),
+                whole(count // nc, embed),
+                whole(1, count),
+                pl.BlockSpec((tile, embed), lambda i: (i, 0)),
+            ]
+            + ([] if first else [whole(3, count)]),
+            out_specs=whole(height, count),
+            out_shape=jax.ShapeDtypeStruct((height, count), F32),
+            scratch_shapes=[pltpu.VMEM((3, count), F32)],
+            compiler_params=pltpu.CompilerParams(vmem_limit_bytes=56 * 1024 * 1024),
+            cost_estimate=cost(
+                2 * count * vocab.shape[0] * embed, (count + vocab.shape[0]) * embed * 2
+            ),
+        )(place, tokens, other, labels, vocab, *([] if first else [known]))
+
+    known = score(gathered_1, (held + early, held, 0, vocab_local), gathered_1.shape[0])
+    late = gathered_2.shape[0] // 2
+    both = score(gathered_2, (share - early, 0, early, vocab_local), late, known)
     both = copies(both, ("x", "y", "c"))
     part, picked = both[:, 0], both[:, 1]
     peak = jnp.max(part, axis=0)

time: 274 us -> 244 us (0.89)
  starting transfers between devices: 112 us -> 82.1 us
  waiting for transfers between devices: 60.3 us -> 44.9 us
  Pallas kernels: 21.6 us -> 28.2 us
  local copies, waits for them, and re-layouts: 12.5 us -> 18.2 us
  other arithmetic: 4.95 us -> 7.87 us
    ppermute x13 -> x7, starting transfers between devices: 52.8 us -> 24.1 us  [spread(): piece = lax.ppermute(value, axis, pairs) if step else value]
    ppermute x13 -> x7, waiting for transfers between devices: 33.9 us -> 5.38 us  [spread(): piece = lax.ppermute(value, axis, pairs) if step else value]
    all_to_all x1, waiting for transfers between devices: 0.01 us -> 14.4 us  [per_device(): entering = lax.all_to_all(entering, ('x', 'z'), 0, 0, tiled=True)]
    pallas_call x1 -> x2, Pallas kernels: 7.25 us -> 13.8 us  [score(): pl.pallas_call(functools.partial(score_kernel, layout, first, not first),...]
    all_to_all x2, starting transfers between devices: 13.7 us -> 7.86 us  [copies(): return lax.all_to_all(sent, axes, 0, 0, tiled=True)]
    all_to_all x1, starting transfers between devices: 9.68 us -> 14.7 us  [per_device(): entering = lax.all_to_all(entering, ('x', 'z'), 0, 0, tiled=True)]
    unnamed x17 -> x22, local copies, waits for them, and re-layouts: 4.88 us -> 7.9 us
  transfers between devices with their start and end apart: 21 -> 16, of which waited for: 8 -> 9; matrix products, arithmetic and copies ran while one was open for 4% -> 9% of each run, Pallas kernels for 5% -> 9%
where the time goes in v3:
time: 244 us; the launch traced here: 242 us
  starting transfers between devices  82.1 us (34%)
  waiting for transfers between devices  44.9 us (18%)
  blocking collectives  42.8 us (18%)
  Pallas kernels  28.2 us (12%)
  local copies, waits for them, and re-layouts  18.2 us (7%)
  between operations  14.6 us (6%)
  other arithmetic  7.87 us (3%)
  matrix products  3.17 us (1%)
    all_to_all x1, blocking collectives, copies(): return lax.all_to_all(sent, axes, 0, 0, tiled=True)  31.8 us
    ppermute x7, starting transfers between devices, spread(): piece = lax.ppermute(value, axis, pairs) if step else value  24.1 us
    all_to_all x1, starting transfers between devices, per_device(): moved = lax.all_to_all(end, ('x', 'z'), 0, 0, tiled=True)  19.1 us
    all_to_all x2, waiting for transfers between devices, copies(): return lax.all_to_all(sent, axes, 0, 0, tiled=True)  18.4 us
    all_to_all x1, starting transfers between devices, per_device(): entering = lax.all_to_all(entering, ('x', 'z'), 0, 0, tiled=True)  14.7 us
    all_to_all x1, waiting for transfers between devices, per_device(): entering = lax.all_to_all(entering, ('x', 'z'), 0, 0, tiled=True)  14.4 us
    pallas_call x2, Pallas kernels, score(): pl.pallas_call(functools.partial(score_kernel, layout, first, not first),...  13.8 us
    ppermute x2, starting transfers between devices, shifted(): lax.ppermute(value, axis, [(i, (i + steps) % count) for i in range(count)])  11.2 us
  transfers between devices with their start and end apart: 16, of which 9 were waited for; matrix products, arithmetic and copies ran while one was open for 9% of the time, Pallas kernels for 9%

profile of v3, /device:TPU:1, one launch (start us, length us, event | category | flops | bytes accessed | tf_op | source)
XLA Modules:
  0.0 241.8 jit_solution(14090646785275673849)
XLA Ops:
  7.2 0.9 constant_dynamic-slice_fusion.2
  8.2 1.6 pad_maximum_fusion
  9.8 3.7 %shard_map.176 = f32[64,8,128]{2,1,0:T(8,128)} custom-call(bf16[128,512]{1,0:T(8,128)(2,1)} %k_ref.3, bf16[128,512]{1,0:T(8,128)(2,1)} %v_ref.3, bf16[128,512]{1,0:T(8,128)(2,1)} %w_ref.3), custom_call_target="tpu_custom_call" | custom-call | flops 80000000 | bytes 393216 | tf_op jit(solution)/shard_map/pallas_call | solution.py:262
  13.5 19.1 %all-to-all-start = ((f32[64,8,128]{2,1,0:T(8,128)}), f32[64,8,128]{2,1,0:T(8,128)S(1)}, u32[]{:S(2)}, u32[]{:S(2)}) async-start(f32[64,8,128]{2,1,0:T(8,128)} %shard_map.176), calls=%async_computation | async-start | bytes 524288 | tf_op jit(solution)/shard_map/all_to_all | solution.py:270
  33.9 0.7 pad_maximum_fusion.1
  34.7 2.9 %collective-permute-start = (f32[1,128]{1,0:T(1,128)S(1)}, f32[1,128]{1,0:T(1,128)S(1)}, u32[]{:S(2)}, u32[]{:S(2)}) collective-permute-start(f32[1,128]{1,0:T(1,128)S(1)} %get-tuple-element.37), channel_id=1, source_target_pairs={{0,1},{1,0},{2,3},{3,2},{4,5},{5,4},{6,7},{7,6},{8,9},{9,8},{10,11... | collective-permute-start | bytes 1544 | tf_op jit(solution)/shard_map/ppermute | solution.py:211
  37.7 1.1 reshape.97
  39.7 0.8 fusion.12
  41.2 0.8 gather_fusion
  42.0 4.8 %shard_map.177 = (f32[128,512]{1,0:T(8,128)}, bf16[128,512]{1,0:T(8,128)(2,1)}, bf16[128,512]{1,0:T(8,128)(2,1)}) custom-call(bf16[128,512]{1,0:T(8,128)(2,1)} %r_ref.1, bf16[128,512]{1,0:T(8,128)(2,1)} %k_ref.3, bf16[128,512]{1,0:T(8,128)(2,1)} %v_ref.3, bf16[128,512]{1,0:T(8,128)(2,1)} %w_ref.3, f32[1,512]{1,0:T(1,128)} %bitcast.142), custom_call_target="tpu_custom_call" | custom-call | flops 240000000 | bytes 1048576 | tf_op jit(solution)/shard_map/pallas_call | solution.py:290
  47.4 3.2 %collective-permute-start.1 = (f32[2,1,128]{2,0,1:T(2,128)S(1)}, f32[2,1,128]{2,0,1:T(2,128)S(1)}, u32[]{:S(2)}, u32[]{:S(2)}) collective-permute-start(f32[2,1,128]{2,0,1:T(2,128)S(1)} %dynamic_update_slice.34), channel_id=1, source_target_pairs={{0,2},{2,4},{4,6},{6,0},{1,3},{3,5},{5,7},{7,1},{8,10},{10,12},{12... | collective-permute-start | bytes 3080 | tf_op jit(solution)/shard_map/ppermute | solution.py:211
  50.6 4.5 %collective-permute-start.2 = (f32[2,1,128]{2,0,1:T(2,128)S(1)}, f32[2,1,128]{2,0,1:T(2,128)S(1)}, u32[]{:S(2)}, u32[]{:S(2)}) collective-permute-start(f32[2,1,128]{2,0,1:T(2,128)S(1)} %dynamic_update_slice.34), channel_id=1, source_target_pairs={{0,4},{2,6},{4,0},{6,2},{1,5},{3,7},{5,1},{7,3},{8,12},{10,14},{12... | collective-permute-start | bytes 3080 | tf_op jit(solution)/shard_map/ppermute | solution.py:211
  55.2 3.0 %collective-permute-start.3 = (f32[2,1,128]{2,0,1:T(2,128)S(1)}, f32[2,1,128]{2,0,1:T(2,128)S(1)}, u32[]{:S(2)}, u32[]{:S(2)}) collective-permute-start(f32[2,1,128]{2,0,1:T(2,128)S(1)} %dynamic_update_slice.34), channel_id=1, source_target_pairs={{0,6},{2,0},{4,2},{6,4},{1,7},{3,1},{5,3},{7,5},{8,14},{10,8},{12,... | collective-permute-start | bytes 3080 | tf_op jit(solution)/shard_map/ppermute | solution.py:211
  58.2 1.6 collective-permute-done.3
  59.9 0.7 copy-done.3
  60.6 1.9 shard_map.178
  62.5 14.7 %all-to-all-start.1 = ((f32[64,4,128]{2,1,0:T(4,128)}), f32[64,4,128]{2,1,0:T(4,128)S(1)}, u32[]{:S(2)}, u32[]{:S(2)}) async-start(f32[64,4,128]{2,1,0:T(4,128)} %shard_map.178), calls=%async_computation.1 | async-start | bytes 262144 | tf_op jit(solution)/shard_map/all_to_all | solution.py:318
  77.2 1.7 constant_dynamic-slice_fusion.1
  79.0 14.4 %all-to-all-done.1 = f32[64,4,128]{2,1,0:T(4,128)S(1)} async-done(((f32[64,4,128]{2,1,0:T(4,128)}), f32[64,4,128]{2,1,0:T(4,128)S(1)}, u32[]{:S(2)}, u32[]{:S(2)}) %all-to-all-start.1) | async-done | bytes 131104 | tf_op jit(solution)/shard_map/all_to_all | solution.py:318
  94.0 3.9 %shard_map.179 = bf16[128,512]{1,0:T(8,128)(2,1)} custom-call(f32[128,512]{1,0:T(8,128)} %get-tuple-element.22.wkv_ref, bf16[128,512]{1,0:T(8,128)(2,1)} %get-tuple-element.23.high_ref, bf16[128,512]{1,0:T(8,128)(2,1)} %get-tuple-element.24.low_ref, bf16[128,512]{1,0:T(8,128)(2,1)} %g_ref.1, f32[1,512]{1,0:T(1,128)} %bitcast.139, f32[256,128]{1,0:T(8,128)} %bitcast.130), custom_call_target="tpu_custom_call" | custom-call | flops 80000000 | bytes 786432 | tf_op jit(solution)/shard_map/pallas_call | solution.py:321
  97.9 11.1 %all-gather = bf16[512,512]{1,0:T(8,128)(2,1)S(1)} all-gather(bf16[128,512]{1,0:T(8,128)(2,1)} %shard_map.179), channel_id=2, replica_groups=mesh['x'=4,'z'=16,'y'=4,'c'=2] {'x'}, dimensions={0}, use_global_device_ids=true | all-gather | bytes 655360 | tf_op jit(solution)/shard_map/all_gather | solution.py:334
  109.0 0.9 slice_dynamic-update-slice_fusion.7
  110.0 0.9 slice_dynamic-update-slice_fusion.6
  110.9 0.9 slice_dynamic-update-slice_fusion.5
  111.8 0.9 slice_dynamic-update-slice_fusion.4
  112.7 0.9 slice_dynamic-update-slice_fusion.3
  113.6 0.9 slice_dynamic-update-slice_fusion.2
  114.5 0.9 slice_dynamic-update-slice_fusion.1
  115.5 0.9 slice_dynamic-update-slice_fusion
  116.9 7.4 %collective-permute-start.4 = (f32[256,1024]{1,0:T(8,128)S(1)}, f32[256,1024]{1,0:T(8,128)}, u32[]{:S(2)}, u32[]{:S(2)}) collective-permute-start(f32[256,1024]{1,0:T(8,128)S(1)} %fusion), channel_id=1, source_target_pairs={{0,1},{1,0},{2,3},{3,2},{4,5},{5,4},{6,7},{7,6},{8,9},{9,8},{10,11... | collective-permute-start | bytes 3145736 | tf_op jit(solution)/shard_map/ppermute | solution.py:192
  124.3 2.4 collective-permute-done.4
  126.7 2.7 %convolution_add_fusion = f32[256,1024]{1,0:T(8,128)} fusion(f32[256,1024]{1,0:T(8,128)} %collective-permute-done.4, bf16[1024,512]{1,0:T(8,128)(2,1)S(1)} %bitcast.121, bf16[2,256,512]{2,1,0:T(8,128)(2,1)S(1)} %bitcast.127, s32[]{:T(128)S(6)} %select_n.166), kind=kOutput, calls=%fused_computation.1 | convolution fusion | flops 268697600 | bytes 3407876 | tf_op jit(solution)/shard_map/dot_general | solution.py:36
  129.4 5.0 %all-to-all-start.2 = ((f32[16,16,1024]{2,1,0:T(8,128)}), f32[16,16,1024]{2,1,0:T(8,128)S(1)}, u32[]{:S(2)}, u32[]{:S(2)}) async-start(f32[16,16,1024]{2,1,0:T(8,128)} %bitcast.31), calls=%async_computation.2 | async-start | bytes 2097152 | tf_op jit(solution)/shard_map/all_to_all | solution.py:343
  134.5 3.2 %collective-permute-start.5 = (f32[4,2,1,128]{3,1,0,2:T(2,128)S(1)}, f32[4,2,1,128]{3,1,0,2:T(2,128)S(1)}, u32[]{:S(2)}, u32[]{:S(2)}) collective-permute-start(f32[4,2,1,128]{3,1,0,2:T(2,128)S(1)} %constant_dynamic-update-slice_fusion), channel_id=1, source_target_pairs={{0,128},{128,256},{256,384},{384,0},{1,129},{129,257},{257,385},{3... | collective-permute-start | bytes 12296 | tf_op jit(solution)/shard_map/ppermute | solution.py:211
  137.7 4.3 %collective-permute-start.6 = (f32[4,2,1,128]{3,1,0,2:T(2,128)S(1)}, f32[4,2,1,128]{3,1,0,2:T(2,128)S(1)}, u32[]{:S(2)}, u32[]{:S(2)}) collective-permute-start(f32[4,2,1,128]{3,1,0,2:T(2,128)S(1)} %constant_dynamic-update-slice_fusion), channel_id=1, source_target_pairs={{0,256},{128,384},{256,0},{384,128},{1,257},{129,385},{257,1},{385... | collective-permute-start | bytes 12296 | tf_op jit(solution)/shard_map/ppermute | solution.py:211
  142.0 3.1 %collective-permute-start.7 = (f32[4,2,1,128]{3,1,0,2:T(2,128)S(1)}, f32[4,2,1,128]{3,1,0,2:T(2,128)S(1)}, u32[]{:S(2)}, u32[]{:S(2)}) collective-permute-start(f32[4,2,1,128]{3,1,0,2:T(2,128)S(1)} %constant_dynamic-update-slice_fusion), channel_id=1, source_target_pairs={{0,384},{128,0},{256,128},{384,256},{1,385},{129,1},{257,129},{385... | collective-permute-start | bytes 12296 | tf_op jit(solution)/shard_map/ppermute | solution.py:211
  145.1 3.3 %collective-permute-done.5 = f32[4,2,1,128]{3,1,0,2:T(2,128)S(1)} collective-permute-done((f32[4,2,1,128]{3,1,0,2:T(2,128)S(1)}, f32[4,2,1,128]{3,1,0,2:T(2,128)S(1)}, u32[]{:S(2)}, u32[]{:S(2)}) %collective-permute-start.5) | collective-permute-done | bytes 4128 | tf_op jit(solution)/shard_map/ppermute | solution.py:211
  148.9 1.9 all-to-all-done.2
  151.6 31.8 %all_to_all.30 = bf16[16,16,4096]{2,1,0:T(8,128)(2,1)S(1)} all-to-all(bf16[16,16,4096]{2,1,0:T(8,128)(2,1)S(1)} %broadcast_in_dim.104), channel_id=1, replica_groups=mesh['x'=4,'z'=16,'y'=4,'c'=2] {'y','x'}, dimensions={0} | all-to-all | bytes 4194304 | tf_op jit(solution)/shard_map/all_to_all | solution.py:198
  183.4 3.8 %collective-permute-start.8 = (bf16[256,4096]{1,0:T(8,128)(2,1)S(1)}, bf16[256,4096]{1,0:T(8,128)(2,1)}, u32[]{:S(2)}, u32[]{:S(2)}) collective-permute-start(bf16[256,4096]{1,0:T(8,128)(2,1)S(1)} %bitcast.109), channel_id=1, source_target_pairs={{0,1},{1,0},{2,3},{3,2},{4,5},{5,4},{6,7},{7,6},{8,9},{9,8},{10,11... | collective-permute-start | bytes 6291464 | tf_op jit(solution)/shard_map/ppermute | solution.py:192
  188.7 2.4 %collective-permute-done.8.theirs_ref = bf16[256,4096]{1,0:T(8,128)(2,1)} collective-permute-done((bf16[256,4096]{1,0:T(8,128)(2,1)S(1)}, bf16[256,4096]{1,0:T(8,128)(2,1)}, u32[]{:S(2)}, u32[]{:S(2)}) %collective-permute-start.8) | collective-permute-done | bytes 2097184 | tf_op jit(solution)/shard_map/ppermute | solution.py:192
  191.1 6.7 %shard_map.180.refs_0_ = f32[3,512]{1,0:T(4,128)} custom-call(s32[2]{0:T(128)} %pad_add_fusion.1.place_ref, bf16[256,4096]{1,0:T(8,128)(2,1)} %bitcast.110, bf16[256,4096]{1,0:T(8,128)(2,1)} %collective-permute-done.8.theirs_ref, s32[1,512]{1,0:T(1,128)} %convert_element_type.40.label_ref, bf16[512,4096]{1,0:T(8,128)(2,1)} %all-gather.4.cloned.1.call-done.vocab_ref), custom_call_target="tpu_custom_call" | custom-call | flops 2147483648 | bytes 8388608 | tf_op jit(solution)/shard_map/pallas_call | solution.py:365
  197.8 7.1 %shard_map.181 = f32[2,512]{1,0:T(2,128)} custom-call(s32[2]{0:T(128)} %pad_add_fusion.1.place_ref, bf16[256,4096]{1,0:T(8,128)(2,1)} %bitcast.111, bf16[256,4096]{1,0:T(8,128)(2,1)} %collective-permute-done.8.theirs_ref, s32[1,512]{1,0:T(1,128)} %convert_element_type.40.label_ref, bf16[640,4096]{1,0:T(8,128)(2,1)} %all-gather.6.cloned.1.call-done.vocab_ref, ...), custom_call_target="tpu_custom_call" | custom-call | flops 2684354560 | bytes 9437184 | tf_op jit(solution)/shard_map/pallas_call | solution.py:365
  205.0 1.4 broadcast_in_dim.105
  206.3 3.9 %all-to-all-start.4 = ((f32[32,2,512]{2,1,0:T(2,128)}), f32[32,2,512]{2,1,0:T(2,128)S(1)}, u32[]{:S(2)}, u32[]{:S(2)}) async-start(f32[32,2,512]{2,1,0:T(2,128)} %broadcast_in_dim.105), calls=%async_computation.4 | async-start | bytes 262144 | tf_op jit(solution)/shard_map/all_to_all | solution.py:198
  210.3 7.7 %all-to-all-done.4 = f32[32,2,512]{2,1,0:T(2,128)S(1)} async-done(((f32[32,2,512]{2,1,0:T(2,128)}), f32[32,2,512]{2,1,0:T(2,128)S(1)}, u32[]{:S(2)}, u32[]{:S(2)}) %all-to-all-start.4) | async-done | bytes 131104 | tf_op jit(solution)/shard_map/all_to_all | solution.py:198
  219.1 4.0 %all-to-all-start.5 = ((f32[16,1,128]{2,1,0:T(1,128)}), f32[16,1,128]{2,1,0:T(1,128)S(1)}, u32[]{:S(2)}, u32[]{:S(2)}) async-start(f32[16,1,128]{2,1,0:T(1,128)} %broadcast_in_dim.106), calls=%async_computation.5 | async-start | bytes 16384 | tf_op jit(solution)/shard_map/all_to_all | solution.py:198
  223.6 10.7 %all-to-all-done.5 = f32[16,1,128]{2,1,0:T(1,128)S(1)} async-done(((f32[16,1,128]{2,1,0:T(1,128)}), f32[16,1,128]{2,1,0:T(1,128)S(1)}, u32[]{:S(2)}, u32[]{:S(2)}) %all-to-all-start.5) | async-done | bytes 8224 | tf_op jit(solution)/shard_map/all_to_all | solution.py:198
  (75 shorter events, 10.0 us)
Async XLA Ops:
  7.2 34.0 %copy-start = (s32[16]{0:T(128)S(1)}, s32[16]{0:T(128)}, u32[]{:S(2)}) copy-start(s32[16]{0:T(128)} %param.33) | copy-start | bytes 196
  7.2 101.8 %all-gather.4.cloned.1.call-start = ((), (), s32[]{:S(2)}) async-start(), calls=%async_computation.6 | async-start | bytes 4456448 | tf_op jit(solution)/shard_map/all_gather | solution.py:254
  13.5 46.4 %all-to-all-start = ((f32[64,8,128]{2,1,0:T(8,128)}), f32[64,8,128]{2,1,0:T(8,128)S(1)}, u32[]{:S(2)}, u32[]{:S(2)}) async-start(f32[64,8,128]{2,1,0:T(8,128)} %shard_map.176), calls=%async_computation | async-start | bytes 524288 | tf_op jit(solution)/shard_map/all_to_all | solution.py:270
  34.7 12.7 %collective-permute-start = (f32[1,128]{1,0:T(1,128)S(1)}, f32[1,128]{1,0:T(1,128)S(1)}, u32[]{:S(2)}, u32[]{:S(2)}) collective-permute-start(f32[1,128]{1,0:T(1,128)S(1)} %get-tuple-element.37), channel_id=1, source_target_pairs={{0,1},{1,0},{2,3},{3,2},{4,5},{5,4},{6,7},{7,6},{8,9},{9,8},{10,11... | collective-permute-start | bytes 1544 | tf_op jit(solution)/shard_map/ppermute | solution.py:211
  47.4 10.8 %collective-permute-start.1 = (f32[2,1,128]{2,0,1:T(2,128)S(1)}, f32[2,1,128]{2,0,1:T(2,128)S(1)}, u32[]{:S(2)}, u32[]{:S(2)}) collective-permute-start(f32[2,1,128]{2,0,1:T(2,128)S(1)} %dynamic_update_slice.34), channel_id=1, source_target_pairs={{0,2},{2,4},{4,6},{6,0},{1,3},{3,5},{5,7},{7,1},{8,10},{10,12},{12... | collective-permute-start | bytes 3080 | tf_op jit(solution)/shard_map/ppermute | solution.py:211
  50.6 7.6 %collective-permute-start.2 = (f32[2,1,128]{2,0,1:T(2,128)S(1)}, f32[2,1,128]{2,0,1:T(2,128)S(1)}, u32[]{:S(2)}, u32[]{:S(2)}) collective-permute-start(f32[2,1,128]{2,0,1:T(2,128)S(1)} %dynamic_update_slice.34), channel_id=1, source_target_pairs={{0,4},{2,6},{4,0},{6,2},{1,5},{3,7},{5,1},{7,3},{8,12},{10,14},{12... | collective-permute-start | bytes 3080 | tf_op jit(solution)/shard_map/ppermute | solution.py:211
  55.2 4.7 %collective-permute-start.3 = (f32[2,1,128]{2,0,1:T(2,128)S(1)}, f32[2,1,128]{2,0,1:T(2,128)S(1)}, u32[]{:S(2)}, u32[]{:S(2)}) collective-permute-start(f32[2,1,128]{2,0,1:T(2,128)S(1)} %dynamic_update_slice.34), channel_id=1, source_target_pairs={{0,6},{2,0},{4,2},{6,4},{1,7},{3,1},{5,3},{7,5},{8,14},{10,8},{12,... | collective-permute-start | bytes 3080 | tf_op jit(solution)/shard_map/ppermute | solution.py:211
  59.9 0.7 copy-start.3
  62.5 30.8 %all-to-all-start.1 = ((f32[64,4,128]{2,1,0:T(4,128)}), f32[64,4,128]{2,1,0:T(4,128)S(1)}, u32[]{:S(2)}, u32[]{:S(2)}) async-start(f32[64,4,128]{2,1,0:T(4,128)} %shard_map.178), calls=%async_computation.1 | async-start | bytes 262144 | tf_op jit(solution)/shard_map/all_to_all | solution.py:318
  77.2 120.7 %all-gather.6.cloned.1.call-start = ((), (), s32[]{:S(2)}) async-start(), calls=%async_computation.7 | async-start | bytes 5570560 | tf_op jit(solution)/shard_map/all_gather | solution.py:257
  93.3 0.7 copy-start.4
  116.9 34.0 %copy-start.2 = (bf16[16,4096]{1,0:T(8,128)(2,1)S(1)}, bf16[16,4096]{1,0:T(8,128)(2,1)}, u32[]{:S(2)}) copy-start(bf16[16,4096]{1,0:T(8,128)(2,1)} %param.26) | copy-start | bytes 393220
  116.9 34.4 %copy-start.5 = (f32[4096]{0:T(1024)S(1)}, f32[4096]{0:T(1024)}, u32[]{:S(2)}) copy-start(f32[4096]{0:T(1024)} %param.25) | copy-start | bytes 49156
  116.9 9.8 %collective-permute-start.4 = (f32[256,1024]{1,0:T(8,128)S(1)}, f32[256,1024]{1,0:T(8,128)}, u32[]{:S(2)}, u32[]{:S(2)}) collective-permute-start(f32[256,1024]{1,0:T(8,128)S(1)} %fusion), channel_id=1, source_target_pairs={{0,1},{1,0},{2,3},{3,2},{4,5},{5,4},{6,7},{7,6},{8,9},{9,8},{10,11... | collective-permute-start | bytes 3145736 | tf_op jit(solution)/shard_map/ppermute | solution.py:192
  129.4 21.3 %all-to-all-start.2 = ((f32[16,16,1024]{2,1,0:T(8,128)}), f32[16,16,1024]{2,1,0:T(8,128)S(1)}, u32[]{:S(2)}, u32[]{:S(2)}) async-start(f32[16,16,1024]{2,1,0:T(8,128)} %bitcast.31), calls=%async_computation.2 | async-start | bytes 2097152 | tf_op jit(solution)/shard_map/all_to_all | solution.py:343
  134.5 13.9 %collective-permute-start.5 = (f32[4,2,1,128]{3,1,0,2:T(2,128)S(1)}, f32[4,2,1,128]{3,1,0,2:T(2,128)S(1)}, u32[]{:S(2)}, u32[]{:S(2)}) collective-permute-start(f32[4,2,1,128]{3,1,0,2:T(2,128)S(1)} %constant_dynamic-update-slice_fusion), channel_id=1, source_target_pairs={{0,128},{128,256},{256,384},{384,0},{1,129},{129,257},{257,385},{3... | collective-permute-start | bytes 12296 | tf_op jit(solution)/shard_map/ppermute | solution.py:211
  137.7 11.2 %collective-permute-start.6 = (f32[4,2,1,128]{3,1,0,2:T(2,128)S(1)}, f32[4,2,1,128]{3,1,0,2:T(2,128)S(1)}, u32[]{:S(2)}, u32[]{:S(2)}) collective-permute-start(f32[4,2,1,128]{3,1,0,2:T(2,128)S(1)} %constant_dynamic-update-slice_fusion), channel_id=1, source_target_pairs={{0,256},{128,384},{256,0},{384,128},{1,257},{129,385},{257,1},{385... | collective-permute-start | bytes 12296 | tf_op jit(solution)/shard_map/ppermute | solution.py:211
  142.0 6.9 %collective-permute-start.7 = (f32[4,2,1,128]{3,1,0,2:T(2,128)S(1)}, f32[4,2,1,128]{3,1,0,2:T(2,128)S(1)}, u32[]{:S(2)}, u32[]{:S(2)}) collective-permute-start(f32[4,2,1,128]{3,1,0,2:T(2,128)S(1)} %constant_dynamic-update-slice_fusion), channel_id=1, source_target_pairs={{0,384},{128,0},{256,128},{384,256},{1,385},{129,1},{257,129},{385... | collective-permute-start | bytes 12296 | tf_op jit(solution)/shard_map/ppermute | solution.py:211
  183.4 7.7 %copy-start.1 = (bf16[16,16,4096]{2,1,0:T(8,128)(2,1)}, bf16[16,16,4096]{2,1,0:T(8,128)(2,1)S(1)}, u32[]{:S(2)}) copy-start(bf16[16,16,4096]{2,1,0:T(8,128)(2,1)S(1)} %all_to_all.30) | copy-start | bytes 6291460
  183.4 7.7 %collective-permute-start.8 = (bf16[256,4096]{1,0:T(8,128)(2,1)S(1)}, bf16[256,4096]{1,0:T(8,128)(2,1)}, u32[]{:S(2)}, u32[]{:S(2)}) collective-permute-start(bf16[256,4096]{1,0:T(8,128)(2,1)S(1)} %bitcast.109), channel_id=1, source_target_pairs={{0,1},{1,0},{2,3},{3,2},{4,5},{5,4},{6,7},{7,6},{8,9},{9,8},{10,11... | collective-permute-start | bytes 6291464 | tf_op jit(solution)/shard_map/ppermute | solution.py:192
  197.8 12.4 %copy-start.6 = (s32[64]{0:T(128)S(1)}, s32[64]{0:T(128)}, u32[]{:S(2)}) copy-start(s32[64]{0:T(128)} %param.32) | copy-start | bytes 772
  206.3 11.7 %all-to-all-start.4 = ((f32[32,2,512]{2,1,0:T(2,128)}), f32[32,2,512]{2,1,0:T(2,128)S(1)}, u32[]{:S(2)}, u32[]{:S(2)}) async-start(f32[32,2,512]{2,1,0:T(2,128)} %broadcast_in_dim.105), calls=%async_computation.4 | async-start | bytes 262144 | tf_op jit(solution)/shard_map/all_to_all | solution.py:198
  219.1 15.2 %all-to-all-start.5 = ((f32[16,1,128]{2,1,0:T(1,128)}), f32[16,1,128]{2,1,0:T(1,128)S(1)}, u32[]{:S(2)}, u32[]{:S(2)}) async-start(f32[16,1,128]{2,1,0:T(1,128)} %broadcast_in_dim.106), calls=%async_computation.5 | async-start | bytes 16384 | tf_op jit(solution)/shard_map/all_to_all | solution.py:198
Sparse Core Ops, SparseCore 0:
  10.1 91.7 all-gather.3
  104.0 77.9 all-gather.5

commit v4 on v3

--- a/solution.py
+++ b/solution.py
@@ -134,6 +134,23 @@
     out_ref[...] = (y * (g / (1.0 + jnp.exp(-g)))).astype(out_ref.dtype)
 
 
+def project_kernel(shape, place_ref, mixed_ref, block_ref, mine_ref, theirs_ref, columns_ref):
+    ny, nc, own = shape
+    fold, held = block_ref.shape[2] // columns_ref.shape[1], block_ref.shape[1]
+    width = columns_ref.shape[1]
+    for z in range(block_ref.shape[0]):
+        for b in range(fold):
+            at = (z * fold + b) * held
+            columns_ref[at : at + held, :] = block_ref[z, :, b * width : (b + 1) * width]
+    for out_ref, core in ((theirs_ref, 1 - place_ref[0]), (mine_ref, place_ref[0])):
+        rows = [
+            mixed_ref[x, pl.ds(pl.multiple_of((y * nc + core) * own, own), own), :]
+            for y in range(ny)
+            for x in range(mixed_ref.shape[0])
+        ]
+        out_ref[...] = mm_t(jnp.concatenate(rows, axis=0), columns_ref[...])
+
+
 def score_kernel(
     layout, first, final, place_ref, mine_ref, theirs_ref, label_ref, vocab_ref, *refs
 ):
@@ -185,6 +202,18 @@
 
 def cost(flops, nbytes):
     return pl.CostEstimate(flops=flops, bytes_accessed=nbytes, transcendentals=0)
+
+
+def limit(mib):
+    return pltpu.CompilerParams(vmem_limit_bytes=mib * 1024 * 1024)
+
+
+def in_hbm(value):
+    return pltpu.with_memory_space_constraint(value, pltpu.HBM)
+
+
+def whole(*shape):
+    return pl.BlockSpec(shape, lambda i: (0,) * len(shape))
 
 
 def shifted(value, axis, steps):
@@ -246,15 +275,12 @@
     own_columns = closing_projection.shape[1]
     fold = embed // width
     held = own_columns // fold
-    early = share * 3 // 8
+    early = share // 4
     block = closing_projection.T.reshape(fold, held, width).transpose(1, 0, 2).reshape(held, embed)
     rows_1 = jnp.concatenate(
         [block, lax.dynamic_slice_in_dim(vocabulary_readout, head * share, early)], axis=0
     )
     gathered_1 = lax.all_gather(rows_1, "z", axis=0, tiled=True)
-    rows_2 = lax.dynamic_slice_in_dim(vocabulary_readout, head * share + early, share - early)
-    rows_2, _ = lax.optimization_barrier((rows_2, rows_1))
-    gathered_2 = lax.all_gather(rows_2, "z", axis=0, tiled=True)
 
     chunks = n_blk // pairs
     chunk_rows = CHAN // chunks
@@ -265,6 +291,7 @@
         in_specs=[col] * 3,
         out_specs=pl.BlockSpec((chunks, 2 * chunk_rows, LANES), lambda p: (p, 0, 0)),
         out_shape=jax.ShapeDtypeStruct((n_blk, 2 * chunk_rows, LANES), F32),
+        compiler_params=limit(60),
         cost_estimate=cost(pairs * 20_000_000, 3 * rows * width * 2),
     )(lookup_vector_array, payload_vector_array, raw_forgetting_rate)
     moved = lax.all_to_all(end, ("x", "z"), 0, 0, tiled=True)
@@ -285,6 +312,8 @@
     plane = nx * ny * nc
     facts = jnp.pad(facts, (0, LANES - 3 * own)).reshape(1, LANES)
     facts = spread(facts, "c", [list(range(nc))])
+    vocabulary, facts = lax.optimization_barrier((vocabulary_readout, facts))
+    rows_2 = lax.dynamic_slice_in_dim(vocabulary, head * share + early, share - early)
     facts = spread(facts, "y", [list(range(ny))])
     row = pl.BlockSpec((1, LANES), lambda p: (0, p))
     within, high, low = pl.pallas_call(
@@ -293,10 +322,10 @@
         in_specs=[col] * 4 + [row],
         out_specs=[col] * 3,
         out_shape=[jax.ShapeDtypeStruct((rows, width), t) for t in (F32, BF16, BF16)],
+        compiler_params=limit(60),
         cost_estimate=cost(pairs * 60_000_000, 8 * rows * width * 2),
     )(acceptance_vector, lookup_vector_array, payload_vector_array, raw_forgetting_rate, bonus)
 
-    moved, within, high, low, facts = lax.optimization_barrier((moved, within, high, low, facts))
     prev_seq = jnp.concatenate([jnp.full((1,), -1, jnp.int32), rollout_for_segment[:-1]])
     starts = (rollout_for_segment != prev_seq).astype(jnp.int32)
     meta = jnp.stack([starts, query_text_for_rollout[rollout_for_segment]])
@@ -307,12 +336,17 @@
         (prompts, 1, 2, chunk_rows, CHAN),
     )[:, 0]
     prompt = prompt.transpose(0, 2, 1, 3).reshape(prompts, chunk_rows, LANES).astype(F32)
+    moved, within, high, low, facts, rows_2, meta, prompt = lax.optimization_barrier(
+        (moved, within, high, low, facts, rows_2, meta, prompt)
+    )
+    gathered_2 = lax.all_gather(rows_2, "z", axis=0, tiled=True)
     vmem = pl.BlockSpec(memory_space=pltpu.VMEM)
     entering = pl.pallas_call(
         functools.partial(relay_kernel, chunk_rows),
         in_specs=[pl.BlockSpec(memory_space=pltpu.SMEM), vmem, vmem],
         out_specs=vmem,
         out_shape=jax.ShapeDtypeStruct((n_blk, chunk_rows, LANES), F32),
+        compiler_params=limit(4),
         cost_estimate=cost(1_000_000, 500_000),
     )(meta, moved, prompt)
     entering = lax.all_to_all(entering, ("x", "z"), 0, 0, tiled=True)
@@ -324,18 +358,28 @@
         in_specs=[col] * 4 + [row, pl.BlockSpec((CHAN, LANES), lambda p: (p, 0))],
         out_specs=col,
         out_shape=jax.ShapeDtypeStruct((rows, width), BF16),
+        compiler_params=limit(8),
         cost_estimate=cost(pairs * 20_000_000, 6 * rows * width * 2),
     )(within, high, low, raw_gating_signal, group_layernorm_scaling[None, :], entering)
 
-    columns = gathered_1.reshape(nz, held + early, embed)[:, :held]
-    columns = jnp.concatenate(jnp.split(columns, fold, axis=2), axis=1)
-    columns = columns.reshape(nz * own_columns, width)
-
     mixed = lax.all_gather(mixed, "x", axis=0)
-    mixed = mixed.reshape(nx, ny, nc, own, width).transpose(2, 1, 0, 3, 4)
-    mixed = mixed.reshape(nc, ny * nx * own, width)
-    theirs = mm_t(lax.dynamic_index_in_dim(mixed, 1 - ic, 0, False), columns)
-    mine = mm_t(lax.dynamic_index_in_dim(mixed, ic, 0, False), columns)
+    place = jnp.stack([ic, ix * nz * vocab_local + head * share]).astype(jnp.int32)
+    half = jax.ShapeDtypeStruct((ny * nx * own, embed // nx), F32)
+    smem = pl.BlockSpec(memory_space=pltpu.SMEM)
+    mine, theirs = pl.pallas_call(
+        functools.partial(project_kernel, (ny, nc, own)),
+        grid=(1,),
+        in_specs=[
+            smem,
+            whole(nx, rows, width),
+            pl.BlockSpec((nz, held, embed), lambda i: (0, 0, 0)),
+        ],
+        out_specs=[whole(*half.shape)] * 2,
+        out_shape=[half, half],
+        scratch_shapes=[pltpu.VMEM((nz * own_columns, width), BF16)],
+        compiler_params=limit(24),
+        cost_estimate=cost(4 * half.size * width, 4_000_000),
+    )(place, mixed, in_hbm(gathered_1.reshape(nz, held + early, embed)))
     partial = mine + shifted(theirs, "c", 1)
     partial = partial.reshape(ny * nx, own, embed // nx)
     partial, facts = lax.optimization_barrier((partial, facts))
@@ -349,41 +393,36 @@
     normed = ((hidden - hmean) / jnp.sqrt(hvar + 1e-05) * closing_layernorm_scaling).astype(BF16)
 
     normed, facts = lax.optimization_barrier((normed, facts))
+
+    tokens = copies(normed, ("y", "x")).reshape(ny * nx * own, embed)
     facts = facts[..., 0, : 3 * own].reshape(nx, ny, nc, 3, own).transpose(3, 2, 1, 0, 4)
-
-    tokens = copies(normed, ("y", "x")).reshape(ny * nx * own, embed)
     other = shifted(tokens, "c", 1)
     count = plane * own
     labels = facts[0].reshape(1, count).astype(jnp.int32)
-    place = jnp.stack([ic, ix * nz * vocab_local + head * share]).astype(jnp.int32)
-
-    def whole(*shape):
-        return pl.BlockSpec(shape, lambda i: (0,) * len(shape))
-
     def score(vocab, layout, tile, known=None):
         first, height = known is None, 3 if known is None else 2
         return pl.pallas_call(
             functools.partial(score_kernel, layout, first, not first),
             grid=(vocab.shape[0] // tile,),
             in_specs=[
-                pl.BlockSpec(memory_space=pltpu.SMEM),
-                whole(count // nc, embed),
-                whole(count // nc, embed),
-                whole(1, count),
+                smem,
+                vmem,
+                vmem,
+                vmem,
                 pl.BlockSpec((tile, embed), lambda i: (i, 0)),
             ]
-            + ([] if first else [whole(3, count)]),
+            + ([] if first else [vmem]),
             out_specs=whole(height, count),
             out_shape=jax.ShapeDtypeStruct((height, count), F32),
             scratch_shapes=[pltpu.VMEM((3, count), F32)],
-            compiler_params=pltpu.CompilerParams(vmem_limit_bytes=56 * 1024 * 1024),
+            compiler_params=limit(24),
             cost_estimate=cost(
                 2 * count * vocab.shape[0] * embed, (count + vocab.shape[0]) * embed * 2
             ),
-        )(place, tokens, other, labels, vocab, *([] if first else [known]))
+        )(place, tokens, other, labels, in_hbm(vocab), *([] if first else [known]))
 
     known = score(gathered_1, (held + early, held, 0, vocab_local), gathered_1.shape[0])
-    late = gathered_2.shape[0] // 2
+    late = gathered_2.shape[0] // 3
     both = score(gathered_2, (share - early, 0, early, vocab_local), late, known)
     both = copies(both, ("x", "y", "c"))
     part, picked = both[:, 0], both[:, 1]

time: 244 us -> 241 us (0.988)
  starting transfers between devices: 82.1 us -> 91.2 us
  local copies, waits for them, and re-layouts: 18.2 us -> 10.4 us
  matrix products: 3.17 us -> 0 us
  Pallas kernels: 28.2 us -> 25.3 us
  waiting for transfers between devices: 44.9 us -> 47.6 us
    all_to_all x2, starting transfers between devices: 7.86 us -> 17.2 us  [copies(): return lax.all_to_all(sent, axes, 0, 0, tiled=True)]
    unnamed x22 -> x19, local copies, waits for them, and re-layouts: 7.9 us -> 2.9 us
    dot_general x2 -> x0, matrix products: 3.17 us -> none  [mm_t(): lax.dot_general(a, b, (((1,), (1,)), ((), ())), preferred_element_type=F32)]
    pallas_call x2, Pallas kernels: 13.8 us -> 11.3 us  [score(): pl.pallas_call(functools.partial(score_kernel, layout, first, not first),...]
  transfers between devices with their start and end apart: 16 -> 16, of which waited for: 9 -> 9; matrix products, arithmetic and copies ran while one was open for 9% -> 4% of each run, Pallas kernels for 9% -> 8%
where the time goes in v4:
time: 241 us; the launch traced here: 239 us
  starting transfers between devices  91.2 us (38%)
  waiting for transfers between devices  47.6 us (20%)
  blocking collectives  43.2 us (18%)
  Pallas kernels  25.3 us (10%)
  between operations  14.7 us (6%)
  local copies, waits for them, and re-layouts  10.4 us (4%)
  other arithmetic  7.09 us (3%)
    all_to_all x1, blocking collectives, copies(): return lax.all_to_all(sent, axes, 0, 0, tiled=True)  32 us
    ppermute x7, starting transfers between devices, spread(): piece = lax.ppermute(value, axis, pairs) if step else value  24.1 us
    all_to_all x1, starting transfers between devices, per_device(): moved = lax.all_to_all(end, ('x', 'z'), 0, 0, tiled=True)  19.1 us
    all_to_all x2, waiting for transfers between devices, copies(): return lax.all_to_all(sent, axes, 0, 0, tiled=True)  18.4 us
    all_to_all x2, starting transfers between devices, copies(): return lax.all_to_all(sent, axes, 0, 0, tiled=True)  17.2 us
    all_to_all x1, waiting for transfers between devices, per_device(): entering = lax.all_to_all(entering, ('x', 'z'), 0, 0, tiled=True)  15.8 us
    all_to_all x1, starting transfers between devices, per_device(): entering = lax.all_to_all(entering, ('x', 'z'), 0, 0, tiled=True)  14.8 us
    pallas_call x2, Pallas kernels, score(): pl.pallas_call(functools.partial(score_kernel, layout, first, not first),...  11.3 us
  transfers between devices with their start and end apart: 16, of which 9 were waited for; matrix products, arithmetic and copies ran while one was open for 4% of the time, Pallas kernels for 8%

profile of v4, /device:TPU:1, one launch (start us, length us, event | category | flops | bytes accessed | tf_op | source)
XLA Modules:
  0.0 239.4 jit_solution(1368927661744758089)
XLA Ops:
  7.3 0.9 constant_dynamic-slice_fusion.1
  8.2 1.6 pad_maximum_fusion
  9.8 3.7 %shard_map.176 = f32[64,8,128]{2,1,0:T(8,128)} custom-call(bf16[128,512]{1,0:T(8,128)(2,1)} %k_ref.3, bf16[128,512]{1,0:T(8,128)(2,1)} %v_ref.3, bf16[128,512]{1,0:T(8,128)(2,1)} %w_ref.3), custom_call_target="tpu_custom_call" | custom-call | flops 80000000 | bytes 393216 | tf_op jit(solution)/shard_map/pallas_call | solution.py:288
  13.5 19.1 %all-to-all-start = ((f32[64,8,128]{2,1,0:T(8,128)}), f32[64,8,128]{2,1,0:T(8,128)S(1)}, u32[]{:S(2)}, u32[]{:S(2)}) async-start(f32[64,8,128]{2,1,0:T(8,128)} %shard_map.176), calls=%async_computation | async-start | bytes 524288 | tf_op jit(solution)/shard_map/all_to_all | solution.py:297
  32.6 0.7 convert_element_type.35
  33.3 0.7 convert_element_type.36
  34.0 0.7 pad_maximum_fusion.1
  34.7 2.9 %collective-permute-start = (f32[1,128]{1,0:T(1,128)S(1)}, f32[1,128]{1,0:T(1,128)S(1)}, u32[]{:S(2)}, u32[]{:S(2)}) collective-permute-start(f32[1,128]{1,0:T(1,128)S(1)} %get-tuple-element.49), channel_id=1, source_target_pairs={{0,1},{1,0},{2,3},{3,2},{4,5},{5,4},{6,7},{7,6},{8,9},{9,8},{10,11... | collective-permute-start | bytes 1544 | tf_op jit(solution)/shard_map/ppermute | solution.py:240
  37.7 1.1 reshape.88
  39.2 0.7 compare_select_fusion
  39.8 0.8 gather_fusion
  40.6 4.8 %shard_map.177 = (f32[128,512]{1,0:T(8,128)}, bf16[128,512]{1,0:T(8,128)(2,1)}, bf16[128,512]{1,0:T(8,128)(2,1)}) custom-call(bf16[128,512]{1,0:T(8,128)(2,1)} %r_ref.1, bf16[128,512]{1,0:T(8,128)(2,1)} %k_ref.3, bf16[128,512]{1,0:T(8,128)(2,1)} %v_ref.3, bf16[128,512]{1,0:T(8,128)(2,1)} %w_ref.3, f32[1,512]{1,0:T(1,128)} %bitcast.119), custom_call_target="tpu_custom_call" | custom-call | flops 240000000 | bytes 1048576 | tf_op jit(solution)/shard_map/pallas_call | solution.py:319
  45.6 3.2 %collective-permute-start.1 = (f32[2,1,128]{2,0,1:T(2,128)S(1)}, f32[2,1,128]{2,0,1:T(2,128)S(1)}, u32[]{:S(2)}, u32[]{:S(2)}) collective-permute-start(f32[2,1,128]{2,0,1:T(2,128)S(1)} %dynamic_update_slice.34), channel_id=1, source_target_pairs={{0,2},{2,4},{4,6},{6,0},{1,3},{3,5},{5,7},{7,1},{8,10},{10,12},{12... | collective-permute-start | bytes 3080 | tf_op jit(solution)/shard_map/ppermute | solution.py:240
  48.8 4.5 %collective-permute-start.2 = (f32[2,1,128]{2,0,1:T(2,128)S(1)}, f32[2,1,128]{2,0,1:T(2,128)S(1)}, u32[]{:S(2)}, u32[]{:S(2)}) collective-permute-start(f32[2,1,128]{2,0,1:T(2,128)S(1)} %dynamic_update_slice.34), channel_id=1, source_target_pairs={{0,4},{2,6},{4,0},{6,2},{1,5},{3,7},{5,1},{7,3},{8,12},{10,14},{12... | collective-permute-start | bytes 3080 | tf_op jit(solution)/shard_map/ppermute | solution.py:240
  53.3 3.0 %collective-permute-start.3 = (f32[2,1,128]{2,0,1:T(2,128)S(1)}, f32[2,1,128]{2,0,1:T(2,128)S(1)}, u32[]{:S(2)}, u32[]{:S(2)}) collective-permute-start(f32[2,1,128]{2,0,1:T(2,128)S(1)} %dynamic_update_slice.34), channel_id=1, source_target_pairs={{0,6},{2,0},{4,2},{6,4},{1,7},{3,1},{5,3},{7,5},{8,14},{10,8},{12,... | collective-permute-start | bytes 3080 | tf_op jit(solution)/shard_map/ppermute | solution.py:240
  56.3 1.8 constant_dynamic-slice_fusion.3
  58.2 1.5 shard_map.178
  59.7 14.8 %all-to-all-start.1 = ((f32[64,4,128]{2,1,0:T(4,128)}), f32[64,4,128]{2,1,0:T(4,128)S(1)}, u32[]{:S(2)}, u32[]{:S(2)}) async-start(f32[64,4,128]{2,1,0:T(4,128)} %shard_map.178), calls=%async_computation.1 | async-start | bytes 262144 | tf_op jit(solution)/shard_map/all_to_all | solution.py:352
  74.7 15.8 %all-to-all-done.1 = f32[64,4,128]{2,1,0:T(4,128)S(1)} async-done(((f32[64,4,128]{2,1,0:T(4,128)}), f32[64,4,128]{2,1,0:T(4,128)S(1)}, u32[]{:S(2)}, u32[]{:S(2)}) %all-to-all-start.1) | async-done | bytes 131104 | tf_op jit(solution)/shard_map/all_to_all | solution.py:352
  90.4 0.9 copy-done.1
  91.4 0.9 copy-done.3
  92.3 0.9 copy-done.4
  93.2 2.0 shard_map.179
  95.2 11.2 %all-gather = bf16[512,512]{1,0:T(8,128)(2,1)S(1)} all-gather(bf16[128,512]{1,0:T(8,128)(2,1)S(1)} %shard_map.179), channel_id=2, replica_groups=mesh['x'=4,'z'=16,'y'=4,'c'=2] {'x'}, dimensions={0}, use_global_device_ids=true | all-gather | bytes 655360 | tf_op jit(solution)/shard_map/all_gather | solution.py:365
  106.5 2.0 shard_map.180
  108.5 7.4 %collective-permute-start.4 = (f32[256,1024]{1,0:T(8,128)S(1)}, f32[256,1024]{1,0:T(8,128)S(1)}, u32[]{:S(2)}, u32[]{:S(2)}) collective-permute-start(f32[256,1024]{1,0:T(8,128)S(1)} %get-tuple-element.37), channel_id=1, source_target_pairs={{0,1},{1,0},{2,3},{3,2},{4,5},{5,4},{6,7},{7,6},{8,9},{9,8},{10,11... | collective-permute-start | bytes 3145736 | tf_op jit(solution)/shard_map/ppermute | solution.py:221
  115.8 2.3 collective-permute-done.4
  118.1 1.1 add.175
  119.2 4.8 %all-to-all-start.2 = ((f32[16,16,1024]{2,1,0:T(8,128)}), f32[16,16,1024]{2,1,0:T(8,128)S(1)}, u32[]{:S(2)}, u32[]{:S(2)}) async-start(f32[16,16,1024]{2,1,0:T(8,128)} %bitcast.27), calls=%async_computation.2 | async-start | bytes 2097152 | tf_op jit(solution)/shard_map/all_to_all | solution.py:387
  124.1 3.2 %collective-permute-start.5 = (f32[4,2,1,128]{3,1,0,2:T(2,128)S(1)}, f32[4,2,1,128]{3,1,0,2:T(2,128)S(1)}, u32[]{:S(2)}, u32[]{:S(2)}) collective-permute-start(f32[4,2,1,128]{3,1,0,2:T(2,128)S(1)} %constant_dynamic-update-slice_fusion), channel_id=1, source_target_pairs={{0,128},{128,256},{256,384},{384,0},{1,129},{129,257},{257,385},{3... | collective-permute-start | bytes 12296 | tf_op jit(solution)/shard_map/ppermute | solution.py:240
  127.3 4.3 %collective-permute-start.6 = (f32[4,2,1,128]{3,1,0,2:T(2,128)S(1)}, f32[4,2,1,128]{3,1,0,2:T(2,128)S(1)}, u32[]{:S(2)}, u32[]{:S(2)}) collective-permute-start(f32[4,2,1,128]{3,1,0,2:T(2,128)S(1)} %constant_dynamic-update-slice_fusion), channel_id=1, source_target_pairs={{0,256},{128,384},{256,0},{384,128},{1,257},{129,385},{257,1},{385... | collective-permute-start | bytes 12296 | tf_op jit(solution)/shard_map/ppermute | solution.py:240
  131.6 3.1 %collective-permute-start.7 = (f32[4,2,1,128]{3,1,0,2:T(2,128)S(1)}, f32[4,2,1,128]{3,1,0,2:T(2,128)S(1)}, u32[]{:S(2)}, u32[]{:S(2)}) collective-permute-start(f32[4,2,1,128]{3,1,0,2:T(2,128)S(1)} %constant_dynamic-update-slice_fusion), channel_id=1, source_target_pairs={{0,384},{128,0},{256,128},{384,256},{1,385},{129,1},{257,129},{385... | collective-permute-start | bytes 12296 | tf_op jit(solution)/shard_map/ppermute | solution.py:240
  134.7 3.3 %collective-permute-done.5 = f32[4,2,1,128]{3,1,0,2:T(2,128)S(1)} collective-permute-done((f32[4,2,1,128]{3,1,0,2:T(2,128)S(1)}, f32[4,2,1,128]{3,1,0,2:T(2,128)S(1)}, u32[]{:S(2)}, u32[]{:S(2)}) %collective-permute-start.5) | collective-permute-done | bytes 4128 | tf_op jit(solution)/shard_map/ppermute | solution.py:240
  138.5 1.8 all-to-all-done.2
  141.2 32.0 %all_to_all.30 = bf16[16,16,4096]{2,1,0:T(8,128)(2,1)S(1)} all-to-all(bf16[16,16,4096]{2,1,0:T(8,128)(2,1)S(1)} %broadcast_in_dim.104), channel_id=1, replica_groups=mesh['x'=4,'z'=16,'y'=4,'c'=2] {'y','x'}, dimensions={0} | all-to-all | bytes 4194304 | tf_op jit(solution)/shard_map/all_to_all | solution.py:227
  173.2 3.7 %collective-permute-start.8 = (bf16[256,4096]{1,0:T(8,128)(2,1)S(1)}, bf16[256,4096]{1,0:T(8,128)(2,1)}, u32[]{:S(2)}, u32[]{:S(2)}) collective-permute-start(bf16[256,4096]{1,0:T(8,128)(2,1)S(1)} %bitcast.97), channel_id=1, source_target_pairs={{0,1},{1,0},{2,3},{3,2},{4,5},{5,4},{6,7},{7,6},{8,9},{9,8},{10,11... | collective-permute-start | bytes 6291464 | tf_op jit(solution)/shard_map/ppermute | solution.py:221
  177.2 3.6 %collective-permute-done.8.theirs_ref = bf16[256,4096]{1,0:T(8,128)(2,1)} collective-permute-done((bf16[256,4096]{1,0:T(8,128)(2,1)S(1)}, bf16[256,4096]{1,0:T(8,128)(2,1)}, u32[]{:S(2)}, u32[]{:S(2)}) %collective-permute-start.8) | collective-permute-done | bytes 2097184 | tf_op jit(solution)/shard_map/ppermute | solution.py:221
  180.8 4.6 %shard_map.181.refs_0_ = f32[3,512]{1,0:T(4,128)S(1)} custom-call(s32[2]{0:T(128)S(1)} %pad_add_fusion.1.place_ref, bf16[256,4096]{1,0:T(8,128)(2,1)S(1)} %bitcast.98, bf16[256,4096]{1,0:T(8,128)(2,1)} %collective-permute-done.8.theirs_ref, s32[1,512]{1,0:T(1,128)S(1)} %convert_element_type.43.label_ref, bf16[384,4096]{1,0:T(8,128)(2,1)} %all-gather.4.cloned.1.call-done.vocab_ref), custom_call_target="tpu_custom_call" | custom-call | flops 1610612736 | bytes 7340032 | tf_op jit(solution)/shard_map/pallas_call | solution.py:404
  185.4 1.8 all-gather.6.cloned.1.call-done.vocab_ref
  187.2 6.7 %shard_map.182 = f32[2,512]{1,0:T(2,128)S(1)} custom-call(s32[2]{0:T(128)S(1)} %pad_add_fusion.1.place_ref, bf16[256,4096]{1,0:T(8,128)(2,1)S(1)} %bitcast.99, bf16[256,4096]{1,0:T(8,128)(2,1)} %collective-permute-done.8.theirs_ref, s32[1,512]{1,0:T(1,128)S(1)} %convert_element_type.43.label_ref, bf16[768,4096]{1,0:T(8,128)(2,1)} %all-gather.6.cloned.1.call-done.vocab_ref, ...), custom_call_target="tpu_custom_call" | custom-call | flops 3221225472 | bytes 10485760 | tf_op jit(solution)/shard_map/pallas_call | solution.py:404
  193.9 0.7 broadcast_in_dim.105
  194.6 9.9 %all-to-all-start.4 = ((f32[32,2,512]{2,1,0:T(2,128)}), f32[32,2,512]{2,1,0:T(2,128)S(1)}, u32[]{:S(2)}, u32[]{:S(2)}) async-start(f32[32,2,512]{2,1,0:T(2,128)} %broadcast_in_dim.105), calls=%async_computation.4 | async-start | bytes 262144 | tf_op jit(solution)/shard_map/all_to_all | solution.py:227
  204.7 7.6 %all-to-all-done.4 = f32[32,2,512]{2,1,0:T(2,128)S(1)} async-done(((f32[32,2,512]{2,1,0:T(2,128)}), f32[32,2,512]{2,1,0:T(2,128)S(1)}, u32[]{:S(2)}, u32[]{:S(2)}) %all-to-all-start.4) | async-done | bytes 131104 | tf_op jit(solution)/shard_map/all_to_all | solution.py:227
  212.7 0.6 broadcast_in_dim.106
  213.3 7.2 %all-to-all-start.5 = ((f32[16,1,128]{2,1,0:T(1,128)}), f32[16,1,128]{2,1,0:T(1,128)S(1)}, u32[]{:S(2)}, u32[]{:S(2)}) async-start(f32[16,1,128]{2,1,0:T(1,128)} %broadcast_in_dim.106), calls=%async_computation.5 | async-start | bytes 16384 | tf_op jit(solution)/shard_map/all_to_all | solution.py:227
  220.6 0.5 fusion.6
  221.1 10.8 %all-to-all-done.5 = f32[16,1,128]{2,1,0:T(1,128)S(1)} async-done(((f32[16,1,128]{2,1,0:T(1,128)}), f32[16,1,128]{2,1,0:T(1,128)S(1)}, u32[]{:S(2)}, u32[]{:S(2)}) %all-to-all-start.5) | async-done | bytes 8224 | tf_op jit(solution)/shard_map/all_to_all | solution.py:227
  232.1 0.5 broadcast_multiply_fusion
  (70 shorter events, 3.0 us)
Async XLA Ops:
  7.2 32.7 %copy-start = (s32[16]{0:T(128)S(1)}, s32[16]{0:T(128)}, u32[]{:S(2)}) copy-start(s32[16]{0:T(128)} %param.33) | copy-start | bytes 196
  7.2 38.2 %copy-start.8 = (s32[64]{0:T(128)S(1)}, s32[64]{0:T(128)}, u32[]{:S(2)}) copy-start(s32[64]{0:T(128)} %param.32) | copy-start | bytes 772
  7.2 83.2 %copy-start.5 = (f32[512]{0:T(512)S(1)}, f32[512]{0:T(512)}, u32[]{:S(2)}) copy-start(f32[512]{0:T(512)} %param.24) | copy-start | bytes 6148
  7.2 83.2 %copy-start.2 = (bf16[128,512]{1,0:T(8,128)(2,1)S(1)}, bf16[128,512]{1,0:T(8,128)(2,1)}, u32[]{:S(2)}) copy-start(bf16[128,512]{1,0:T(8,128)(2,1)} %g_ref.1) | copy-start | bytes 393220
  7.2 99.2 %all-gather.4.cloned.1.call-start = ((), (), s32[]{:S(2)}) async-start(), calls=%async_computation.6 | async-start | bytes 3342336 | tf_op jit(solution)/shard_map/all_gather | solution.py:283
  13.5 44.7 %all-to-all-start = ((f32[64,8,128]{2,1,0:T(8,128)}), f32[64,8,128]{2,1,0:T(8,128)S(1)}, u32[]{:S(2)}, u32[]{:S(2)}) async-start(f32[64,8,128]{2,1,0:T(8,128)} %shard_map.176), calls=%async_computation | async-start | bytes 524288 | tf_op jit(solution)/shard_map/all_to_all | solution.py:297
  32.6 154.6 %all-gather.6.cloned.1.call-start = ((), (), s32[]{:S(2)}) async-start(), calls=%async_computation.7 | async-start | bytes 6684672 | tf_op jit(solution)/shard_map/all_gather | solution.py:342
  34.7 10.9 %collective-permute-start = (f32[1,128]{1,0:T(1,128)S(1)}, f32[1,128]{1,0:T(1,128)S(1)}, u32[]{:S(2)}, u32[]{:S(2)}) collective-permute-start(f32[1,128]{1,0:T(1,128)S(1)} %get-tuple-element.49), channel_id=1, source_target_pairs={{0,1},{1,0},{2,3},{3,2},{4,5},{5,4},{6,7},{7,6},{8,9},{9,8},{10,11... | collective-permute-start | bytes 1544 | tf_op jit(solution)/shard_map/ppermute | solution.py:240
  45.6 12.5 %collective-permute-start.1 = (f32[2,1,128]{2,0,1:T(2,128)S(1)}, f32[2,1,128]{2,0,1:T(2,128)S(1)}, u32[]{:S(2)}, u32[]{:S(2)}) collective-permute-start(f32[2,1,128]{2,0,1:T(2,128)S(1)} %dynamic_update_slice.34), channel_id=1, source_target_pairs={{0,2},{2,4},{4,6},{6,0},{1,3},{3,5},{5,7},{7,1},{8,10},{10,12},{12... | collective-permute-start | bytes 3080 | tf_op jit(solution)/shard_map/ppermute | solution.py:240
  48.8 9.3 %collective-permute-start.2 = (f32[2,1,128]{2,0,1:T(2,128)S(1)}, f32[2,1,128]{2,0,1:T(2,128)S(1)}, u32[]{:S(2)}, u32[]{:S(2)}) collective-permute-start(f32[2,1,128]{2,0,1:T(2,128)S(1)} %dynamic_update_slice.34), channel_id=1, source_target_pairs={{0,4},{2,6},{4,0},{6,2},{1,5},{3,7},{5,1},{7,3},{8,12},{10,14},{12... | collective-permute-start | bytes 3080 | tf_op jit(solution)/shard_map/ppermute | solution.py:240
  53.3 4.8 %collective-permute-start.3 = (f32[2,1,128]{2,0,1:T(2,128)S(1)}, f32[2,1,128]{2,0,1:T(2,128)S(1)}, u32[]{:S(2)}, u32[]{:S(2)}) collective-permute-start(f32[2,1,128]{2,0,1:T(2,128)S(1)} %dynamic_update_slice.34), channel_id=1, source_target_pairs={{0,6},{2,0},{4,2},{6,4},{1,7},{3,1},{5,3},{7,5},{8,14},{10,8},{12,... | collective-permute-start | bytes 3080 | tf_op jit(solution)/shard_map/ppermute | solution.py:240
  59.7 30.7 %all-to-all-start.1 = ((f32[64,4,128]{2,1,0:T(4,128)}), f32[64,4,128]{2,1,0:T(4,128)S(1)}, u32[]{:S(2)}, u32[]{:S(2)}) async-start(f32[64,4,128]{2,1,0:T(4,128)} %shard_map.178), calls=%async_computation.1 | async-start | bytes 262144 | tf_op jit(solution)/shard_map/all_to_all | solution.py:352
  90.4 1.0 copy-start.1
  91.4 0.9 copy-start.3
  92.3 0.9 copy-start.4
  108.4 32.0 %copy-start.6 = (bf16[16,4096]{1,0:T(8,128)(2,1)S(1)}, bf16[16,4096]{1,0:T(8,128)(2,1)}, u32[]{:S(2)}) copy-start(bf16[16,4096]{1,0:T(8,128)(2,1)} %param.26) | copy-start | bytes 393220
  108.4 32.4 %copy-start.7 = (f32[4096]{0:T(1024)S(1)}, f32[4096]{0:T(1024)}, u32[]{:S(2)}) copy-start(f32[4096]{0:T(1024)} %param.25) | copy-start | bytes 49156
  108.5 9.7 %collective-permute-start.4 = (f32[256,1024]{1,0:T(8,128)S(1)}, f32[256,1024]{1,0:T(8,128)S(1)}, u32[]{:S(2)}, u32[]{:S(2)}) collective-permute-start(f32[256,1024]{1,0:T(8,128)S(1)} %get-tuple-element.37), channel_id=1, source_target_pairs={{0,1},{1,0},{2,3},{3,2},{4,5},{5,4},{6,7},{7,6},{8,9},{9,8},{10,11... | collective-permute-start | bytes 3145736 | tf_op jit(solution)/shard_map/ppermute | solution.py:221
  119.2 21.1 %all-to-all-start.2 = ((f32[16,16,1024]{2,1,0:T(8,128)}), f32[16,16,1024]{2,1,0:T(8,128)S(1)}, u32[]{:S(2)}, u32[]{:S(2)}) async-start(f32[16,16,1024]{2,1,0:T(8,128)} %bitcast.27), calls=%async_computation.2 | async-start | bytes 2097152 | tf_op jit(solution)/shard_map/all_to_all | solution.py:387
  124.1 14.0 %collective-permute-start.5 = (f32[4,2,1,128]{3,1,0,2:T(2,128)S(1)}, f32[4,2,1,128]{3,1,0,2:T(2,128)S(1)}, u32[]{:S(2)}, u32[]{:S(2)}) collective-permute-start(f32[4,2,1,128]{3,1,0,2:T(2,128)S(1)} %constant_dynamic-update-slice_fusion), channel_id=1, source_target_pairs={{0,128},{128,256},{256,384},{384,0},{1,129},{129,257},{257,385},{3... | collective-permute-start | bytes 12296 | tf_op jit(solution)/shard_map/ppermute | solution.py:240
  127.3 11.2 %collective-permute-start.6 = (f32[4,2,1,128]{3,1,0,2:T(2,128)S(1)}, f32[4,2,1,128]{3,1,0,2:T(2,128)S(1)}, u32[]{:S(2)}, u32[]{:S(2)}) collective-permute-start(f32[4,2,1,128]{3,1,0,2:T(2,128)S(1)} %constant_dynamic-update-slice_fusion), channel_id=1, source_target_pairs={{0,256},{128,384},{256,0},{384,128},{1,257},{129,385},{257,1},{385... | collective-permute-start | bytes 12296 | tf_op jit(solution)/shard_map/ppermute | solution.py:240
  131.6 6.9 %collective-permute-start.7 = (f32[4,2,1,128]{3,1,0,2:T(2,128)S(1)}, f32[4,2,1,128]{3,1,0,2:T(2,128)S(1)}, u32[]{:S(2)}, u32[]{:S(2)}) collective-permute-start(f32[4,2,1,128]{3,1,0,2:T(2,128)S(1)} %constant_dynamic-update-slice_fusion), channel_id=1, source_target_pairs={{0,384},{128,0},{256,128},{384,256},{1,385},{129,1},{257,129},{385... | collective-permute-start | bytes 12296 | tf_op jit(solution)/shard_map/ppermute | solution.py:240
  173.2 7.6 %collective-permute-start.8 = (bf16[256,4096]{1,0:T(8,128)(2,1)S(1)}, bf16[256,4096]{1,0:T(8,128)(2,1)}, u32[]{:S(2)}, u32[]{:S(2)}) collective-permute-start(bf16[256,4096]{1,0:T(8,128)(2,1)S(1)} %bitcast.97), channel_id=1, source_target_pairs={{0,1},{1,0},{2,3},{3,2},{4,5},{5,4},{6,7},{7,6},{8,9},{9,8},{10,11... | collective-permute-start | bytes 6291464 | tf_op jit(solution)/shard_map/ppermute | solution.py:221
  194.6 17.7 %all-to-all-start.4 = ((f32[32,2,512]{2,1,0:T(2,128)}), f32[32,2,512]{2,1,0:T(2,128)S(1)}, u32[]{:S(2)}, u32[]{:S(2)}) async-start(f32[32,2,512]{2,1,0:T(2,128)} %broadcast_in_dim.105), calls=%async_computation.4 | async-start | bytes 262144 | tf_op jit(solution)/shard_map/all_to_all | solution.py:227
  213.3 18.6 %all-to-all-start.5 = ((f32[16,1,128]{2,1,0:T(1,128)}), f32[16,1,128]{2,1,0:T(1,128)S(1)}, u32[]{:S(2)}, u32[]{:S(2)}) async-start(f32[16,1,128]{2,1,0:T(1,128)} %broadcast_in_dim.106), calls=%async_computation.5 | async-start | bytes 16384 | tf_op jit(solution)/shard_map/all_to_all | solution.py:227
Sparse Core Ops, SparseCore 0:
  10.1 87.5 all-gather.3
  99.8 87.3 all-gather.5

commit v5 on v4

--- a/solution.py
+++ b/solution.py
@@ -275,7 +275,7 @@
     own_columns = closing_projection.shape[1]
     fold = embed // width
     held = own_columns // fold
-    early = share // 4
+    early = share * 3 // 8
     block = closing_projection.T.reshape(fold, held, width).transpose(1, 0, 2).reshape(held, embed)
     rows_1 = jnp.concatenate(
         [block, lax.dynamic_slice_in_dim(vocabulary_readout, head * share, early)], axis=0
@@ -311,10 +311,6 @@
     )
     plane = nx * ny * nc
     facts = jnp.pad(facts, (0, LANES - 3 * own)).reshape(1, LANES)
-    facts = spread(facts, "c", [list(range(nc))])
-    vocabulary, facts = lax.optimization_barrier((vocabulary_readout, facts))
-    rows_2 = lax.dynamic_slice_in_dim(vocabulary, head * share + early, share - early)
-    facts = spread(facts, "y", [list(range(ny))])
     row = pl.BlockSpec((1, LANES), lambda p: (0, p))
     within, high, low = pl.pallas_call(
         within_kernel,
@@ -336,6 +332,8 @@
         (prompts, 1, 2, chunk_rows, CHAN),
     )[:, 0]
     prompt = prompt.transpose(0, 2, 1, 3).reshape(prompts, chunk_rows, LANES).astype(F32)
+    vocabulary, within = lax.optimization_barrier((vocabulary_readout, within))
+    rows_2 = lax.dynamic_slice_in_dim(vocabulary, head * share + early, share - early)
     moved, within, high, low, facts, rows_2, meta, prompt = lax.optimization_barrier(
         (moved, within, high, low, facts, rows_2, meta, prompt)
     )
@@ -349,7 +347,11 @@
         compiler_params=limit(4),
         cost_estimate=cost(1_000_000, 500_000),
     )(meta, moved, prompt)
+    facts, _ = lax.optimization_barrier((facts, entering))
     entering = lax.all_to_all(entering, ("x", "z"), 0, 0, tiled=True)
+    facts = spread(facts, "c", [list(range(nc))])
+    facts = spread(facts, "y", [list(range(ny))])
+    entering, facts = lax.optimization_barrier((entering, facts))
     entering = entering.reshape(pairs * CHAN, LANES)
 
     mixed = pl.pallas_call(
@@ -422,7 +424,7 @@
         )(place, tokens, other, labels, in_hbm(vocab), *([] if first else [known]))
 
     known = score(gathered_1, (held + early, held, 0, vocab_local), gathered_1.shape[0])
-    late = gathered_2.shape[0] // 3
+    late = gathered_2.shape[0] // 2
     both = score(gathered_2, (share - early, 0, early, vocab_local), late, known)
     both = copies(both, ("x", "y", "c"))
     part, picked = both[:, 0], both[:, 1]

time: 241 us -> 239 us (level)
  starting transfers between devices: 91.2 us -> 87.7 us
    all_to_all x1, waiting for transfers between devices: 15.8 us -> 4.48 us  [per_device(): entering = lax.all_to_all(entering, ('x', 'z'), 0, 0, tiled=True)]
    all_to_all x1, waiting for transfers between devices: 0.01 us -> 11.2 us  [per_device(): moved = lax.all_to_all(end, ('x', 'z'), 0, 0, tiled=True)]
    all_to_all x1, starting transfers between devices: 14.8 us -> 6.02 us  [per_device(): entering = lax.all_to_all(entering, ('x', 'z'), 0, 0, tiled=True)]
    ppermute x2, starting transfers between devices: 11.1 us -> 14.6 us  [shifted(): lax.ppermute(value, axis, [(i, (i + steps) % count) for i in range(count)])]
  transfers between devices with their start and end apart: 16 -> 16, of which waited for: 9 -> 11; matrix products, arithmetic and copies ran while one was open for 4% -> 4% of each run, Pallas kernels for 8% -> 8%
where the time goes in v5:
time: 239 us; the launch traced here: 237 us
  starting transfers between devices  87.7 us (37%)
  waiting for transfers between devices  47.9 us (20%)
  blocking collectives  44 us (18%)
  Pallas kernels  25.4 us (11%)
  between operations  14.7 us (6%)
  local copies, waits for them, and re-layouts  10.4 us (4%)
  other arithmetic  7.11 us (3%)
    all_to_all x1, blocking collectives, copies(): return lax.all_to_all(sent, axes, 0, 0, tiled=True)  32 us
    ppermute x7, starting transfers between devices, spread(): piece = lax.ppermute(value, axis, pairs) if step else value  25.4 us
    all_to_all x1, starting transfers between devices, per_device(): moved = lax.all_to_all(end, ('x', 'z'), 0, 0, tiled=True)  19.1 us
    all_to_all x2, waiting for transfers between devices, copies(): return lax.all_to_all(sent, axes, 0, 0, tiled=True)  18.4 us
    all_to_all x2, starting transfers between devices, copies(): return lax.all_to_all(sent, axes, 0, 0, tiled=True)  16.3 us
    ppermute x2, starting transfers between devices, shifted(): lax.ppermute(value, axis, [(i, (i + steps) % count) for i in range(count)])  14.6 us
    all_gather x1, blocking collectives, per_device(): mixed = lax.all_gather(mixed, 'x', axis=0)  12 us
    pallas_call x2, Pallas kernels, score(): pl.pallas_call(functools.partial(score_kernel, layout, first, not first),...  11.4 us
  transfers between devices with their start and end apart: 16, of which 11 were waited for; matrix products, arithmetic and copies ran while one was open for 4% of the time, Pallas kernels for 8%

profile of v5, /device:TPU:1, one launch (start us, length us, event | category | flops | bytes accessed | tf_op | source)
XLA Modules:
  0.0 237.2 jit_solution(12769602134604258766)
XLA Ops:
  7.3 1.0 constant_dynamic-slice_fusion.1
  8.2 1.6 pad_maximum_fusion
  9.8 3.7 %shard_map.176 = f32[64,8,128]{2,1,0:T(8,128)} custom-call(bf16[128,512]{1,0:T(8,128)(2,1)} %k_ref.3, bf16[128,512]{1,0:T(8,128)(2,1)} %v_ref.3, bf16[128,512]{1,0:T(8,128)(2,1)} %w_ref.3), custom_call_target="tpu_custom_call" | custom-call | flops 80000000 | bytes 393216 | tf_op jit(solution)/shard_map/pallas_call | solution.py:288
  13.6 19.1 %all-to-all-start = ((f32[64,8,128]{2,1,0:T(8,128)}), f32[64,8,128]{2,1,0:T(8,128)S(1)}, u32[]{:S(2)}, u32[]{:S(2)}) async-start(f32[64,8,128]{2,1,0:T(8,128)} %shard_map.176), calls=%async_computation | async-start | bytes 524288 | tf_op jit(solution)/shard_map/all_to_all | solution.py:297
  32.8 1.1 reshape.87
  34.2 0.7 convert_element_type.35
  34.9 0.7 convert_element_type.36
  35.5 0.7 pad_maximum_fusion.1
  36.3 0.7 compare_select_fusion
  36.9 4.8 %shard_map.177 = (f32[128,512]{1,0:T(8,128)}, bf16[128,512]{1,0:T(8,128)(2,1)}, bf16[128,512]{1,0:T(8,128)(2,1)}) custom-call(bf16[128,512]{1,0:T(8,128)(2,1)} %r_ref.1, bf16[128,512]{1,0:T(8,128)(2,1)} %k_ref.3, bf16[128,512]{1,0:T(8,128)(2,1)} %v_ref.3, bf16[128,512]{1,0:T(8,128)(2,1)} %w_ref.3, f32[1,512]{1,0:T(1,128)} %bitcast.119), custom_call_target="tpu_custom_call" | custom-call | flops 240000000 | bytes 1048576 | tf_op jit(solution)/shard_map/pallas_call | solution.py:315
  41.7 0.8 gather_fusion
  42.6 1.7 constant_dynamic-slice_fusion.3
  44.3 11.2 %all-to-all-done.moved_ref = f32[64,8,128]{2,1,0:T(8,128)S(1)} async-done(((f32[64,8,128]{2,1,0:T(8,128)}), f32[64,8,128]{2,1,0:T(8,128)S(1)}, u32[]{:S(2)}, u32[]{:S(2)}) %all-to-all-start) | async-done | bytes 262176 | tf_op jit(solution)/shard_map/all_to_all | solution.py:297
  55.8 1.5 shard_map.178
  57.3 4.2 %collective-permute-start = (f32[1,128]{1,0:T(1,128)S(1)}, f32[1,128]{1,0:T(1,128)S(1)}, u32[]{:S(2)}, u32[]{:S(2)}) collective-permute-start(f32[1,128]{1,0:T(1,128)S(1)} %pad_bitcast_fusion), channel_id=1, source_target_pairs={{0,1},{1,0},{2,3},{3,2},{4,5},{5,4},{6,7},{7,6},{8,9},{9,8},{10,11... | collective-permute-start | bytes 1544 | tf_op jit(solution)/shard_map/ppermute | solution.py:240
  61.5 6.0 %all-to-all-start.1 = ((f32[64,4,128]{2,1,0:T(4,128)}), f32[64,4,128]{2,1,0:T(4,128)S(1)}, u32[]{:S(2)}, u32[]{:S(2)}) async-start(f32[64,4,128]{2,1,0:T(4,128)} %shard_map.178), calls=%async_computation.1 | async-start | bytes 262144 | tf_op jit(solution)/shard_map/all_to_all | solution.py:351
  67.6 3.2 %collective-permute-start.1 = (f32[2,1,128]{2,0,1:T(2,128)S(1)}, f32[2,1,128]{2,0,1:T(2,128)S(1)}, u32[]{:S(2)}, u32[]{:S(2)}) collective-permute-start(f32[2,1,128]{2,0,1:T(2,128)S(1)} %dynamic_update_slice.34), channel_id=1, source_target_pairs={{0,2},{2,4},{4,6},{6,0},{1,3},{3,5},{5,7},{7,1},{8,10},{10,12},{12... | collective-permute-start | bytes 3080 | tf_op jit(solution)/shard_map/ppermute | solution.py:240
  70.8 4.5 %collective-permute-start.2 = (f32[2,1,128]{2,0,1:T(2,128)S(1)}, f32[2,1,128]{2,0,1:T(2,128)S(1)}, u32[]{:S(2)}, u32[]{:S(2)}) collective-permute-start(f32[2,1,128]{2,0,1:T(2,128)S(1)} %dynamic_update_slice.34), channel_id=1, source_target_pairs={{0,4},{2,6},{4,0},{6,2},{1,5},{3,7},{5,1},{7,3},{8,12},{10,14},{12... | collective-permute-start | bytes 3080 | tf_op jit(solution)/shard_map/ppermute | solution.py:240
  75.3 3.0 %collective-permute-start.3 = (f32[2,1,128]{2,0,1:T(2,128)S(1)}, f32[2,1,128]{2,0,1:T(2,128)S(1)}, u32[]{:S(2)}, u32[]{:S(2)}) collective-permute-start(f32[2,1,128]{2,0,1:T(2,128)S(1)} %dynamic_update_slice.34), channel_id=1, source_target_pairs={{0,6},{2,0},{4,2},{6,4},{1,7},{3,1},{5,3},{7,5},{8,14},{10,8},{12,... | collective-permute-start | bytes 3080 | tf_op jit(solution)/shard_map/ppermute | solution.py:240
  78.4 1.6 collective-permute-done.3
  80.0 4.5 %all-to-all-done.1 = f32[64,4,128]{2,1,0:T(4,128)S(1)} async-done(((f32[64,4,128]{2,1,0:T(4,128)}), f32[64,4,128]{2,1,0:T(4,128)S(1)}, u32[]{:S(2)}, u32[]{:S(2)}) %all-to-all-start.1) | async-done | bytes 131104 | tf_op jit(solution)/shard_map/all_to_all | solution.py:351
  84.5 1.0 copy-done.1
  85.4 0.9 copy-done.3
  86.3 0.9 copy-done.4
  87.2 2.0 shard_map.179
  89.3 12.0 %all-gather = bf16[512,512]{1,0:T(8,128)(2,1)S(1)} all-gather(bf16[128,512]{1,0:T(8,128)(2,1)S(1)} %shard_map.179), channel_id=2, replica_groups=mesh['x'=4,'z'=16,'y'=4,'c'=2] {'x'}, dimensions={0}, use_global_device_ids=true | all-gather | bytes 655360 | tf_op jit(solution)/shard_map/all_gather | solution.py:367
  101.3 0.6 all-gather.4.cloned.1.call-done.vocab_ref
  102.0 2.0 shard_map.180
  104.0 10.9 %collective-permute-start.4 = (f32[256,1024]{1,0:T(8,128)S(1)}, f32[256,1024]{1,0:T(8,128)S(1)}, u32[]{:S(2)}, u32[]{:S(2)}) collective-permute-start(f32[256,1024]{1,0:T(8,128)S(1)} %get-tuple-element.43), channel_id=1, source_target_pairs={{0,1},{1,0},{2,3},{3,2},{4,5},{5,4},{6,7},{7,6},{8,9},{9,8},{10,11... | collective-permute-start | bytes 3145736 | tf_op jit(solution)/shard_map/ppermute | solution.py:221
  114.8 2.3 collective-permute-done.4
  117.1 1.1 add.175
  118.2 6.1 %all-to-all-start.2 = ((f32[16,16,1024]{2,1,0:T(8,128)}), f32[16,16,1024]{2,1,0:T(8,128)S(1)}, u32[]{:S(2)}, u32[]{:S(2)}) async-start(f32[16,16,1024]{2,1,0:T(8,128)} %bitcast.27), calls=%async_computation.2 | async-start | bytes 2097152 | tf_op jit(solution)/shard_map/all_to_all | solution.py:389
  124.4 3.2 %collective-permute-start.5 = (f32[4,2,1,128]{3,1,0,2:T(2,128)S(1)}, f32[4,2,1,128]{3,1,0,2:T(2,128)S(1)}, u32[]{:S(2)}, u32[]{:S(2)}) collective-permute-start(f32[4,2,1,128]{3,1,0,2:T(2,128)S(1)} %constant_dynamic-update-slice_fusion), channel_id=1, source_target_pairs={{0,128},{128,256},{256,384},{384,0},{1,129},{129,257},{257,385},{3... | collective-permute-start | bytes 12296 | tf_op jit(solution)/shard_map/ppermute | solution.py:240
  127.6 4.3 %collective-permute-start.6 = (f32[4,2,1,128]{3,1,0,2:T(2,128)S(1)}, f32[4,2,1,128]{3,1,0,2:T(2,128)S(1)}, u32[]{:S(2)}, u32[]{:S(2)}) collective-permute-start(f32[4,2,1,128]{3,1,0,2:T(2,128)S(1)} %constant_dynamic-update-slice_fusion), channel_id=1, source_target_pairs={{0,256},{128,384},{256,0},{384,128},{1,257},{129,385},{257,1},{385... | collective-permute-start | bytes 12296 | tf_op jit(solution)/shard_map/ppermute | solution.py:240
  131.9 3.1 %collective-permute-start.7 = (f32[4,2,1,128]{3,1,0,2:T(2,128)S(1)}, f32[4,2,1,128]{3,1,0,2:T(2,128)S(1)}, u32[]{:S(2)}, u32[]{:S(2)}) collective-permute-start(f32[4,2,1,128]{3,1,0,2:T(2,128)S(1)} %constant_dynamic-update-slice_fusion), channel_id=1, source_target_pairs={{0,384},{128,0},{256,128},{384,256},{1,385},{129,1},{257,129},{385... | collective-permute-start | bytes 12296 | tf_op jit(solution)/shard_map/ppermute | solution.py:240
  135.0 3.3 %collective-permute-done.5 = f32[4,2,1,128]{3,1,0,2:T(2,128)S(1)} collective-permute-done((f32[4,2,1,128]{3,1,0,2:T(2,128)S(1)}, f32[4,2,1,128]{3,1,0,2:T(2,128)S(1)}, u32[]{:S(2)}, u32[]{:S(2)}) %collective-permute-start.5) | collective-permute-done | bytes 4128 | tf_op jit(solution)/shard_map/ppermute | solution.py:240
  138.8 1.8 all-to-all-done.2
  141.5 32.0 %all_to_all.30 = bf16[16,16,4096]{2,1,0:T(8,128)(2,1)S(1)} all-to-all(bf16[16,16,4096]{2,1,0:T(8,128)(2,1)S(1)} %broadcast_in_dim.104), channel_id=1, replica_groups=mesh['x'=4,'z'=16,'y'=4,'c'=2] {'y','x'}, dimensions={0} | all-to-all | bytes 4194304 | tf_op jit(solution)/shard_map/all_to_all | solution.py:227
  173.5 3.7 %collective-permute-start.8 = (bf16[256,4096]{1,0:T(8,128)(2,1)S(1)}, bf16[256,4096]{1,0:T(8,128)(2,1)}, u32[]{:S(2)}, u32[]{:S(2)}) collective-permute-start(bf16[256,4096]{1,0:T(8,128)(2,1)S(1)} %bitcast.96), channel_id=1, source_target_pairs={{0,1},{1,0},{2,3},{3,2},{4,5},{5,4},{6,7},{7,6},{8,9},{9,8},{10,11... | collective-permute-start | bytes 6291464 | tf_op jit(solution)/shard_map/ppermute | solution.py:221
  177.5 3.6 %collective-permute-done.8.theirs_ref = bf16[256,4096]{1,0:T(8,128)(2,1)} collective-permute-done((bf16[256,4096]{1,0:T(8,128)(2,1)S(1)}, bf16[256,4096]{1,0:T(8,128)(2,1)}, u32[]{:S(2)}, u32[]{:S(2)}) %collective-permute-start.8) | collective-permute-done | bytes 2097184 | tf_op jit(solution)/shard_map/ppermute | solution.py:221
  181.1 5.5 %shard_map.181.refs_0_ = f32[3,512]{1,0:T(4,128)S(1)} custom-call(s32[2]{0:T(128)S(1)} %pad_add_fusion.1.place_ref, bf16[256,4096]{1,0:T(8,128)(2,1)S(1)} %bitcast.97, bf16[256,4096]{1,0:T(8,128)(2,1)} %collective-permute-done.8.theirs_ref, s32[1,512]{1,0:T(1,128)S(1)} %convert_element_type.43.label_ref, bf16[512,4096]{1,0:T(8,128)(2,1)} %all-gather.4.cloned.1.call-done.vocab_ref), custom_call_target="tpu_custom_call" | custom-call | flops 2147483648 | bytes 8388608 | tf_op jit(solution)/shard_map/pallas_call | solution.py:406
  186.6 5.9 %shard_map.182 = f32[2,512]{1,0:T(2,128)S(1)} custom-call(s32[2]{0:T(128)S(1)} %pad_add_fusion.1.place_ref, bf16[256,4096]{1,0:T(8,128)(2,1)S(1)} %bitcast.98, bf16[256,4096]{1,0:T(8,128)(2,1)} %collective-permute-done.8.theirs_ref, s32[1,512]{1,0:T(1,128)S(1)} %convert_element_type.43.label_ref, bf16[640,4096]{1,0:T(8,128)(2,1)} %all-gather.6.cloned.1.call-done.vocab_ref, ...), custom_call_target="tpu_custom_call" | custom-call | flops 2684354560 | bytes 9437184 | tf_op jit(solution)/shard_map/pallas_call | solution.py:406
  192.6 0.7 broadcast_in_dim.105
  193.3 9.8 %all-to-all-start.4 = ((f32[32,2,512]{2,1,0:T(2,128)}), f32[32,2,512]{2,1,0:T(2,128)S(1)}, u32[]{:S(2)}, u32[]{:S(2)}) async-start(f32[32,2,512]{2,1,0:T(2,128)} %broadcast_in_dim.105), calls=%async_computation.4 | async-start | bytes 262144 | tf_op jit(solution)/shard_map/all_to_all | solution.py:227
  203.1 7.6 %all-to-all-done.4 = f32[32,2,512]{2,1,0:T(2,128)S(1)} async-done(((f32[32,2,512]{2,1,0:T(2,128)}), f32[32,2,512]{2,1,0:T(2,128)S(1)}, u32[]{:S(2)}, u32[]{:S(2)}) %all-to-all-start.4) | async-done | bytes 131104 | tf_op jit(solution)/shard_map/all_to_all | solution.py:227
  211.2 0.6 broadcast_in_dim.106
  211.8 6.6 %all-to-all-start.5 = ((f32[16,1,128]{2,1,0:T(1,128)}), f32[16,1,128]{2,1,0:T(1,128)S(1)}, u32[]{:S(2)}, u32[]{:S(2)}) async-start(f32[16,1,128]{2,1,0:T(1,128)} %broadcast_in_dim.106), calls=%async_computation.5 | async-start | bytes 16384 | tf_op jit(solution)/shard_map/all_to_all | solution.py:227
  218.8 10.8 %all-to-all-done.5 = f32[16,1,128]{2,1,0:T(1,128)S(1)} async-done(((f32[16,1,128]{2,1,0:T(1,128)}), f32[16,1,128]{2,1,0:T(1,128)S(1)}, u32[]{:S(2)}, u32[]{:S(2)}) %all-to-all-start.5) | async-done | bytes 8224 | tf_op jit(solution)/shard_map/all_to_all | solution.py:227
  (70 shorter events, 4.1 us)
Async XLA Ops:
  7.2 34.5 %copy-start = (s32[16]{0:T(128)S(1)}, s32[16]{0:T(128)}, u32[]{:S(2)}) copy-start(s32[16]{0:T(128)} %param.33) | copy-start | bytes 196
  7.2 35.3 %copy-start.8 = (s32[64]{0:T(128)S(1)}, s32[64]{0:T(128)}, u32[]{:S(2)}) copy-start(s32[64]{0:T(128)} %param.32) | copy-start | bytes 772
  7.2 77.3 %copy-start.5 = (f32[512]{0:T(512)S(1)}, f32[512]{0:T(512)}, u32[]{:S(2)}) copy-start(f32[512]{0:T(512)} %param.24) | copy-start | bytes 6148
  7.2 77.3 %copy-start.2 = (bf16[128,512]{1,0:T(8,128)(2,1)S(1)}, bf16[128,512]{1,0:T(8,128)(2,1)}, u32[]{:S(2)}) copy-start(bf16[128,512]{1,0:T(8,128)(2,1)} %g_ref.1) | copy-start | bytes 393220
  7.2 94.7 %all-gather.4.cloned.1.call-start = ((), (), s32[]{:S(2)}) async-start(), calls=%async_computation.6 | async-start | bytes 4456448 | tf_op jit(solution)/shard_map/all_gather | solution.py:283
  13.6 42.0 %all-to-all-start = ((f32[64,8,128]{2,1,0:T(8,128)}), f32[64,8,128]{2,1,0:T(8,128)S(1)}, u32[]{:S(2)}, u32[]{:S(2)}) async-start(f32[64,8,128]{2,1,0:T(8,128)} %shard_map.176), calls=%async_computation | async-start | bytes 524288 | tf_op jit(solution)/shard_map/all_to_all | solution.py:297
  32.7 153.9 %all-gather.6.cloned.1.call-start = ((), (), s32[]{:S(2)}) async-start(), calls=%async_computation.7 | async-start | bytes 5570560 | tf_op jit(solution)/shard_map/all_gather | solution.py:340
  57.3 10.3 %collective-permute-start = (f32[1,128]{1,0:T(1,128)S(1)}, f32[1,128]{1,0:T(1,128)S(1)}, u32[]{:S(2)}, u32[]{:S(2)}) collective-permute-start(f32[1,128]{1,0:T(1,128)S(1)} %pad_bitcast_fusion), channel_id=1, source_target_pairs={{0,1},{1,0},{2,3},{3,2},{4,5},{5,4},{6,7},{7,6},{8,9},{9,8},{10,11... | collective-permute-start | bytes 1544 | tf_op jit(solution)/shard_map/ppermute | solution.py:240
  61.5 23.0 %all-to-all-start.1 = ((f32[64,4,128]{2,1,0:T(4,128)}), f32[64,4,128]{2,1,0:T(4,128)S(1)}, u32[]{:S(2)}, u32[]{:S(2)}) async-start(f32[64,4,128]{2,1,0:T(4,128)} %shard_map.178), calls=%async_computation.1 | async-start | bytes 262144 | tf_op jit(solution)/shard_map/all_to_all | solution.py:351
  67.6 10.7 %collective-permute-start.1 = (f32[2,1,128]{2,0,1:T(2,128)S(1)}, f32[2,1,128]{2,0,1:T(2,128)S(1)}, u32[]{:S(2)}, u32[]{:S(2)}) collective-permute-start(f32[2,1,128]{2,0,1:T(2,128)S(1)} %dynamic_update_slice.34), channel_id=1, source_target_pairs={{0,2},{2,4},{4,6},{6,0},{1,3},{3,5},{5,7},{7,1},{8,10},{10,12},{12... | collective-permute-start | bytes 3080 | tf_op jit(solution)/shard_map/ppermute | solution.py:240
  70.8 7.6 %collective-permute-start.2 = (f32[2,1,128]{2,0,1:T(2,128)S(1)}, f32[2,1,128]{2,0,1:T(2,128)S(1)}, u32[]{:S(2)}, u32[]{:S(2)}) collective-permute-start(f32[2,1,128]{2,0,1:T(2,128)S(1)} %dynamic_update_slice.34), channel_id=1, source_target_pairs={{0,4},{2,6},{4,0},{6,2},{1,5},{3,7},{5,1},{7,3},{8,12},{10,14},{12... | collective-permute-start | bytes 3080 | tf_op jit(solution)/shard_map/ppermute | solution.py:240
  75.3 4.7 %collective-permute-start.3 = (f32[2,1,128]{2,0,1:T(2,128)S(1)}, f32[2,1,128]{2,0,1:T(2,128)S(1)}, u32[]{:S(2)}, u32[]{:S(2)}) collective-permute-start(f32[2,1,128]{2,0,1:T(2,128)S(1)} %dynamic_update_slice.34), channel_id=1, source_target_pairs={{0,6},{2,0},{4,2},{6,4},{1,7},{3,1},{5,3},{7,5},{8,14},{10,8},{12,... | collective-permute-start | bytes 3080 | tf_op jit(solution)/shard_map/ppermute | solution.py:240
  84.5 1.0 copy-start.1
  85.4 0.9 copy-start.3
  86.3 0.9 copy-start.4
  103.9 36.8 %copy-start.6 = (bf16[16,4096]{1,0:T(8,128)(2,1)S(1)}, bf16[16,4096]{1,0:T(8,128)(2,1)}, u32[]{:S(2)}) copy-start(bf16[16,4096]{1,0:T(8,128)(2,1)} %param.26) | copy-start | bytes 393220
  103.9 37.2 %copy-start.7 = (f32[4096]{0:T(1024)S(1)}, f32[4096]{0:T(1024)}, u32[]{:S(2)}) copy-start(f32[4096]{0:T(1024)} %param.25) | copy-start | bytes 49156
  104.0 13.1 %collective-permute-start.4 = (f32[256,1024]{1,0:T(8,128)S(1)}, f32[256,1024]{1,0:T(8,128)S(1)}, u32[]{:S(2)}, u32[]{:S(2)}) collective-permute-start(f32[256,1024]{1,0:T(8,128)S(1)} %get-tuple-element.43), channel_id=1, source_target_pairs={{0,1},{1,0},{2,3},{3,2},{4,5},{5,4},{6,7},{7,6},{8,9},{9,8},{10,11... | collective-permute-start | bytes 3145736 | tf_op jit(solution)/shard_map/ppermute | solution.py:221
  118.2 22.5 %all-to-all-start.2 = ((f32[16,16,1024]{2,1,0:T(8,128)}), f32[16,16,1024]{2,1,0:T(8,128)S(1)}, u32[]{:S(2)}, u32[]{:S(2)}) async-start(f32[16,16,1024]{2,1,0:T(8,128)} %bitcast.27), calls=%async_computation.2 | async-start | bytes 2097152 | tf_op jit(solution)/shard_map/all_to_all | solution.py:389
  124.4 14.0 %collective-permute-start.5 = (f32[4,2,1,128]{3,1,0,2:T(2,128)S(1)}, f32[4,2,1,128]{3,1,0,2:T(2,128)S(1)}, u32[]{:S(2)}, u32[]{:S(2)}) collective-permute-start(f32[4,2,1,128]{3,1,0,2:T(2,128)S(1)} %constant_dynamic-update-slice_fusion), channel_id=1, source_target_pairs={{0,128},{128,256},{256,384},{384,0},{1,129},{129,257},{257,385},{3... | collective-permute-start | bytes 12296 | tf_op jit(solution)/shard_map/ppermute | solution.py:240
  127.6 11.2 %collective-permute-start.6 = (f32[4,2,1,128]{3,1,0,2:T(2,128)S(1)}, f32[4,2,1,128]{3,1,0,2:T(2,128)S(1)}, u32[]{:S(2)}, u32[]{:S(2)}) collective-permute-start(f32[4,2,1,128]{3,1,0,2:T(2,128)S(1)} %constant_dynamic-update-slice_fusion), channel_id=1, source_target_pairs={{0,256},{128,384},{256,0},{384,128},{1,257},{129,385},{257,1},{385... | collective-permute-start | bytes 12296 | tf_op jit(solution)/shard_map/ppermute | solution.py:240
  131.9 6.9 %collective-permute-start.7 = (f32[4,2,1,128]{3,1,0,2:T(2,128)S(1)}, f32[4,2,1,128]{3,1,0,2:T(2,128)S(1)}, u32[]{:S(2)}, u32[]{:S(2)}) collective-permute-start(f32[4,2,1,128]{3,1,0,2:T(2,128)S(1)} %constant_dynamic-update-slice_fusion), channel_id=1, source_target_pairs={{0,384},{128,0},{256,128},{384,256},{1,385},{129,1},{257,129},{385... | collective-permute-start | bytes 12296 | tf_op jit(solution)/shard_map/ppermute | solution.py:240
  173.5 7.6 %collective-permute-start.8 = (bf16[256,4096]{1,0:T(8,128)(2,1)S(1)}, bf16[256,4096]{1,0:T(8,128)(2,1)}, u32[]{:S(2)}, u32[]{:S(2)}) collective-permute-start(bf16[256,4096]{1,0:T(8,128)(2,1)S(1)} %bitcast.96), channel_id=1, source_target_pairs={{0,1},{1,0},{2,3},{3,2},{4,5},{5,4},{6,7},{7,6},{8,9},{9,8},{10,11... | collective-permute-start | bytes 6291464 | tf_op jit(solution)/shard_map/ppermute | solution.py:221
  193.3 17.5 %all-to-all-start.4 = ((f32[32,2,512]{2,1,0:T(2,128)}), f32[32,2,512]{2,1,0:T(2,128)S(1)}, u32[]{:S(2)}, u32[]{:S(2)}) async-start(f32[32,2,512]{2,1,0:T(2,128)} %broadcast_in_dim.105), calls=%async_computation.4 | async-start | bytes 262144 | tf_op jit(solution)/shard_map/all_to_all | solution.py:227
  211.8 17.8 %all-to-all-start.5 = ((f32[16,1,128]{2,1,0:T(1,128)}), f32[16,1,128]{2,1,0:T(1,128)S(1)}, u32[]{:S(2)}, u32[]{:S(2)}) async-start(f32[16,1,128]{2,1,0:T(1,128)} %broadcast_in_dim.106), calls=%async_computation.5 | async-start | bytes 16384 | tf_op jit(solution)/shard_map/all_to_all | solution.py:227
Sparse Core Ops, SparseCore 0:
  10.1 91.7 all-gather.3
  104.0 78.2 all-gather.5

commit v6 on v5

--- a/solution.py
+++ b/solution.py
@@ -63,18 +63,36 @@
     left = left_lanes(CHAN)
     both = jnp.where(left, both[:CHAN], both[CHAN:])
     fall = jnp.where(left, fall[:CHAN], fall[CHAN:])
-    for q in range(CHAN // chunk_rows):
+    span = CHAN // chunk_rows
+    row = lax.broadcasted_iota(jnp.int32, (CHAN, LANES), 0) % chunk_rows
+    lane = lax.broadcasted_iota(jnp.int32, (CHAN, LANES), 1) % CHAN // span
+    fall = jnp.where(row == lane, fall, 0.0)
+    for q in range(span):
+        for r in range(chunk_rows):
+            at = q * chunk_rows + r
+            out_ref[q, :, r * LANES : (r + 1) * LANES] = both[at : at + 1]
         rows = slice(q * chunk_rows, (q + 1) * chunk_rows)
-        out_ref[q, :chunk_rows, :] = both[rows]
-        out_ref[q, chunk_rows:, :] = fall[rows]
+        out_ref[q, :, chunk_rows * LANES :] = jnp.sum(fall[rows], axis=0, keepdims=True)
 
 
 def relay_kernel(chunk_rows, meta_ref, moved_ref, prompt_ref, out_ref):
+    left = left_lanes(chunk_rows)
+    row = lax.broadcasted_iota(jnp.int32, (chunk_rows, LANES), 0)
+    lane = lax.broadcasted_iota(jnp.int32, (chunk_rows, LANES), 1) % CHAN
+    chosen = lane == row * (CHAN // chunk_rows)
+
     def step(b, state):
         prompt = jnp.where(meta_ref[1, b] == 0, prompt_ref[0], prompt_ref[1])
         state = jnp.where(meta_ref[0, b] != 0, prompt, state)
         out_ref[b] = state
-        return moved_ref[b, chunk_rows:, :] * state + moved_ref[b, :chunk_rows, :]
+        change = jnp.concatenate(
+            [moved_ref[b, :, r * LANES : (r + 1) * LANES] for r in range(chunk_rows)], axis=0
+        )
+        fall = moved_ref[b, :, chunk_rows * LANES :]
+        fall = jnp.where(chosen, jnp.broadcast_to(fall, (chunk_rows, LANES)), 0.0)
+        first = jnp.sum(jnp.where(left, fall, 0.0), axis=1, keepdims=True)
+        second = jnp.sum(jnp.where(left, 0.0, fall), axis=1, keepdims=True)
+        return jnp.where(left, first, second) * state + change
 
     lax.fori_loop(
         0, moved_ref.shape[0], step, jnp.zeros((chunk_rows, LANES), F32), unroll=8
@@ -289,8 +307,8 @@
         functools.partial(block_end_kernel, chunk_rows),
         grid=(pairs,),
         in_specs=[col] * 3,
-        out_specs=pl.BlockSpec((chunks, 2 * chunk_rows, LANES), lambda p: (p, 0, 0)),
-        out_shape=jax.ShapeDtypeStruct((n_blk, 2 * chunk_rows, LANES), F32),
+        out_specs=pl.BlockSpec((chunks, 1, (chunk_rows + 1) * LANES), lambda p: (p, 0, 0)),
+        out_shape=jax.ShapeDtypeStruct((n_blk, 1, (chunk_rows + 1) * LANES), F32),
         compiler_params=limit(60),
         cost_estimate=cost(pairs * 20_000_000, 3 * rows * width * 2),
     )(lookup_vector_array, payload_vector_array, raw_forgetting_rate)

time: 239 us -> 235 us (0.983)
  waiting for transfers between devices: 47.9 us -> 42.2 us
    all_to_all x1, waiting for transfers between devices: 11.2 us -> 6.68 us  [per_device(): moved = lax.all_to_all(end, ('x', 'z'), 0, 0, tiled=True)]
  transfers between devices with their start and end apart: 16 -> 16, of which waited for: 11 -> 10; matrix products, arithmetic and copies ran while one was open for 4% -> 4% of each run, Pallas kernels for 8% -> 9%
where the time goes in v6:
time: 235 us; the launch traced here: 234 us
  starting transfers between devices  89.2 us (38%)
  blocking collectives  44.2 us (19%)
  waiting for transfers between devices  42.2 us (18%)
  Pallas kernels  25.9 us (11%)
  between operations  14.7 us (6%)
  local copies, waits for them, and re-layouts  10.4 us (4%)
  other arithmetic  7.11 us (3%)
    all_to_all x1, blocking collectives, copies(): return lax.all_to_all(sent, axes, 0, 0, tiled=True)  32 us
    ppermute x7, starting transfers between devices, spread(): piece = lax.ppermute(value, axis, pairs) if step else value  24.8 us
    all_to_all x1, starting transfers between devices, per_device(): moved = lax.all_to_all(end, ('x', 'z'), 0, 0, tiled=True)  19.1 us
    all_to_all x2, waiting for transfers between devices, copies(): return lax.all_to_all(sent, axes, 0, 0, tiled=True)  18.4 us
    all_to_all x2, starting transfers between devices, copies(): return lax.all_to_all(sent, axes, 0, 0, tiled=True)  16.8 us
    ppermute x2, starting transfers between devices, shifted(): lax.ppermute(value, axis, [(i, (i + steps) % count) for i in range(count)])  14.7 us
    all_gather x1, blocking collectives, per_device(): mixed = lax.all_gather(mixed, 'x', axis=0)  12.2 us
    pallas_call x2, Pallas kernels, score(): pl.pallas_call(functools.partial(score_kernel, layout, first, not first),...  11.4 us
  transfers between devices with their start and end apart: 16, of which 10 were waited for; matrix products, arithmetic and copies ran while one was open for 4% of the time, Pallas kernels for 9%

profile of v6, /device:TPU:1, one launch (start us, length us, event | category | flops | bytes accessed | tf_op | source)
XLA Modules:
  0.0 233.7 jit_solution(18218950369462311701)
XLA Ops:
  7.3 1.0 constant_dynamic-slice_fusion.1
  8.2 1.6 pad_maximum_fusion
  9.8 3.7 %shard_map.176 = f32[64,1,640]{2,1,0:T(1,128)} custom-call(bf16[128,512]{1,0:T(8,128)(2,1)} %k_ref.3, bf16[128,512]{1,0:T(8,128)(2,1)} %v_ref.3, bf16[128,512]{1,0:T(8,128)(2,1)} %w_ref.3), custom_call_target="tpu_custom_call" | custom-call | flops 80000000 | bytes 393216 | tf_op jit(solution)/shard_map/pallas_call | solution.py:306
  13.5 19.1 %all-to-all-start = ((f32[64,1,640]{2,1,0:T(1,128)}), f32[64,1,640]{2,1,0:T(1,128)S(1)}, u32[]{:S(2)}, u32[]{:S(2)}) async-start(f32[64,1,640]{2,1,0:T(1,128)} %shard_map.176), calls=%async_computation | async-start | bytes 327680 | tf_op jit(solution)/shard_map/all_to_all | solution.py:315
  32.7 1.1 reshape.87
  34.2 0.7 convert_element_type.35
  34.9 0.7 convert_element_type.36
  35.5 0.7 pad_maximum_fusion.1
  36.2 4.8 %shard_map.177 = (f32[128,512]{1,0:T(8,128)}, bf16[128,512]{1,0:T(8,128)(2,1)}, bf16[128,512]{1,0:T(8,128)(2,1)}) custom-call(bf16[128,512]{1,0:T(8,128)(2,1)} %r_ref.1, bf16[128,512]{1,0:T(8,128)(2,1)} %k_ref.3, bf16[128,512]{1,0:T(8,128)(2,1)} %v_ref.3, bf16[128,512]{1,0:T(8,128)(2,1)} %w_ref.3, f32[1,512]{1,0:T(1,128)} %bitcast.119), custom_call_target="tpu_custom_call" | custom-call | flops 240000000 | bytes 1048576 | tf_op jit(solution)/shard_map/pallas_call | solution.py:333
  41.0 0.7 compare_select_fusion
  41.7 0.8 gather_fusion
  42.6 1.7 constant_dynamic-slice_fusion.3
  44.3 6.7 %all-to-all-done.moved_ref = f32[64,1,640]{2,1,0:T(1,128)S(1)} async-done(((f32[64,1,640]{2,1,0:T(1,128)}), f32[64,1,640]{2,1,0:T(1,128)S(1)}, u32[]{:S(2)}, u32[]{:S(2)}) %all-to-all-start) | async-done | bytes 163872 | tf_op jit(solution)/shard_map/all_to_all | solution.py:315
  51.2 2.0 shard_map.178
  53.2 3.5 %collective-permute-start = (f32[1,128]{1,0:T(1,128)S(1)}, f32[1,128]{1,0:T(1,128)S(1)}, u32[]{:S(2)}, u32[]{:S(2)}) collective-permute-start(f32[1,128]{1,0:T(1,128)S(1)} %pad_bitcast_fusion), channel_id=1, source_target_pairs={{0,1},{1,0},{2,3},{3,2},{4,5},{5,4},{6,7},{7,6},{8,9},{9,8},{10,11... | collective-permute-start | bytes 1544 | tf_op jit(solution)/shard_map/ppermute | solution.py:258
  56.8 7.5 %all-to-all-start.1 = ((f32[64,4,128]{2,1,0:T(4,128)}), f32[64,4,128]{2,1,0:T(4,128)S(1)}, u32[]{:S(2)}, u32[]{:S(2)}) async-start(f32[64,4,128]{2,1,0:T(4,128)} %shard_map.178), calls=%async_computation.1 | async-start | bytes 262144 | tf_op jit(solution)/shard_map/all_to_all | solution.py:369
  64.4 3.2 %collective-permute-start.1 = (f32[2,1,128]{2,0,1:T(2,128)S(1)}, f32[2,1,128]{2,0,1:T(2,128)S(1)}, u32[]{:S(2)}, u32[]{:S(2)}) collective-permute-start(f32[2,1,128]{2,0,1:T(2,128)S(1)} %dynamic_update_slice.34), channel_id=1, source_target_pairs={{0,2},{2,4},{4,6},{6,0},{1,3},{3,5},{5,7},{7,1},{8,10},{10,12},{12... | collective-permute-start | bytes 3080 | tf_op jit(solution)/shard_map/ppermute | solution.py:258
  67.6 4.5 %collective-permute-start.2 = (f32[2,1,128]{2,0,1:T(2,128)S(1)}, f32[2,1,128]{2,0,1:T(2,128)S(1)}, u32[]{:S(2)}, u32[]{:S(2)}) collective-permute-start(f32[2,1,128]{2,0,1:T(2,128)S(1)} %dynamic_update_slice.34), channel_id=1, source_target_pairs={{0,4},{2,6},{4,0},{6,2},{1,5},{3,7},{5,1},{7,3},{8,12},{10,14},{12... | collective-permute-start | bytes 3080 | tf_op jit(solution)/shard_map/ppermute | solution.py:258
  72.1 3.0 %collective-permute-start.3 = (f32[2,1,128]{2,0,1:T(2,128)S(1)}, f32[2,1,128]{2,0,1:T(2,128)S(1)}, u32[]{:S(2)}, u32[]{:S(2)}) collective-permute-start(f32[2,1,128]{2,0,1:T(2,128)S(1)} %dynamic_update_slice.34), channel_id=1, source_target_pairs={{0,6},{2,0},{4,2},{6,4},{1,7},{3,1},{5,3},{7,5},{8,14},{10,8},{12,... | collective-permute-start | bytes 3080 | tf_op jit(solution)/shard_map/ppermute | solution.py:258
  75.2 1.6 collective-permute-done.3
  76.8 3.9 %all-to-all-done.1 = f32[64,4,128]{2,1,0:T(4,128)S(1)} async-done(((f32[64,4,128]{2,1,0:T(4,128)}), f32[64,4,128]{2,1,0:T(4,128)S(1)}, u32[]{:S(2)}, u32[]{:S(2)}) %all-to-all-start.1) | async-done | bytes 131104 | tf_op jit(solution)/shard_map/all_to_all | solution.py:369
  80.7 0.9 copy-done.1
  81.7 0.9 copy-done.3
  82.6 0.9 copy-done.4
  83.5 2.0 shard_map.179
  85.5 12.2 %all-gather = bf16[512,512]{1,0:T(8,128)(2,1)S(1)} all-gather(bf16[128,512]{1,0:T(8,128)(2,1)S(1)} %shard_map.179), channel_id=2, replica_groups=mesh['x'=4,'z'=16,'y'=4,'c'=2] {'x'}, dimensions={0}, use_global_device_ids=true | all-gather | bytes 655360 | tf_op jit(solution)/shard_map/all_gather | solution.py:385
  97.7 2.0 shard_map.180
  99.8 10.9 %collective-permute-start.4 = (f32[256,1024]{1,0:T(8,128)S(1)}, f32[256,1024]{1,0:T(8,128)S(1)}, u32[]{:S(2)}, u32[]{:S(2)}) collective-permute-start(f32[256,1024]{1,0:T(8,128)S(1)} %get-tuple-element.43), channel_id=1, source_target_pairs={{0,1},{1,0},{2,3},{3,2},{4,5},{5,4},{6,7},{7,6},{8,9},{9,8},{10,11... | collective-permute-start | bytes 3145736 | tf_op jit(solution)/shard_map/ppermute | solution.py:239
  110.7 2.3 collective-permute-done.4
  113.0 1.1 add.175
  114.1 6.3 %all-to-all-start.2 = ((f32[16,16,1024]{2,1,0:T(8,128)}), f32[16,16,1024]{2,1,0:T(8,128)S(1)}, u32[]{:S(2)}, u32[]{:S(2)}) async-start(f32[16,16,1024]{2,1,0:T(8,128)} %bitcast.27), calls=%async_computation.2 | async-start | bytes 2097152 | tf_op jit(solution)/shard_map/all_to_all | solution.py:407
  120.4 3.2 %collective-permute-start.5 = (f32[4,2,1,128]{3,1,0,2:T(2,128)S(1)}, f32[4,2,1,128]{3,1,0,2:T(2,128)S(1)}, u32[]{:S(2)}, u32[]{:S(2)}) collective-permute-start(f32[4,2,1,128]{3,1,0,2:T(2,128)S(1)} %constant_dynamic-update-slice_fusion), channel_id=1, source_target_pairs={{0,128},{128,256},{256,384},{384,0},{1,129},{129,257},{257,385},{3... | collective-permute-start | bytes 12296 | tf_op jit(solution)/shard_map/ppermute | solution.py:258
  123.6 4.3 %collective-permute-start.6 = (f32[4,2,1,128]{3,1,0,2:T(2,128)S(1)}, f32[4,2,1,128]{3,1,0,2:T(2,128)S(1)}, u32[]{:S(2)}, u32[]{:S(2)}) collective-permute-start(f32[4,2,1,128]{3,1,0,2:T(2,128)S(1)} %constant_dynamic-update-slice_fusion), channel_id=1, source_target_pairs={{0,256},{128,384},{256,0},{384,128},{1,257},{129,385},{257,1},{385... | collective-permute-start | bytes 12296 | tf_op jit(solution)/shard_map/ppermute | solution.py:258
  127.9 3.1 %collective-permute-start.7 = (f32[4,2,1,128]{3,1,0,2:T(2,128)S(1)}, f32[4,2,1,128]{3,1,0,2:T(2,128)S(1)}, u32[]{:S(2)}, u32[]{:S(2)}) collective-permute-start(f32[4,2,1,128]{3,1,0,2:T(2,128)S(1)} %constant_dynamic-update-slice_fusion), channel_id=1, source_target_pairs={{0,384},{128,0},{256,128},{384,256},{1,385},{129,1},{257,129},{385... | collective-permute-start | bytes 12296 | tf_op jit(solution)/shard_map/ppermute | solution.py:258
  131.1 3.2 %collective-permute-done.5 = f32[4,2,1,128]{3,1,0,2:T(2,128)S(1)} collective-permute-done((f32[4,2,1,128]{3,1,0,2:T(2,128)S(1)}, f32[4,2,1,128]{3,1,0,2:T(2,128)S(1)}, u32[]{:S(2)}, u32[]{:S(2)}) %collective-permute-start.5) | collective-permute-done | bytes 4128 | tf_op jit(solution)/shard_map/ppermute | solution.py:258
  134.8 1.8 all-to-all-done.2
  137.6 32.0 %all_to_all.30 = bf16[16,16,4096]{2,1,0:T(8,128)(2,1)S(1)} all-to-all(bf16[16,16,4096]{2,1,0:T(8,128)(2,1)S(1)} %broadcast_in_dim.104), channel_id=1, replica_groups=mesh['x'=4,'z'=16,'y'=4,'c'=2] {'y','x'}, dimensions={0} | all-to-all | bytes 4194304 | tf_op jit(solution)/shard_map/all_to_all | solution.py:245
  169.5 3.7 %collective-permute-start.8 = (bf16[256,4096]{1,0:T(8,128)(2,1)S(1)}, bf16[256,4096]{1,0:T(8,128)(2,1)}, u32[]{:S(2)}, u32[]{:S(2)}) collective-permute-start(bf16[256,4096]{1,0:T(8,128)(2,1)S(1)} %bitcast.96), channel_id=1, source_target_pairs={{0,1},{1,0},{2,3},{3,2},{4,5},{5,4},{6,7},{7,6},{8,9},{9,8},{10,11... | collective-permute-start | bytes 6291464 | tf_op jit(solution)/shard_map/ppermute | solution.py:239
  173.5 3.6 %collective-permute-done.8.theirs_ref = bf16[256,4096]{1,0:T(8,128)(2,1)} collective-permute-done((bf16[256,4096]{1,0:T(8,128)(2,1)S(1)}, bf16[256,4096]{1,0:T(8,128)(2,1)}, u32[]{:S(2)}, u32[]{:S(2)}) %collective-permute-start.8) | collective-permute-done | bytes 2097184 | tf_op jit(solution)/shard_map/ppermute | solution.py:239
  177.2 5.5 %shard_map.181.refs_0_ = f32[3,512]{1,0:T(4,128)S(1)} custom-call(s32[2]{0:T(128)S(1)} %pad_add_fusion.1.place_ref, bf16[256,4096]{1,0:T(8,128)(2,1)S(1)} %bitcast.97, bf16[256,4096]{1,0:T(8,128)(2,1)} %collective-permute-done.8.theirs_ref, s32[1,512]{1,0:T(1,128)S(1)} %convert_element_type.43.label_ref, bf16[512,4096]{1,0:T(8,128)(2,1)} %all-gather.4.cloned.1.call-done.vocab_ref), custom_call_target="tpu_custom_call" | custom-call | flops 2147483648 | bytes 8388608 | tf_op jit(solution)/shard_map/pallas_call | solution.py:424
  182.7 5.9 %shard_map.182 = f32[2,512]{1,0:T(2,128)S(1)} custom-call(s32[2]{0:T(128)S(1)} %pad_add_fusion.1.place_ref, bf16[256,4096]{1,0:T(8,128)(2,1)S(1)} %bitcast.98, bf16[256,4096]{1,0:T(8,128)(2,1)} %collective-permute-done.8.theirs_ref, s32[1,512]{1,0:T(1,128)S(1)} %convert_element_type.43.label_ref, bf16[640,4096]{1,0:T(8,128)(2,1)} %all-gather.6.cloned.1.call-done.vocab_ref, ...), custom_call_target="tpu_custom_call" | custom-call | flops 2684354560 | bytes 9437184 | tf_op jit(solution)/shard_map/pallas_call | solution.py:424
  188.6 0.7 broadcast_in_dim.105
  189.3 10.2 %all-to-all-start.4 = ((f32[32,2,512]{2,1,0:T(2,128)}), f32[32,2,512]{2,1,0:T(2,128)S(1)}, u32[]{:S(2)}, u32[]{:S(2)}) async-start(f32[32,2,512]{2,1,0:T(2,128)} %broadcast_in_dim.105), calls=%async_computation.4 | async-start | bytes 262144 | tf_op jit(solution)/shard_map/all_to_all | solution.py:245
  199.6 7.6 %all-to-all-done.4 = f32[32,2,512]{2,1,0:T(2,128)S(1)} async-done(((f32[32,2,512]{2,1,0:T(2,128)}), f32[32,2,512]{2,1,0:T(2,128)S(1)}, u32[]{:S(2)}, u32[]{:S(2)}) %all-to-all-start.4) | async-done | bytes 131104 | tf_op jit(solution)/shard_map/all_to_all | solution.py:245
  207.6 0.6 broadcast_in_dim.106
  208.2 6.6 %all-to-all-start.5 = ((f32[16,1,128]{2,1,0:T(1,128)}), f32[16,1,128]{2,1,0:T(1,128)S(1)}, u32[]{:S(2)}, u32[]{:S(2)}) async-start(f32[16,1,128]{2,1,0:T(1,128)} %broadcast_in_dim.106), calls=%async_computation.5 | async-start | bytes 16384 | tf_op jit(solution)/shard_map/all_to_all | solution.py:245
  214.8 0.5 fusion.6
  215.4 10.8 %all-to-all-done.5 = f32[16,1,128]{2,1,0:T(1,128)S(1)} async-done(((f32[16,1,128]{2,1,0:T(1,128)}), f32[16,1,128]{2,1,0:T(1,128)S(1)}, u32[]{:S(2)}, u32[]{:S(2)}) %all-to-all-start.5) | async-done | bytes 8224 | tf_op jit(solution)/shard_map/all_to_all | solution.py:245
  (70 shorter events, 3.7 us)
Async XLA Ops:
  7.2 34.5 %copy-start = (s32[16]{0:T(128)S(1)}, s32[16]{0:T(128)}, u32[]{:S(2)}) copy-start(s32[16]{0:T(128)} %param.33) | copy-start | bytes 196
  7.2 35.3 %copy-start.8 = (s32[64]{0:T(128)S(1)}, s32[64]{0:T(128)}, u32[]{:S(2)}) copy-start(s32[64]{0:T(128)} %param.32) | copy-start | bytes 772
  7.2 73.5 %copy-start.5 = (f32[512]{0:T(512)S(1)}, f32[512]{0:T(512)}, u32[]{:S(2)}) copy-start(f32[512]{0:T(512)} %param.24) | copy-start | bytes 6148
  7.2 73.5 %copy-start.2 = (bf16[128,512]{1,0:T(8,128)(2,1)S(1)}, bf16[128,512]{1,0:T(8,128)(2,1)}, u32[]{:S(2)}) copy-start(bf16[128,512]{1,0:T(8,128)(2,1)} %g_ref.1) | copy-start | bytes 393220
  7.2 90.5 %all-gather.4.cloned.1.call-start = ((), (), s32[]{:S(2)}) async-start(), calls=%async_computation.6 | async-start | bytes 4456448 | tf_op jit(solution)/shard_map/all_gather | solution.py:301
  13.5 37.4 %all-to-all-start = ((f32[64,1,640]{2,1,0:T(1,128)}), f32[64,1,640]{2,1,0:T(1,128)S(1)}, u32[]{:S(2)}, u32[]{:S(2)}) async-start(f32[64,1,640]{2,1,0:T(1,128)} %shard_map.176), calls=%async_computation | async-start | bytes 327680 | tf_op jit(solution)/shard_map/all_to_all | solution.py:315
  32.7 150.0 %all-gather.6.cloned.1.call-start = ((), (), s32[]{:S(2)}) async-start(), calls=%async_computation.7 | async-start | bytes 5570560 | tf_op jit(solution)/shard_map/all_gather | solution.py:358
  53.2 11.1 %collective-permute-start = (f32[1,128]{1,0:T(1,128)S(1)}, f32[1,128]{1,0:T(1,128)S(1)}, u32[]{:S(2)}, u32[]{:S(2)}) collective-permute-start(f32[1,128]{1,0:T(1,128)S(1)} %pad_bitcast_fusion), channel_id=1, source_target_pairs={{0,1},{1,0},{2,3},{3,2},{4,5},{5,4},{6,7},{7,6},{8,9},{9,8},{10,11... | collective-permute-start | bytes 1544 | tf_op jit(solution)/shard_map/ppermute | solution.py:258
  56.8 23.9 %all-to-all-start.1 = ((f32[64,4,128]{2,1,0:T(4,128)}), f32[64,4,128]{2,1,0:T(4,128)S(1)}, u32[]{:S(2)}, u32[]{:S(2)}) async-start(f32[64,4,128]{2,1,0:T(4,128)} %shard_map.178), calls=%async_computation.1 | async-start | bytes 262144 | tf_op jit(solution)/shard_map/all_to_all | solution.py:369
  64.4 10.8 %collective-permute-start.1 = (f32[2,1,128]{2,0,1:T(2,128)S(1)}, f32[2,1,128]{2,0,1:T(2,128)S(1)}, u32[]{:S(2)}, u32[]{:S(2)}) collective-permute-start(f32[2,1,128]{2,0,1:T(2,128)S(1)} %dynamic_update_slice.34), channel_id=1, source_target_pairs={{0,2},{2,4},{4,6},{6,0},{1,3},{3,5},{5,7},{7,1},{8,10},{10,12},{12... | collective-permute-start | bytes 3080 | tf_op jit(solution)/shard_map/ppermute | solution.py:258
  67.6 7.6 %collective-permute-start.2 = (f32[2,1,128]{2,0,1:T(2,128)S(1)}, f32[2,1,128]{2,0,1:T(2,128)S(1)}, u32[]{:S(2)}, u32[]{:S(2)}) collective-permute-start(f32[2,1,128]{2,0,1:T(2,128)S(1)} %dynamic_update_slice.34), channel_id=1, source_target_pairs={{0,4},{2,6},{4,0},{6,2},{1,5},{3,7},{5,1},{7,3},{8,12},{10,14},{12... | collective-permute-start | bytes 3080 | tf_op jit(solution)/shard_map/ppermute | solution.py:258
  72.1 4.7 %collective-permute-start.3 = (f32[2,1,128]{2,0,1:T(2,128)S(1)}, f32[2,1,128]{2,0,1:T(2,128)S(1)}, u32[]{:S(2)}, u32[]{:S(2)}) collective-permute-start(f32[2,1,128]{2,0,1:T(2,128)S(1)} %dynamic_update_slice.34), channel_id=1, source_target_pairs={{0,6},{2,0},{4,2},{6,4},{1,7},{3,1},{5,3},{7,5},{8,14},{10,8},{12,... | collective-permute-start | bytes 3080 | tf_op jit(solution)/shard_map/ppermute | solution.py:258
  80.7 1.0 copy-start.1
  81.7 0.9 copy-start.3
  82.6 0.9 copy-start.4
  99.7 37.1 %copy-start.6 = (bf16[16,4096]{1,0:T(8,128)(2,1)S(1)}, bf16[16,4096]{1,0:T(8,128)(2,1)}, u32[]{:S(2)}) copy-start(bf16[16,4096]{1,0:T(8,128)(2,1)} %param.26) | copy-start | bytes 393220
  99.7 37.5 %copy-start.7 = (f32[4096]{0:T(1024)S(1)}, f32[4096]{0:T(1024)}, u32[]{:S(2)}) copy-start(f32[4096]{0:T(1024)} %param.25) | copy-start | bytes 49156
  99.8 13.2 %collective-permute-start.4 = (f32[256,1024]{1,0:T(8,128)S(1)}, f32[256,1024]{1,0:T(8,128)S(1)}, u32[]{:S(2)}, u32[]{:S(2)}) collective-permute-start(f32[256,1024]{1,0:T(8,128)S(1)} %get-tuple-element.43), channel_id=1, source_target_pairs={{0,1},{1,0},{2,3},{3,2},{4,5},{5,4},{6,7},{7,6},{8,9},{9,8},{10,11... | collective-permute-start | bytes 3145736 | tf_op jit(solution)/shard_map/ppermute | solution.py:239
  114.1 22.6 %all-to-all-start.2 = ((f32[16,16,1024]{2,1,0:T(8,128)}), f32[16,16,1024]{2,1,0:T(8,128)S(1)}, u32[]{:S(2)}, u32[]{:S(2)}) async-start(f32[16,16,1024]{2,1,0:T(8,128)} %bitcast.27), calls=%async_computation.2 | async-start | bytes 2097152 | tf_op jit(solution)/shard_map/all_to_all | solution.py:407
  120.4 13.9 %collective-permute-start.5 = (f32[4,2,1,128]{3,1,0,2:T(2,128)S(1)}, f32[4,2,1,128]{3,1,0,2:T(2,128)S(1)}, u32[]{:S(2)}, u32[]{:S(2)}) collective-permute-start(f32[4,2,1,128]{3,1,0,2:T(2,128)S(1)} %constant_dynamic-update-slice_fusion), channel_id=1, source_target_pairs={{0,128},{128,256},{256,384},{384,0},{1,129},{129,257},{257,385},{3... | collective-permute-start | bytes 12296 | tf_op jit(solution)/shard_map/ppermute | solution.py:258
  123.6 11.2 %collective-permute-start.6 = (f32[4,2,1,128]{3,1,0,2:T(2,128)S(1)}, f32[4,2,1,128]{3,1,0,2:T(2,128)S(1)}, u32[]{:S(2)}, u32[]{:S(2)}) collective-permute-start(f32[4,2,1,128]{3,1,0,2:T(2,128)S(1)} %constant_dynamic-update-slice_fusion), channel_id=1, source_target_pairs={{0,256},{128,384},{256,0},{384,128},{1,257},{129,385},{257,1},{385... | collective-permute-start | bytes 12296 | tf_op jit(solution)/shard_map/ppermute | solution.py:258
  127.9 6.9 %collective-permute-start.7 = (f32[4,2,1,128]{3,1,0,2:T(2,128)S(1)}, f32[4,2,1,128]{3,1,0,2:T(2,128)S(1)}, u32[]{:S(2)}, u32[]{:S(2)}) collective-permute-start(f32[4,2,1,128]{3,1,0,2:T(2,128)S(1)} %constant_dynamic-update-slice_fusion), channel_id=1, source_target_pairs={{0,384},{128,0},{256,128},{384,256},{1,385},{129,1},{257,129},{385... | collective-permute-start | bytes 12296 | tf_op jit(solution)/shard_map/ppermute | solution.py:258
  169.5 7.6 %collective-permute-start.8 = (bf16[256,4096]{1,0:T(8,128)(2,1)S(1)}, bf16[256,4096]{1,0:T(8,128)(2,1)}, u32[]{:S(2)}, u32[]{:S(2)}) collective-permute-start(bf16[256,4096]{1,0:T(8,128)(2,1)S(1)} %bitcast.96), channel_id=1, source_target_pairs={{0,1},{1,0},{2,3},{3,2},{4,5},{5,4},{6,7},{7,6},{8,9},{9,8},{10,11... | collective-permute-start | bytes 6291464 | tf_op jit(solution)/shard_map/ppermute | solution.py:239
  189.3 17.9 %all-to-all-start.4 = ((f32[32,2,512]{2,1,0:T(2,128)}), f32[32,2,512]{2,1,0:T(2,128)S(1)}, u32[]{:S(2)}, u32[]{:S(2)}) async-start(f32[32,2,512]{2,1,0:T(2,128)} %broadcast_in_dim.105), calls=%async_computation.4 | async-start | bytes 262144 | tf_op jit(solution)/shard_map/all_to_all | solution.py:245
  208.2 17.9 %all-to-all-start.5 = ((f32[16,1,128]{2,1,0:T(1,128)}), f32[16,1,128]{2,1,0:T(1,128)S(1)}, u32[]{:S(2)}, u32[]{:S(2)}) async-start(f32[16,1,128]{2,1,0:T(1,128)} %broadcast_in_dim.106), calls=%async_computation.5 | async-start | bytes 16384 | tf_op jit(solution)/shard_map/all_to_all | solution.py:245
Sparse Core Ops, SparseCore 0:
  10.1 87.5 all-gather.3
  99.8 79.1 all-gather.5

commit v7 on v6

--- a/solution.py
+++ b/solution.py
@@ -173,13 +173,16 @@
     layout, first, final, place_ref, mine_ref, theirs_ref, label_ref, vocab_ref, *refs
 ):
     group, skipped, offset, vocab_local = layout
-    known_ref, (out_ref, state_ref) = (None, refs) if first else (refs[0], refs[1:])
+    known_ref, refs = (None, refs) if first else (refs[0], refs[1:])
+    out_ref, state_ref, held_ref, arrived = refs
     step = pl.program_id(0)
     tile, half = vocab_ref.shape[0], mine_ref.shape[0]
     core = place_ref[0]
+    copy = pltpu.make_async_copy(theirs_ref, held_ref, arrived)
 
     @pl.when(step == 0)
     def _():
+        copy.start()
         if first:
             state_ref[0:1] = jnp.full((1, 2 * half), -3.0e38, F32)
             state_ref[1:3] = jnp.zeros((2, 2 * half), F32)
@@ -192,7 +195,9 @@
     entry = jnp.where(
         row < skipped, -1, place_ref[1] + source * vocab_local + (row - skipped + offset)
     )
-    for part, tokens in enumerate((mine_ref, theirs_ref)):
+    for part, tokens in enumerate((mine_ref, held_ref)):
+        if part:
+            pl.when(step == 0)(copy.wait)
         at = slice(part * half, (part + 1) * half)
         label = jnp.where(core == part, label_ref[:, :half], label_ref[:, half:])
         logits = mm_t(vocab_ref[...], tokens[...])
@@ -212,10 +217,12 @@
             out_ref[...] = state_ref[...]
             return
         part = state_ref[0:1] + jnp.log(state_ref[1:2])
-        for row, value in enumerate((part, state_ref[2:3])):
-            left, right = value[:, :half], value[:, half:]
-            out_ref[row : row + 1, :half] = jnp.where(core == 0, left, right)
-            out_ref[row : row + 1, half:] = jnp.where(core == 0, right, left)
+        both = jnp.concatenate([part, state_ref[2:3]], axis=0)
+        left, right = both[:, :half], both[:, half:]
+        both = jnp.concatenate(
+            [jnp.where(core == 0, left, right), jnp.where(core == 0, right, left)], axis=1
+        )
+        out_ref[...] = jnp.broadcast_to(both[None], out_ref.shape)
 
 
 def cost(flops, nbytes):
@@ -420,21 +427,26 @@
     count = plane * own
     labels = facts[0].reshape(1, count).astype(jnp.int32)
     def score(vocab, layout, tile, known=None):
-        first, height = known is None, 3 if known is None else 2
+        first = known is None
+        out = (3, count) if first else (plane, 2, count)
         return pl.pallas_call(
             functools.partial(score_kernel, layout, first, not first),
             grid=(vocab.shape[0] // tile,),
             in_specs=[
                 smem,
                 vmem,
-                vmem,
+                pl.BlockSpec(memory_space=pl.ANY),
                 vmem,
                 pl.BlockSpec((tile, embed), lambda i: (i, 0)),
             ]
             + ([] if first else [vmem]),
-            out_specs=whole(height, count),
-            out_shape=jax.ShapeDtypeStruct((height, count), F32),
-            scratch_shapes=[pltpu.VMEM((3, count), F32)],
+            out_specs=whole(*out),
+            out_shape=jax.ShapeDtypeStruct(out, F32),
+            scratch_shapes=[
+                pltpu.VMEM((3, count), F32),
+                pltpu.VMEM((count // nc, embed), BF16),
+                pltpu.SemaphoreType.DMA,
+            ],
             compiler_params=limit(24),
             cost_estimate=cost(
                 2 * count * vocab.shape[0] * embed, (count + vocab.shape[0]) * embed * 2
@@ -444,7 +456,7 @@
     known = score(gathered_1, (held + early, held, 0, vocab_local), gathered_1.shape[0])
     late = gathered_2.shape[0] // 2
     both = score(gathered_2, (share - early, 0, early, vocab_local), late, known)
-    both = copies(both, ("x", "y", "c"))
+    both = lax.all_to_all(both, ("x", "y", "c"), 0, 0, tiled=True)
     part, picked = both[:, 0], both[:, 1]
     peak = jnp.max(part, axis=0)
     logp = jnp.sum(picked, axis=0) - peak - jnp.log(jnp.sum(jnp.exp(part - peak), axis=0))

time: 235 us -> 238 us (1.013)
  Pallas kernels: 25.9 us -> 30.7 us
    all_to_all x2 -> x1, starting transfers between devices: 16.8 us -> 6.6 us  [copies(): return lax.all_to_all(sent, axes, 0, 0, tiled=True)]
    all_to_all x0 -> x1, starting transfers between devices: none -> 8.55 us  [per_device(): both = lax.all_to_all(both, ('x', 'y', 'c'), 0, 0, tiled=True)]
    all_to_all x0 -> x1, waiting for transfers between devices: none -> 7.62 us  [per_device(): both = lax.all_to_all(both, ('x', 'y', 'c'), 0, 0, tiled=True)]
    all_to_all x2 -> x1, waiting for transfers between devices: 18.4 us -> 10.8 us  [copies(): return lax.all_to_all(sent, axes, 0, 0, tiled=True)]
    pallas_call x2, Pallas kernels: 11.4 us -> 16.2 us  [score(): pl.pallas_call(functools.partial(score_kernel, layout, first, not first),...]
where the time goes in v7:
time: 238 us; the launch traced here: 236 us
  starting transfers between devices  87.6 us (37%)
  blocking collectives  44.2 us (19%)
  waiting for transfers between devices  42.2 us (18%)
  Pallas kernels  30.7 us (13%)
  between operations  14.7 us (6%)
  local copies, waits for them, and re-layouts  9.74 us (4%)
  other arithmetic  7.11 us (3%)
    all_to_all x1, blocking collectives, copies(): return lax.all_to_all(sent, axes, 0, 0, tiled=True)  32 us
    ppermute x7, starting transfers between devices, spread(): piece = lax.ppermute(value, axis, pairs) if step else value  24.8 us
    all_to_all x1, starting transfers between devices, per_device(): moved = lax.all_to_all(end, ('x', 'z'), 0, 0, tiled=True)  19.1 us
    pallas_call x2, Pallas kernels, score(): pl.pallas_call(functools.partial(score_kernel, layout, first, not first),...  16.2 us
    ppermute x2, starting transfers between devices, shifted(): lax.ppermute(value, axis, [(i, (i + steps) % count) for i in range(count)])  14.7 us
    all_gather x1, blocking collectives, per_device(): mixed = lax.all_gather(mixed, 'x', axis=0)  12.2 us
    all_to_all x1, waiting for transfers between devices, copies(): return lax.all_to_all(sent, axes, 0, 0, tiled=True)  10.8 us
    all_to_all x1, starting transfers between devices, per_device(): both = lax.all_to_all(both, ('x', 'y', 'c'), 0, 0, tiled=True)  8.55 us
  transfers between devices with their start and end apart: 16, of which 10 were waited for; matrix products, arithmetic and copies ran while one was open for 4% of the time, Pallas kernels for 9%

profile of v7, /device:TPU:1, one launch (start us, length us, event | category | flops | bytes accessed | tf_op | source)
XLA Modules:
  0.0 236.2 jit_solution(1240690088200781503)
XLA Ops:
  7.3 1.0 constant_dynamic-slice_fusion.1
  8.2 1.6 pad_maximum_fusion
  9.8 3.7 %shard_map.176 = f32[64,1,640]{2,1,0:T(1,128)} custom-call(bf16[128,512]{1,0:T(8,128)(2,1)} %k_ref.3, bf16[128,512]{1,0:T(8,128)(2,1)} %v_ref.3, bf16[128,512]{1,0:T(8,128)(2,1)} %w_ref.3), custom_call_target="tpu_custom_call" | custom-call | flops 80000000 | bytes 393216 | tf_op jit(solution)/shard_map/pallas_call | solution.py:313
  13.5 19.1 %all-to-all-start = ((f32[64,1,640]{2,1,0:T(1,128)}), f32[64,1,640]{2,1,0:T(1,128)S(1)}, u32[]{:S(2)}, u32[]{:S(2)}) async-start(f32[64,1,640]{2,1,0:T(1,128)} %shard_map.176), calls=%async_computation | async-start | bytes 327680 | tf_op jit(solution)/shard_map/all_to_all | solution.py:322
  32.7 1.1 reshape.86
  34.2 0.7 convert_element_type.35
  34.9 0.7 convert_element_type.36
  35.5 0.7 pad_maximum_fusion.1
  36.2 4.8 %shard_map.177 = (f32[128,512]{1,0:T(8,128)}, bf16[128,512]{1,0:T(8,128)(2,1)}, bf16[128,512]{1,0:T(8,128)(2,1)}) custom-call(bf16[128,512]{1,0:T(8,128)(2,1)} %r_ref.1, bf16[128,512]{1,0:T(8,128)(2,1)} %k_ref.3, bf16[128,512]{1,0:T(8,128)(2,1)} %v_ref.3, bf16[128,512]{1,0:T(8,128)(2,1)} %w_ref.3, f32[1,512]{1,0:T(1,128)} %bitcast.119), custom_call_target="tpu_custom_call" | custom-call | flops 240000000 | bytes 1048576 | tf_op jit(solution)/shard_map/pallas_call | solution.py:340
  41.0 0.7 compare_select_fusion
  41.7 0.8 gather_fusion
  42.6 1.7 constant_dynamic-slice_fusion.3
  44.3 6.7 %all-to-all-done.moved_ref = f32[64,1,640]{2,1,0:T(1,128)S(1)} async-done(((f32[64,1,640]{2,1,0:T(1,128)}), f32[64,1,640]{2,1,0:T(1,128)S(1)}, u32[]{:S(2)}, u32[]{:S(2)}) %all-to-all-start) | async-done | bytes 163872 | tf_op jit(solution)/shard_map/all_to_all | solution.py:322
  51.2 2.0 shard_map.178
  53.2 3.5 %collective-permute-start = (f32[1,128]{1,0:T(1,128)S(1)}, f32[1,128]{1,0:T(1,128)S(1)}, u32[]{:S(2)}, u32[]{:S(2)}) collective-permute-start(f32[1,128]{1,0:T(1,128)S(1)} %pad_bitcast_fusion), channel_id=1, source_target_pairs={{0,1},{1,0},{2,3},{3,2},{4,5},{5,4},{6,7},{7,6},{8,9},{9,8},{10,11... | collective-permute-start | bytes 1544 | tf_op jit(solution)/shard_map/ppermute | solution.py:265
  56.8 7.5 %all-to-all-start.1 = ((f32[64,4,128]{2,1,0:T(4,128)}), f32[64,4,128]{2,1,0:T(4,128)S(1)}, u32[]{:S(2)}, u32[]{:S(2)}) async-start(f32[64,4,128]{2,1,0:T(4,128)} %shard_map.178), calls=%async_computation.1 | async-start | bytes 262144 | tf_op jit(solution)/shard_map/all_to_all | solution.py:376
  64.4 3.2 %collective-permute-start.1 = (f32[2,1,128]{2,0,1:T(2,128)S(1)}, f32[2,1,128]{2,0,1:T(2,128)S(1)}, u32[]{:S(2)}, u32[]{:S(2)}) collective-permute-start(f32[2,1,128]{2,0,1:T(2,128)S(1)} %dynamic_update_slice.34), channel_id=1, source_target_pairs={{0,2},{2,4},{4,6},{6,0},{1,3},{3,5},{5,7},{7,1},{8,10},{10,12},{12... | collective-permute-start | bytes 3080 | tf_op jit(solution)/shard_map/ppermute | solution.py:265
  67.6 4.5 %collective-permute-start.2 = (f32[2,1,128]{2,0,1:T(2,128)S(1)}, f32[2,1,128]{2,0,1:T(2,128)S(1)}, u32[]{:S(2)}, u32[]{:S(2)}) collective-permute-start(f32[2,1,128]{2,0,1:T(2,128)S(1)} %dynamic_update_slice.34), channel_id=1, source_target_pairs={{0,4},{2,6},{4,0},{6,2},{1,5},{3,7},{5,1},{7,3},{8,12},{10,14},{12... | collective-permute-start | bytes 3080 | tf_op jit(solution)/shard_map/ppermute | solution.py:265
  72.1 3.0 %collective-permute-start.3 = (f32[2,1,128]{2,0,1:T(2,128)S(1)}, f32[2,1,128]{2,0,1:T(2,128)S(1)}, u32[]{:S(2)}, u32[]{:S(2)}) collective-permute-start(f32[2,1,128]{2,0,1:T(2,128)S(1)} %dynamic_update_slice.34), channel_id=1, source_target_pairs={{0,6},{2,0},{4,2},{6,4},{1,7},{3,1},{5,3},{7,5},{8,14},{10,8},{12,... | collective-permute-start | bytes 3080 | tf_op jit(solution)/shard_map/ppermute | solution.py:265
  75.2 1.6 collective-permute-done.3
  76.8 3.9 %all-to-all-done.1 = f32[64,4,128]{2,1,0:T(4,128)S(1)} async-done(((f32[64,4,128]{2,1,0:T(4,128)}), f32[64,4,128]{2,1,0:T(4,128)S(1)}, u32[]{:S(2)}, u32[]{:S(2)}) %all-to-all-start.1) | async-done | bytes 131104 | tf_op jit(solution)/shard_map/all_to_all | solution.py:376
  80.7 0.9 copy-done.1
  81.7 0.9 copy-done.3
  82.6 0.9 copy-done.4
  83.5 2.0 shard_map.179
  85.5 12.2 %all-gather = bf16[512,512]{1,0:T(8,128)(2,1)S(1)} all-gather(bf16[128,512]{1,0:T(8,128)(2,1)S(1)} %shard_map.179), channel_id=2, replica_groups=mesh['x'=4,'z'=16,'y'=4,'c'=2] {'x'}, dimensions={0}, use_global_device_ids=true | all-gather | bytes 655360 | tf_op jit(solution)/shard_map/all_gather | solution.py:392
  97.7 2.0 shard_map.180
  99.8 10.9 %collective-permute-start.4 = (f32[256,1024]{1,0:T(8,128)S(1)}, f32[256,1024]{1,0:T(8,128)S(1)}, u32[]{:S(2)}, u32[]{:S(2)}) collective-permute-start(f32[256,1024]{1,0:T(8,128)S(1)} %get-tuple-element.43), channel_id=1, source_target_pairs={{0,1},{1,0},{2,3},{3,2},{4,5},{5,4},{6,7},{7,6},{8,9},{9,8},{10,11... | collective-permute-start | bytes 3145736 | tf_op jit(solution)/shard_map/ppermute | solution.py:246
  110.7 2.3 collective-permute-done.4
  113.0 1.1 add.175
  114.1 6.3 %all-to-all-start.2 = ((f32[16,16,1024]{2,1,0:T(8,128)}), f32[16,16,1024]{2,1,0:T(8,128)S(1)}, u32[]{:S(2)}, u32[]{:S(2)}) async-start(f32[16,16,1024]{2,1,0:T(8,128)} %bitcast.27), calls=%async_computation.2 | async-start | bytes 2097152 | tf_op jit(solution)/shard_map/all_to_all | solution.py:414
  120.4 3.2 %collective-permute-start.5 = (f32[4,2,1,128]{3,1,0,2:T(2,128)S(1)}, f32[4,2,1,128]{3,1,0,2:T(2,128)S(1)}, u32[]{:S(2)}, u32[]{:S(2)}) collective-permute-start(f32[4,2,1,128]{3,1,0,2:T(2,128)S(1)} %constant_dynamic-update-slice_fusion), channel_id=1, source_target_pairs={{0,128},{128,256},{256,384},{384,0},{1,129},{129,257},{257,385},{3... | collective-permute-start | bytes 12296 | tf_op jit(solution)/shard_map/ppermute | solution.py:265
  123.6 4.3 %collective-permute-start.6 = (f32[4,2,1,128]{3,1,0,2:T(2,128)S(1)}, f32[4,2,1,128]{3,1,0,2:T(2,128)S(1)}, u32[]{:S(2)}, u32[]{:S(2)}) collective-permute-start(f32[4,2,1,128]{3,1,0,2:T(2,128)S(1)} %constant_dynamic-update-slice_fusion), channel_id=1, source_target_pairs={{0,256},{128,384},{256,0},{384,128},{1,257},{129,385},{257,1},{385... | collective-permute-start | bytes 12296 | tf_op jit(solution)/shard_map/ppermute | solution.py:265
  127.9 3.1 %collective-permute-start.7 = (f32[4,2,1,128]{3,1,0,2:T(2,128)S(1)}, f32[4,2,1,128]{3,1,0,2:T(2,128)S(1)}, u32[]{:S(2)}, u32[]{:S(2)}) collective-permute-start(f32[4,2,1,128]{3,1,0,2:T(2,128)S(1)} %constant_dynamic-update-slice_fusion), channel_id=1, source_target_pairs={{0,384},{128,0},{256,128},{384,256},{1,385},{129,1},{257,129},{385... | collective-permute-start | bytes 12296 | tf_op jit(solution)/shard_map/ppermute | solution.py:265
  131.1 3.2 %collective-permute-done.5 = f32[4,2,1,128]{3,1,0,2:T(2,128)S(1)} collective-permute-done((f32[4,2,1,128]{3,1,0,2:T(2,128)S(1)}, f32[4,2,1,128]{3,1,0,2:T(2,128)S(1)}, u32[]{:S(2)}, u32[]{:S(2)}) %collective-permute-start.5) | collective-permute-done | bytes 4128 | tf_op jit(solution)/shard_map/ppermute | solution.py:265
  134.8 1.8 all-to-all-done.2
  137.6 32.0 %all_to_all.30 = bf16[16,16,4096]{2,1,0:T(8,128)(2,1)S(1)} all-to-all(bf16[16,16,4096]{2,1,0:T(8,128)(2,1)S(1)} %broadcast_in_dim.98), channel_id=1, replica_groups=mesh['x'=4,'z'=16,'y'=4,'c'=2] {'y','x'}, dimensions={0} | all-to-all | bytes 4194304 | tf_op jit(solution)/shard_map/all_to_all | solution.py:252
  169.5 3.7 %collective-permute-start.8 = (bf16[256,4096]{1,0:T(8,128)(2,1)S(1)}, bf16[256,4096]{1,0:T(8,128)(2,1)}, u32[]{:S(2)}, u32[]{:S(2)}) collective-permute-start(bf16[256,4096]{1,0:T(8,128)(2,1)S(1)} %bitcast.96), channel_id=1, source_target_pairs={{0,1},{1,0},{2,3},{3,2},{4,5},{5,4},{6,7},{7,6},{8,9},{9,8},{10,11... | collective-permute-start | bytes 6291464 | tf_op jit(solution)/shard_map/ppermute | solution.py:246
  173.5 3.6 %collective-permute-done.8.theirs_ref = bf16[256,4096]{1,0:T(8,128)(2,1)} collective-permute-done((bf16[256,4096]{1,0:T(8,128)(2,1)S(1)}, bf16[256,4096]{1,0:T(8,128)(2,1)}, u32[]{:S(2)}, u32[]{:S(2)}) %collective-permute-start.8) | collective-permute-done | bytes 2097184 | tf_op jit(solution)/shard_map/ppermute | solution.py:246
  177.2 7.1 %shard_map.181.refs_0_ = f32[3,512]{1,0:T(4,128)S(1)} custom-call(s32[2]{0:T(128)S(1)} %pad_add_fusion.1.place_ref, bf16[256,4096]{1,0:T(8,128)(2,1)S(1)} %bitcast.97, bf16[256,4096]{1,0:T(8,128)(2,1)} %collective-permute-done.8.theirs_ref, s32[1,512]{1,0:T(1,128)S(1)} %convert_element_type.43.label_ref, bf16[512,4096]{1,0:T(8,128)(2,1)} %all-gather.4.cloned.1.call-done.vocab_ref), custom_call_target="tpu_custom_call" | custom-call | flops 2147483648 | bytes 8388608 | tf_op jit(solution)/shard_map/pallas_call | solution.py:432
  184.3 9.1 %shard_map.182 = f32[32,2,512]{2,1,0:T(2,128)} custom-call(s32[2]{0:T(128)S(1)} %pad_add_fusion.1.place_ref, bf16[256,4096]{1,0:T(8,128)(2,1)S(1)} %bitcast.98, bf16[256,4096]{1,0:T(8,128)(2,1)} %collective-permute-done.8.theirs_ref, s32[1,512]{1,0:T(1,128)S(1)} %convert_element_type.43.label_ref, bf16[640,4096]{1,0:T(8,128)(2,1)} %all-gather.6.cloned.1.call-done.vocab_ref, ...), custom_call_target="tpu_custom_call" | custom-call | flops 2684354560 | bytes 9437184 | tf_op jit(solution)/shard_map/pallas_call | solution.py:432
  193.4 8.6 %all-to-all-start.4 = ((f32[32,2,512]{2,1,0:T(2,128)}), f32[32,2,512]{2,1,0:T(2,128)S(1)}, u32[]{:S(2)}, u32[]{:S(2)}) async-start(f32[32,2,512]{2,1,0:T(2,128)} %shard_map.182), calls=%async_computation.4 | async-start | bytes 262144 | tf_op jit(solution)/shard_map/all_to_all | solution.py:459
  202.1 7.6 %all-to-all-done.4 = f32[32,2,512]{2,1,0:T(2,128)S(1)} async-done(((f32[32,2,512]{2,1,0:T(2,128)}), f32[32,2,512]{2,1,0:T(2,128)S(1)}, u32[]{:S(2)}, u32[]{:S(2)}) %all-to-all-start.4) | async-done | bytes 131104 | tf_op jit(solution)/shard_map/all_to_all | solution.py:459
  210.1 0.6 broadcast_in_dim.99
  210.7 6.6 %all-to-all-start.5 = ((f32[16,1,128]{2,1,0:T(1,128)}), f32[16,1,128]{2,1,0:T(1,128)S(1)}, u32[]{:S(2)}, u32[]{:S(2)}) async-start(f32[16,1,128]{2,1,0:T(1,128)} %broadcast_in_dim.99), calls=%async_computation.5 | async-start | bytes 16384 | tf_op jit(solution)/shard_map/all_to_all | solution.py:252
  217.3 0.5 fusion.6
  217.8 10.8 %all-to-all-done.5 = f32[16,1,128]{2,1,0:T(1,128)S(1)} async-done(((f32[16,1,128]{2,1,0:T(1,128)}), f32[16,1,128]{2,1,0:T(1,128)S(1)}, u32[]{:S(2)}, u32[]{:S(2)}) %all-to-all-start.5) | async-done | bytes 8224 | tf_op jit(solution)/shard_map/all_to_all | solution.py:252
  228.8 0.5 broadcast_multiply_fusion
  (69 shorter events, 3.2 us)
Async XLA Ops:
  7.2 34.5 %copy-start = (s32[16]{0:T(128)S(1)}, s32[16]{0:T(128)}, u32[]{:S(2)}) copy-start(s32[16]{0:T(128)} %param.33) | copy-start | bytes 196
  7.2 35.3 %copy-start.8 = (s32[64]{0:T(128)S(1)}, s32[64]{0:T(128)}, u32[]{:S(2)}) copy-start(s32[64]{0:T(128)} %param.32) | copy-start | bytes 772
  7.2 73.5 %copy-start.5 = (f32[512]{0:T(512)S(1)}, f32[512]{0:T(512)}, u32[]{:S(2)}) copy-start(f32[512]{0:T(512)} %param.24) | copy-start | bytes 6148
  7.2 73.5 %copy-start.2 = (bf16[128,512]{1,0:T(8,128)(2,1)S(1)}, bf16[128,512]{1,0:T(8,128)(2,1)}, u32[]{:S(2)}) copy-start(bf16[128,512]{1,0:T(8,128)(2,1)} %g_ref.1) | copy-start | bytes 393220
  7.2 90.5 %all-gather.4.cloned.1.call-start = ((), (), s32[]{:S(2)}) async-start(), calls=%async_computation.6 | async-start | bytes 4456448 | tf_op jit(solution)/shard_map/all_gather | solution.py:308
  13.5 37.4 %all-to-all-start = ((f32[64,1,640]{2,1,0:T(1,128)}), f32[64,1,640]{2,1,0:T(1,128)S(1)}, u32[]{:S(2)}, u32[]{:S(2)}) async-start(f32[64,1,640]{2,1,0:T(1,128)} %shard_map.176), calls=%async_computation | async-start | bytes 327680 | tf_op jit(solution)/shard_map/all_to_all | solution.py:322
  32.7 151.7 %all-gather.6.cloned.1.call-start = ((), (), s32[]{:S(2)}) async-start(), calls=%async_computation.7 | async-start | bytes 5570560 | tf_op jit(solution)/shard_map/all_gather | solution.py:365
  53.2 11.1 %collective-permute-start = (f32[1,128]{1,0:T(1,128)S(1)}, f32[1,128]{1,0:T(1,128)S(1)}, u32[]{:S(2)}, u32[]{:S(2)}) collective-permute-start(f32[1,128]{1,0:T(1,128)S(1)} %pad_bitcast_fusion), channel_id=1, source_target_pairs={{0,1},{1,0},{2,3},{3,2},{4,5},{5,4},{6,7},{7,6},{8,9},{9,8},{10,11... | collective-permute-start | bytes 1544 | tf_op jit(solution)/shard_map/ppermute | solution.py:265
  56.8 23.9 %all-to-all-start.1 = ((f32[64,4,128]{2,1,0:T(4,128)}), f32[64,4,128]{2,1,0:T(4,128)S(1)}, u32[]{:S(2)}, u32[]{:S(2)}) async-start(f32[64,4,128]{2,1,0:T(4,128)} %shard_map.178), calls=%async_computation.1 | async-start | bytes 262144 | tf_op jit(solution)/shard_map/all_to_all | solution.py:376
  64.4 10.8 %collective-permute-start.1 = (f32[2,1,128]{2,0,1:T(2,128)S(1)}, f32[2,1,128]{2,0,1:T(2,128)S(1)}, u32[]{:S(2)}, u32[]{:S(2)}) collective-permute-start(f32[2,1,128]{2,0,1:T(2,128)S(1)} %dynamic_update_slice.34), channel_id=1, source_target_pairs={{0,2},{2,4},{4,6},{6,0},{1,3},{3,5},{5,7},{7,1},{8,10},{10,12},{12... | collective-permute-start | bytes 3080 | tf_op jit(solution)/shard_map/ppermute | solution.py:265
  67.6 7.6 %collective-permute-start.2 = (f32[2,1,128]{2,0,1:T(2,128)S(1)}, f32[2,1,128]{2,0,1:T(2,128)S(1)}, u32[]{:S(2)}, u32[]{:S(2)}) collective-permute-start(f32[2,1,128]{2,0,1:T(2,128)S(1)} %dynamic_update_slice.34), channel_id=1, source_target_pairs={{0,4},{2,6},{4,0},{6,2},{1,5},{3,7},{5,1},{7,3},{8,12},{10,14},{12... | collective-permute-start | bytes 3080 | tf_op jit(solution)/shard_map/ppermute | solution.py:265
  72.1 4.7 %collective-permute-start.3 = (f32[2,1,128]{2,0,1:T(2,128)S(1)}, f32[2,1,128]{2,0,1:T(2,128)S(1)}, u32[]{:S(2)}, u32[]{:S(2)}) collective-permute-start(f32[2,1,128]{2,0,1:T(2,128)S(1)} %dynamic_update_slice.34), channel_id=1, source_target_pairs={{0,6},{2,0},{4,2},{6,4},{1,7},{3,1},{5,3},{7,5},{8,14},{10,8},{12,... | collective-permute-start | bytes 3080 | tf_op jit(solution)/shard_map/ppermute | solution.py:265
  80.7 1.0 copy-start.1
  81.7 0.9 copy-start.3
  82.6 0.9 copy-start.4
  99.7 37.1 %copy-start.6 = (bf16[16,4096]{1,0:T(8,128)(2,1)S(1)}, bf16[16,4096]{1,0:T(8,128)(2,1)}, u32[]{:S(2)}) copy-start(bf16[16,4096]{1,0:T(8,128)(2,1)} %param.26) | copy-start | bytes 393220
  99.7 37.5 %copy-start.7 = (f32[4096]{0:T(1024)S(1)}, f32[4096]{0:T(1024)}, u32[]{:S(2)}) copy-start(f32[4096]{0:T(1024)} %param.25) | copy-start | bytes 49156
  99.8 13.2 %collective-permute-start.4 = (f32[256,1024]{1,0:T(8,128)S(1)}, f32[256,1024]{1,0:T(8,128)S(1)}, u32[]{:S(2)}, u32[]{:S(2)}) collective-permute-start(f32[256,1024]{1,0:T(8,128)S(1)} %get-tuple-element.43), channel_id=1, source_target_pairs={{0,1},{1,0},{2,3},{3,2},{4,5},{5,4},{6,7},{7,6},{8,9},{9,8},{10,11... | collective-permute-start | bytes 3145736 | tf_op jit(solution)/shard_map/ppermute | solution.py:246
  114.1 22.6 %all-to-all-start.2 = ((f32[16,16,1024]{2,1,0:T(8,128)}), f32[16,16,1024]{2,1,0:T(8,128)S(1)}, u32[]{:S(2)}, u32[]{:S(2)}) async-start(f32[16,16,1024]{2,1,0:T(8,128)} %bitcast.27), calls=%async_computation.2 | async-start | bytes 2097152 | tf_op jit(solution)/shard_map/all_to_all | solution.py:414
  120.4 13.9 %collective-permute-start.5 = (f32[4,2,1,128]{3,1,0,2:T(2,128)S(1)}, f32[4,2,1,128]{3,1,0,2:T(2,128)S(1)}, u32[]{:S(2)}, u32[]{:S(2)}) collective-permute-start(f32[4,2,1,128]{3,1,0,2:T(2,128)S(1)} %constant_dynamic-update-slice_fusion), channel_id=1, source_target_pairs={{0,128},{128,256},{256,384},{384,0},{1,129},{129,257},{257,385},{3... | collective-permute-start | bytes 12296 | tf_op jit(solution)/shard_map/ppermute | solution.py:265
  123.6 11.2 %collective-permute-start.6 = (f32[4,2,1,128]{3,1,0,2:T(2,128)S(1)}, f32[4,2,1,128]{3,1,0,2:T(2,128)S(1)}, u32[]{:S(2)}, u32[]{:S(2)}) collective-permute-start(f32[4,2,1,128]{3,1,0,2:T(2,128)S(1)} %constant_dynamic-update-slice_fusion), channel_id=1, source_target_pairs={{0,256},{128,384},{256,0},{384,128},{1,257},{129,385},{257,1},{385... | collective-permute-start | bytes 12296 | tf_op jit(solution)/shard_map/ppermute | solution.py:265
  127.9 6.9 %collective-permute-start.7 = (f32[4,2,1,128]{3,1,0,2:T(2,128)S(1)}, f32[4,2,1,128]{3,1,0,2:T(2,128)S(1)}, u32[]{:S(2)}, u32[]{:S(2)}) collective-permute-start(f32[4,2,1,128]{3,1,0,2:T(2,128)S(1)} %constant_dynamic-update-slice_fusion), channel_id=1, source_target_pairs={{0,384},{128,0},{256,128},{384,256},{1,385},{129,1},{257,129},{385... | collective-permute-start | bytes 12296 | tf_op jit(solution)/shard_map/ppermute | solution.py:265
  169.5 7.6 %collective-permute-start.8 = (bf16[256,4096]{1,0:T(8,128)(2,1)S(1)}, bf16[256,4096]{1,0:T(8,128)(2,1)}, u32[]{:S(2)}, u32[]{:S(2)}) collective-permute-start(bf16[256,4096]{1,0:T(8,128)(2,1)S(1)} %bitcast.96), channel_id=1, source_target_pairs={{0,1},{1,0},{2,3},{3,2},{4,5},{5,4},{6,7},{7,6},{8,9},{9,8},{10,11... | collective-permute-start | bytes 6291464 | tf_op jit(solution)/shard_map/ppermute | solution.py:246
  193.4 16.3 %all-to-all-start.4 = ((f32[32,2,512]{2,1,0:T(2,128)}), f32[32,2,512]{2,1,0:T(2,128)S(1)}, u32[]{:S(2)}, u32[]{:S(2)}) async-start(f32[32,2,512]{2,1,0:T(2,128)} %shard_map.182), calls=%async_computation.4 | async-start | bytes 262144 | tf_op jit(solution)/shard_map/all_to_all | solution.py:459
  210.7 17.9 %all-to-all-start.5 = ((f32[16,1,128]{2,1,0:T(1,128)}), f32[16,1,128]{2,1,0:T(1,128)S(1)}, u32[]{:S(2)}, u32[]{:S(2)}) async-start(f32[16,1,128]{2,1,0:T(1,128)} %broadcast_in_dim.99), calls=%async_computation.5 | async-start | bytes 16384 | tf_op jit(solution)/shard_map/all_to_all | solution.py:252
Sparse Core Ops, SparseCore 0:
  10.1 87.5 all-gather.3
  99.8 79.1 all-gather.5

commit v8 on v7

--- a/solution.py
+++ b/solution.py
@@ -173,16 +173,13 @@
     layout, first, final, place_ref, mine_ref, theirs_ref, label_ref, vocab_ref, *refs
 ):
     group, skipped, offset, vocab_local = layout
-    known_ref, refs = (None, refs) if first else (refs[0], refs[1:])
-    out_ref, state_ref, held_ref, arrived = refs
+    known_ref, (out_ref, state_ref) = (None, refs) if first else (refs[0], refs[1:])
     step = pl.program_id(0)
     tile, half = vocab_ref.shape[0], mine_ref.shape[0]
     core = place_ref[0]
-    copy = pltpu.make_async_copy(theirs_ref, held_ref, arrived)
 
     @pl.when(step == 0)
     def _():
-        copy.start()
         if first:
             state_ref[0:1] = jnp.full((1, 2 * half), -3.0e38, F32)
             state_ref[1:3] = jnp.zeros((2, 2 * half), F32)
@@ -193,11 +190,9 @@
     source = lax.div(index, jnp.int32(group))
     row = index - source * group
     entry = jnp.where(
-        row < skipped, -1, place_ref[1] + source * vocab_local + (row - skipped + offset)
-    )
-    for part, tokens in enumerate((mine_ref, held_ref)):
-        if part:
-            pl.when(step == 0)(copy.wait)
+        row >= group - skipped, -1, place_ref[1] + source * vocab_local + (row + offset)
+    )
+    for part, tokens in enumerate((mine_ref, theirs_ref)):
         at = slice(part * half, (part + 1) * half)
         label = jnp.where(core == part, label_ref[:, :half], label_ref[:, half:])
         logits = mm_t(vocab_ref[...], tokens[...])
@@ -302,9 +297,8 @@
     held = own_columns // fold
     early = share * 3 // 8
     block = closing_projection.T.reshape(fold, held, width).transpose(1, 0, 2).reshape(held, embed)
-    rows_1 = jnp.concatenate(
-        [block, lax.dynamic_slice_in_dim(vocabulary_readout, head * share, early)], axis=0
-    )
+    rows_1 = lax.dynamic_slice_in_dim(vocabulary_readout, head * share, early + held)
+    rows_1 = lax.dynamic_update_slice_in_dim(rows_1, block, early, 0)
     gathered_1 = lax.all_gather(rows_1, "z", axis=0, tiled=True)
 
     chunks = n_blk // pairs
@@ -399,7 +393,7 @@
         in_specs=[
             smem,
             whole(nx, rows, width),
-            pl.BlockSpec((nz, held, embed), lambda i: (0, 0, 0)),
+            pl.BlockSpec((nz, held, embed), lambda i: (0, early // held, 0)),
         ],
         out_specs=[whole(*half.shape)] * 2,
         out_shape=[half, half],
@@ -435,18 +429,14 @@
             in_specs=[
                 smem,
                 vmem,
-                pl.BlockSpec(memory_space=pl.ANY),
+                vmem,
                 vmem,
                 pl.BlockSpec((tile, embed), lambda i: (i, 0)),
             ]
             + ([] if first else [vmem]),
             out_specs=whole(*out),
             out_shape=jax.ShapeDtypeStruct(out, F32),
-            scratch_shapes=[
-                pltpu.VMEM((3, count), F32),
-                pltpu.VMEM((count // nc, embed), BF16),
-                pltpu.SemaphoreType.DMA,
-            ],
+            scratch_shapes=[pltpu.VMEM((3, count), F32)],
             compiler_params=limit(24),
             cost_estimate=cost(
                 2 * count * vocab.shape[0] * embed, (count + vocab.shape[0]) * embed * 2

time: 238 us -> 235 us (0.987)
  Pallas kernels: 30.7 us -> 26.5 us
    pallas_call x2, Pallas kernels: 16.2 us -> 12.1 us  [score(): pl.pallas_call(functools.partial(score_kernel, layout, first, not first),...]
where the time goes in v8:
time: 235 us; the launch traced here: 234 us
  starting transfers between devices  89.7 us (38%)
  blocking collectives  43.5 us (19%)
  waiting for transfers between devices  41.6 us (18%)
  Pallas kernels  26.5 us (11%)
  between operations  14.7 us (6%)
  local copies, waits for them, and re-layouts  11.3 us (5%)
  other arithmetic  6.28 us (3%)
    all_to_all x1, blocking collectives, copies(): return lax.all_to_all(sent, axes, 0, 0, tiled=True)  32 us
    ppermute x7, starting transfers between devices, spread(): piece = lax.ppermute(value, axis, pairs) if step else value  24.9 us
    all_to_all x1, starting transfers between devices, per_device(): moved = lax.all_to_all(end, ('x', 'z'), 0, 0, tiled=True)  19.1 us
    ppermute x2, starting transfers between devices, shifted(): lax.ppermute(value, axis, [(i, (i + steps) % count) for i in range(count)])  14 us
    pallas_call x2, Pallas kernels, score(): pl.pallas_call(functools.partial(score_kernel, layout, first, not first),...  12.1 us
    all_gather x1, blocking collectives, per_device(): mixed = lax.all_gather(mixed, 'x', axis=0)  11.6 us
    all_to_all x1, waiting for transfers between devices, copies(): return lax.all_to_all(sent, axes, 0, 0, tiled=True)  10.8 us
    all_to_all x1, starting transfers between devices, per_device(): both = lax.all_to_all(both, ('x', 'y', 'c'), 0, 0, tiled=True)  10.3 us
  transfers between devices with their start and end apart: 16, of which 10 were waited for; matrix products, arithmetic and copies ran while one was open for 4% of the time, Pallas kernels for 9%

profile of v8, /device:TPU:1, one launch (start us, length us, event | category | flops | bytes accessed | tf_op | source)
XLA Modules:
  0.0 233.7 jit_solution(12532776801927218961)
XLA Ops:
  7.3 1.0 constant_dynamic-slice_fusion.1
  8.3 0.8 constant_dynamic-update-slice_fusion
  9.1 0.7 copy-done.7
  9.8 3.7 %shard_map.176 = f32[64,1,640]{2,1,0:T(1,128)} custom-call(bf16[128,512]{1,0:T(8,128)(2,1)} %k_ref.3, bf16[128,512]{1,0:T(8,128)(2,1)} %v_ref.3, bf16[128,512]{1,0:T(8,128)(2,1)} %w_ref.3), custom_call_target="tpu_custom_call" | custom-call | flops 80000000 | bytes 393216 | tf_op jit(solution)/shard_map/pallas_call | solution.py:307
  13.5 19.1 %all-to-all-start = ((f32[64,1,640]{2,1,0:T(1,128)}), f32[64,1,640]{2,1,0:T(1,128)S(1)}, u32[]{:S(2)}, u32[]{:S(2)}) async-start(f32[64,1,640]{2,1,0:T(1,128)} %shard_map.176), calls=%async_computation | async-start | bytes 327680 | tf_op jit(solution)/shard_map/all_to_all | solution.py:316
  32.7 1.1 reshape.86
  34.2 0.7 convert_element_type.35
  34.9 0.7 convert_element_type.36
  35.5 0.7 pad_maximum_fusion
  36.3 4.8 %shard_map.177 = (f32[128,512]{1,0:T(8,128)}, bf16[128,512]{1,0:T(8,128)(2,1)}, bf16[128,512]{1,0:T(8,128)(2,1)}) custom-call(bf16[128,512]{1,0:T(8,128)(2,1)} %r_ref.1, bf16[128,512]{1,0:T(8,128)(2,1)} %k_ref.3, bf16[128,512]{1,0:T(8,128)(2,1)} %v_ref.3, bf16[128,512]{1,0:T(8,128)(2,1)} %w_ref.3, f32[1,512]{1,0:T(1,128)} %bitcast.119), custom_call_target="tpu_custom_call" | custom-call | flops 240000000 | bytes 1048576 | tf_op jit(solution)/shard_map/pallas_call | solution.py:334
  41.0 0.7 compare_select_fusion
  41.7 0.8 gather_fusion
  42.5 0.8 fusion.5
  43.3 1.7 constant_dynamic-slice_fusion.3
  45.0 5.9 %all-to-all-done.moved_ref = f32[64,1,640]{2,1,0:T(1,128)S(1)} async-done(((f32[64,1,640]{2,1,0:T(1,128)}), f32[64,1,640]{2,1,0:T(1,128)S(1)}, u32[]{:S(2)}, u32[]{:S(2)}) %all-to-all-start) | async-done | bytes 163872 | tf_op jit(solution)/shard_map/all_to_all | solution.py:316
  51.1 2.0 shard_map.178
  53.1 3.7 %collective-permute-start = (f32[1,128]{1,0:T(1,128)S(1)}, f32[1,128]{1,0:T(1,128)S(1)}, u32[]{:S(2)}, u32[]{:S(2)}) collective-permute-start(f32[1,128]{1,0:T(1,128)S(1)} %pad_bitcast_fusion), channel_id=1, source_target_pairs={{0,1},{1,0},{2,3},{3,2},{4,5},{5,4},{6,7},{7,6},{8,9},{9,8},{10,11... | collective-permute-start | bytes 1544 | tf_op jit(solution)/shard_map/ppermute | solution.py:260
  56.8 8.2 %all-to-all-start.1 = ((f32[64,4,128]{2,1,0:T(4,128)}), f32[64,4,128]{2,1,0:T(4,128)S(1)}, u32[]{:S(2)}, u32[]{:S(2)}) async-start(f32[64,4,128]{2,1,0:T(4,128)} %shard_map.178), calls=%async_computation.1 | async-start | bytes 262144 | tf_op jit(solution)/shard_map/all_to_all | solution.py:370
  65.1 3.2 %collective-permute-start.1 = (f32[2,1,128]{2,0,1:T(2,128)S(1)}, f32[2,1,128]{2,0,1:T(2,128)S(1)}, u32[]{:S(2)}, u32[]{:S(2)}) collective-permute-start(f32[2,1,128]{2,0,1:T(2,128)S(1)} %dynamic_update_slice.37), channel_id=1, source_target_pairs={{0,2},{2,4},{4,6},{6,0},{1,3},{3,5},{5,7},{7,1},{8,10},{10,12},{12... | collective-permute-start | bytes 3080 | tf_op jit(solution)/shard_map/ppermute | solution.py:260
  68.3 4.5 %collective-permute-start.2 = (f32[2,1,128]{2,0,1:T(2,128)S(1)}, f32[2,1,128]{2,0,1:T(2,128)S(1)}, u32[]{:S(2)}, u32[]{:S(2)}) collective-permute-start(f32[2,1,128]{2,0,1:T(2,128)S(1)} %dynamic_update_slice.37), channel_id=1, source_target_pairs={{0,4},{2,6},{4,0},{6,2},{1,5},{3,7},{5,1},{7,3},{8,12},{10,14},{12... | collective-permute-start | bytes 3080 | tf_op jit(solution)/shard_map/ppermute | solution.py:260
  72.8 3.0 %collective-permute-start.3 = (f32[2,1,128]{2,0,1:T(2,128)S(1)}, f32[2,1,128]{2,0,1:T(2,128)S(1)}, u32[]{:S(2)}, u32[]{:S(2)}) collective-permute-start(f32[2,1,128]{2,0,1:T(2,128)S(1)} %dynamic_update_slice.37), channel_id=1, source_target_pairs={{0,6},{2,0},{4,2},{6,4},{1,7},{3,1},{5,3},{7,5},{8,14},{10,8},{12,... | collective-permute-start | bytes 3080 | tf_op jit(solution)/shard_map/ppermute | solution.py:260
  75.9 1.6 collective-permute-done.3
  77.5 4.1 %all-to-all-done.1 = f32[64,4,128]{2,1,0:T(4,128)S(1)} async-done(((f32[64,4,128]{2,1,0:T(4,128)}), f32[64,4,128]{2,1,0:T(4,128)S(1)}, u32[]{:S(2)}, u32[]{:S(2)}) %all-to-all-start.1) | async-done | bytes 131104 | tf_op jit(solution)/shard_map/all_to_all | solution.py:370
  81.7 1.0 copy-done.1
  82.6 0.9 copy-done.3
  83.5 0.9 copy-done.4
  84.4 2.0 shard_map.179
  86.5 11.6 %all-gather = bf16[512,512]{1,0:T(8,128)(2,1)S(1)} all-gather(bf16[128,512]{1,0:T(8,128)(2,1)S(1)} %shard_map.179), channel_id=2, replica_groups=mesh['x'=4,'z'=16,'y'=4,'c'=2] {'x'}, dimensions={0}, use_global_device_ids=true | all-gather | bytes 655360 | tf_op jit(solution)/shard_map/all_gather | solution.py:386
  98.1 2.0 shard_map.180
  100.1 10.3 %collective-permute-start.4 = (f32[256,1024]{1,0:T(8,128)S(1)}, f32[256,1024]{1,0:T(8,128)S(1)}, u32[]{:S(2)}, u32[]{:S(2)}) collective-permute-start(f32[256,1024]{1,0:T(8,128)S(1)} %get-tuple-element.43), channel_id=1, source_target_pairs={{0,1},{1,0},{2,3},{3,2},{4,5},{5,4},{6,7},{7,6},{8,9},{9,8},{10,11... | collective-permute-start | bytes 3145736 | tf_op jit(solution)/shard_map/ppermute | solution.py:241
  110.3 2.3 collective-permute-done.4
  112.6 1.1 add.175
  113.7 6.5 %all-to-all-start.2 = ((f32[16,16,1024]{2,1,0:T(8,128)}), f32[16,16,1024]{2,1,0:T(8,128)S(1)}, u32[]{:S(2)}, u32[]{:S(2)}) async-start(f32[16,16,1024]{2,1,0:T(8,128)} %bitcast.27), calls=%async_computation.2 | async-start | bytes 2097152 | tf_op jit(solution)/shard_map/all_to_all | solution.py:408
  120.3 3.2 %collective-permute-start.5 = (f32[4,2,1,128]{3,1,0,2:T(2,128)S(1)}, f32[4,2,1,128]{3,1,0,2:T(2,128)S(1)}, u32[]{:S(2)}, u32[]{:S(2)}) collective-permute-start(f32[4,2,1,128]{3,1,0,2:T(2,128)S(1)} %constant_dynamic-update-slice_fusion.1), channel_id=1, source_target_pairs={{0,128},{128,256},{256,384},{384,0},{1,129},{129,257},{257,385},{3... | collective-permute-start | bytes 12296 | tf_op jit(solution)/shard_map/ppermute | solution.py:260
  123.4 4.3 %collective-permute-start.6 = (f32[4,2,1,128]{3,1,0,2:T(2,128)S(1)}, f32[4,2,1,128]{3,1,0,2:T(2,128)S(1)}, u32[]{:S(2)}, u32[]{:S(2)}) collective-permute-start(f32[4,2,1,128]{3,1,0,2:T(2,128)S(1)} %constant_dynamic-update-slice_fusion.1), channel_id=1, source_target_pairs={{0,256},{128,384},{256,0},{384,128},{1,257},{129,385},{257,1},{385... | collective-permute-start | bytes 12296 | tf_op jit(solution)/shard_map/ppermute | solution.py:260
  127.8 3.1 %collective-permute-start.7 = (f32[4,2,1,128]{3,1,0,2:T(2,128)S(1)}, f32[4,2,1,128]{3,1,0,2:T(2,128)S(1)}, u32[]{:S(2)}, u32[]{:S(2)}) collective-permute-start(f32[4,2,1,128]{3,1,0,2:T(2,128)S(1)} %constant_dynamic-update-slice_fusion.1), channel_id=1, source_target_pairs={{0,384},{128,0},{256,128},{384,256},{1,385},{129,1},{257,129},{385... | collective-permute-start | bytes 12296 | tf_op jit(solution)/shard_map/ppermute | solution.py:260
  130.9 3.3 %collective-permute-done.5 = f32[4,2,1,128]{3,1,0,2:T(2,128)S(1)} collective-permute-done((f32[4,2,1,128]{3,1,0,2:T(2,128)S(1)}, f32[4,2,1,128]{3,1,0,2:T(2,128)S(1)}, u32[]{:S(2)}, u32[]{:S(2)}) %collective-permute-start.5) | collective-permute-done | bytes 4128 | tf_op jit(solution)/shard_map/ppermute | solution.py:260
  134.7 1.8 all-to-all-done.2
  137.4 32.0 %all_to_all.30 = bf16[16,16,4096]{2,1,0:T(8,128)(2,1)S(1)} all-to-all(bf16[16,16,4096]{2,1,0:T(8,128)(2,1)S(1)} %broadcast_in_dim.98), channel_id=1, replica_groups=mesh['x'=4,'z'=16,'y'=4,'c'=2] {'y','x'}, dimensions={0} | all-to-all | bytes 4194304 | tf_op jit(solution)/shard_map/all_to_all | solution.py:247
  169.3 3.7 %collective-permute-start.8 = (bf16[256,4096]{1,0:T(8,128)(2,1)S(1)}, bf16[256,4096]{1,0:T(8,128)(2,1)}, u32[]{:S(2)}, u32[]{:S(2)}) collective-permute-start(bf16[256,4096]{1,0:T(8,128)(2,1)S(1)} %bitcast.96), channel_id=1, source_target_pairs={{0,1},{1,0},{2,3},{3,2},{4,5},{5,4},{6,7},{7,6},{8,9},{9,8},{10,11... | collective-permute-start | bytes 6291464 | tf_op jit(solution)/shard_map/ppermute | solution.py:241
  173.3 3.6 %collective-permute-done.8.theirs_ref = bf16[256,4096]{1,0:T(8,128)(2,1)} collective-permute-done((bf16[256,4096]{1,0:T(8,128)(2,1)S(1)}, bf16[256,4096]{1,0:T(8,128)(2,1)}, u32[]{:S(2)}, u32[]{:S(2)}) %collective-permute-start.8) | collective-permute-done | bytes 2097184 | tf_op jit(solution)/shard_map/ppermute | solution.py:241
  177.0 5.5 %shard_map.181.refs_0_ = f32[3,512]{1,0:T(4,128)S(1)} custom-call(s32[2]{0:T(128)S(1)} %pad_add_fusion.1.place_ref, bf16[256,4096]{1,0:T(8,128)(2,1)S(1)} %bitcast.97, bf16[256,4096]{1,0:T(8,128)(2,1)} %collective-permute-done.8.theirs_ref, s32[1,512]{1,0:T(1,128)S(1)} %convert_element_type.43.label_ref, bf16[512,4096]{1,0:T(8,128)(2,1)} %all-gather.4.cloned.1.call-done.vocab_ref), custom_call_target="tpu_custom_call" | custom-call | flops 2147483648 | bytes 8388608 | tf_op jit(solution)/shard_map/pallas_call | solution.py:426
  182.5 6.6 %shard_map.182 = f32[32,2,512]{2,1,0:T(2,128)} custom-call(s32[2]{0:T(128)S(1)} %pad_add_fusion.1.place_ref, bf16[256,4096]{1,0:T(8,128)(2,1)S(1)} %bitcast.98, bf16[256,4096]{1,0:T(8,128)(2,1)} %collective-permute-done.8.theirs_ref, s32[1,512]{1,0:T(1,128)S(1)} %convert_element_type.43.label_ref, bf16[640,4096]{1,0:T(8,128)(2,1)} %all-gather.6.cloned.1.call-done.vocab_ref, ...), custom_call_target="tpu_custom_call" | custom-call | flops 2684354560 | bytes 9437184 | tf_op jit(solution)/shard_map/pallas_call | solution.py:426
  189.1 10.3 %all-to-all-start.4 = ((f32[32,2,512]{2,1,0:T(2,128)}), f32[32,2,512]{2,1,0:T(2,128)S(1)}, u32[]{:S(2)}, u32[]{:S(2)}) async-start(f32[32,2,512]{2,1,0:T(2,128)} %shard_map.182), calls=%async_computation.4 | async-start | bytes 262144 | tf_op jit(solution)/shard_map/all_to_all | solution.py:449
  199.5 7.6 %all-to-all-done.4 = f32[32,2,512]{2,1,0:T(2,128)S(1)} async-done(((f32[32,2,512]{2,1,0:T(2,128)}), f32[32,2,512]{2,1,0:T(2,128)S(1)}, u32[]{:S(2)}, u32[]{:S(2)}) %all-to-all-start.4) | async-done | bytes 131104 | tf_op jit(solution)/shard_map/all_to_all | solution.py:449
  207.5 0.6 broadcast_in_dim.99
  208.1 6.7 %all-to-all-start.5 = ((f32[16,1,128]{2,1,0:T(1,128)}), f32[16,1,128]{2,1,0:T(1,128)S(1)}, u32[]{:S(2)}, u32[]{:S(2)}) async-start(f32[16,1,128]{2,1,0:T(1,128)} %broadcast_in_dim.99), calls=%async_computation.5 | async-start | bytes 16384 | tf_op jit(solution)/shard_map/all_to_all | solution.py:247
  215.3 10.8 %all-to-all-done.5 = f32[16,1,128]{2,1,0:T(1,128)S(1)} async-done(((f32[16,1,128]{2,1,0:T(1,128)}), f32[16,1,128]{2,1,0:T(1,128)S(1)}, u32[]{:S(2)}, u32[]{:S(2)}) %all-to-all-start.5) | async-done | bytes 8224 | tf_op jit(solution)/shard_map/all_to_all | solution.py:247
  (71 shorter events, 4.0 us)
Async XLA Ops:
  7.2 34.5 %copy-start = (s32[16]{0:T(128)S(1)}, s32[16]{0:T(128)}, u32[]{:S(2)}) copy-start(s32[16]{0:T(128)} %param.33) | copy-start | bytes 196
  7.2 74.5 %copy-start.5 = (f32[512]{0:T(512)S(1)}, f32[512]{0:T(512)}, u32[]{:S(2)}) copy-start(f32[512]{0:T(512)} %param.24) | copy-start | bytes 6148
  7.2 74.5 %copy-start.2 = (bf16[128,512]{1,0:T(8,128)(2,1)S(1)}, bf16[128,512]{1,0:T(8,128)(2,1)}, u32[]{:S(2)}) copy-start(bf16[128,512]{1,0:T(8,128)(2,1)} %g_ref.1) | copy-start | bytes 393220
  7.2 90.9 %all-gather.4.cloned.1.call-start = ((), (), s32[]{:S(2)}) async-start(), calls=%async_computation.6 | async-start | bytes 4456448 | tf_op jit(solution)/shard_map/all_gather | solution.py:302
  9.1 0.7 copy-start.7
  13.5 37.4 %all-to-all-start = ((f32[64,1,640]{2,1,0:T(1,128)}), f32[64,1,640]{2,1,0:T(1,128)S(1)}, u32[]{:S(2)}, u32[]{:S(2)}) async-start(f32[64,1,640]{2,1,0:T(1,128)} %shard_map.176), calls=%async_computation | async-start | bytes 327680 | tf_op jit(solution)/shard_map/all_to_all | solution.py:316
  32.7 149.8 %all-gather.6.cloned.1.call-start = ((), (), s32[]{:S(2)}) async-start(), calls=%async_computation.7 | async-start | bytes 5570560 | tf_op jit(solution)/shard_map/all_gather | solution.py:359
  53.1 11.9 %collective-permute-start = (f32[1,128]{1,0:T(1,128)S(1)}, f32[1,128]{1,0:T(1,128)S(1)}, u32[]{:S(2)}, u32[]{:S(2)}) collective-permute-start(f32[1,128]{1,0:T(1,128)S(1)} %pad_bitcast_fusion), channel_id=1, source_target_pairs={{0,1},{1,0},{2,3},{3,2},{4,5},{5,4},{6,7},{7,6},{8,9},{9,8},{10,11... | collective-permute-start | bytes 1544 | tf_op jit(solution)/shard_map/ppermute | solution.py:260
  56.8 24.8 %all-to-all-start.1 = ((f32[64,4,128]{2,1,0:T(4,128)}), f32[64,4,128]{2,1,0:T(4,128)S(1)}, u32[]{:S(2)}, u32[]{:S(2)}) async-start(f32[64,4,128]{2,1,0:T(4,128)} %shard_map.178), calls=%async_computation.1 | async-start | bytes 262144 | tf_op jit(solution)/shard_map/all_to_all | solution.py:370
  65.1 10.8 %collective-permute-start.1 = (f32[2,1,128]{2,0,1:T(2,128)S(1)}, f32[2,1,128]{2,0,1:T(2,128)S(1)}, u32[]{:S(2)}, u32[]{:S(2)}) collective-permute-start(f32[2,1,128]{2,0,1:T(2,128)S(1)} %dynamic_update_slice.37), channel_id=1, source_target_pairs={{0,2},{2,4},{4,6},{6,0},{1,3},{3,5},{5,7},{7,1},{8,10},{10,12},{12... | collective-permute-start | bytes 3080 | tf_op jit(solution)/shard_map/ppermute | solution.py:260
  68.3 7.6 %collective-permute-start.2 = (f32[2,1,128]{2,0,1:T(2,128)S(1)}, f32[2,1,128]{2,0,1:T(2,128)S(1)}, u32[]{:S(2)}, u32[]{:S(2)}) collective-permute-start(f32[2,1,128]{2,0,1:T(2,128)S(1)} %dynamic_update_slice.37), channel_id=1, source_target_pairs={{0,4},{2,6},{4,0},{6,2},{1,5},{3,7},{5,1},{7,3},{8,12},{10,14},{12... | collective-permute-start | bytes 3080 | tf_op jit(solution)/shard_map/ppermute | solution.py:260
  72.8 4.7 %collective-permute-start.3 = (f32[2,1,128]{2,0,1:T(2,128)S(1)}, f32[2,1,128]{2,0,1:T(2,128)S(1)}, u32[]{:S(2)}, u32[]{:S(2)}) collective-permute-start(f32[2,1,128]{2,0,1:T(2,128)S(1)} %dynamic_update_slice.37), channel_id=1, source_target_pairs={{0,6},{2,0},{4,2},{6,4},{1,7},{3,1},{5,3},{7,5},{8,14},{10,8},{12,... | collective-permute-start | bytes 3080 | tf_op jit(solution)/shard_map/ppermute | solution.py:260
  81.7 1.0 copy-start.1
  82.6 0.9 copy-start.3
  83.5 0.9 copy-start.4
  100.0 36.6 %copy-start.6 = (bf16[16,4096]{1,0:T(8,128)(2,1)S(1)}, bf16[16,4096]{1,0:T(8,128)(2,1)}, u32[]{:S(2)}) copy-start(bf16[16,4096]{1,0:T(8,128)(2,1)} %param.26) | copy-start | bytes 393220
  100.1 37.0 %copy-start.8 = (f32[4096]{0:T(1024)S(1)}, f32[4096]{0:T(1024)}, u32[]{:S(2)}) copy-start(f32[4096]{0:T(1024)} %param.25) | copy-start | bytes 49156
  100.1 12.5 %collective-permute-start.4 = (f32[256,1024]{1,0:T(8,128)S(1)}, f32[256,1024]{1,0:T(8,128)S(1)}, u32[]{:S(2)}, u32[]{:S(2)}) collective-permute-start(f32[256,1024]{1,0:T(8,128)S(1)} %get-tuple-element.43), channel_id=1, source_target_pairs={{0,1},{1,0},{2,3},{3,2},{4,5},{5,4},{6,7},{7,6},{8,9},{9,8},{10,11... | collective-permute-start | bytes 3145736 | tf_op jit(solution)/shard_map/ppermute | solution.py:241
  113.7 22.8 %all-to-all-start.2 = ((f32[16,16,1024]{2,1,0:T(8,128)}), f32[16,16,1024]{2,1,0:T(8,128)S(1)}, u32[]{:S(2)}, u32[]{:S(2)}) async-start(f32[16,16,1024]{2,1,0:T(8,128)} %bitcast.27), calls=%async_computation.2 | async-start | bytes 2097152 | tf_op jit(solution)/shard_map/all_to_all | solution.py:408
  120.3 14.0 %collective-permute-start.5 = (f32[4,2,1,128]{3,1,0,2:T(2,128)S(1)}, f32[4,2,1,128]{3,1,0,2:T(2,128)S(1)}, u32[]{:S(2)}, u32[]{:S(2)}) collective-permute-start(f32[4,2,1,128]{3,1,0,2:T(2,128)S(1)} %constant_dynamic-update-slice_fusion.1), channel_id=1, source_target_pairs={{0,128},{128,256},{256,384},{384,0},{1,129},{129,257},{257,385},{3... | collective-permute-start | bytes 12296 | tf_op jit(solution)/shard_map/ppermute | solution.py:260
  123.4 11.2 %collective-permute-start.6 = (f32[4,2,1,128]{3,1,0,2:T(2,128)S(1)}, f32[4,2,1,128]{3,1,0,2:T(2,128)S(1)}, u32[]{:S(2)}, u32[]{:S(2)}) collective-permute-start(f32[4,2,1,128]{3,1,0,2:T(2,128)S(1)} %constant_dynamic-update-slice_fusion.1), channel_id=1, source_target_pairs={{0,256},{128,384},{256,0},{384,128},{1,257},{129,385},{257,1},{385... | collective-permute-start | bytes 12296 | tf_op jit(solution)/shard_map/ppermute | solution.py:260
  127.8 6.9 %collective-permute-start.7 = (f32[4,2,1,128]{3,1,0,2:T(2,128)S(1)}, f32[4,2,1,128]{3,1,0,2:T(2,128)S(1)}, u32[]{:S(2)}, u32[]{:S(2)}) collective-permute-start(f32[4,2,1,128]{3,1,0,2:T(2,128)S(1)} %constant_dynamic-update-slice_fusion.1), channel_id=1, source_target_pairs={{0,384},{128,0},{256,128},{384,256},{1,385},{129,1},{257,129},{385... | collective-permute-start | bytes 12296 | tf_op jit(solution)/shard_map/ppermute | solution.py:260
  169.3 7.6 %collective-permute-start.8 = (bf16[256,4096]{1,0:T(8,128)(2,1)S(1)}, bf16[256,4096]{1,0:T(8,128)(2,1)}, u32[]{:S(2)}, u32[]{:S(2)}) collective-permute-start(bf16[256,4096]{1,0:T(8,128)(2,1)S(1)} %bitcast.96), channel_id=1, source_target_pairs={{0,1},{1,0},{2,3},{3,2},{4,5},{5,4},{6,7},{7,6},{8,9},{9,8},{10,11... | collective-permute-start | bytes 6291464 | tf_op jit(solution)/shard_map/ppermute | solution.py:241
  182.5 16.9 %copy-start.9 = (s32[64]{0:T(128)S(1)}, s32[64]{0:T(128)}, u32[]{:S(2)}) copy-start(s32[64]{0:T(128)} %param.32) | copy-start | bytes 772
  189.1 18.0 %all-to-all-start.4 = ((f32[32,2,512]{2,1,0:T(2,128)}), f32[32,2,512]{2,1,0:T(2,128)S(1)}, u32[]{:S(2)}, u32[]{:S(2)}) async-start(f32[32,2,512]{2,1,0:T(2,128)} %shard_map.182), calls=%async_computation.4 | async-start | bytes 262144 | tf_op jit(solution)/shard_map/all_to_all | solution.py:449
  208.1 18.0 %all-to-all-start.5 = ((f32[16,1,128]{2,1,0:T(1,128)}), f32[16,1,128]{2,1,0:T(1,128)S(1)}, u32[]{:S(2)}, u32[]{:S(2)}) async-start(f32[16,1,128]{2,1,0:T(1,128)} %broadcast_in_dim.99), calls=%async_computation.5 | async-start | bytes 16384 | tf_op jit(solution)/shard_map/all_to_all | solution.py:247
Sparse Core Ops, SparseCore 0:
  10.1 87.6 all-gather.3
  99.9 78.8 all-gather.5
